TPU v7x, 256 devices: a whole 4x4x8 slice. The times are simulated.
256 devices in a mesh: ctx: 64 (over y_hi, z, x), head: 4 (over y_lo, core).
Axes of the slice: x: 4, y: 4 (y_hi: 2, y_lo: 2; y = y_hi * 2 + y_lo), z: 8, core: 2. Of those that a mesh axis runs over, the one named last changes fastest.
Arguments:
- queries: bfloat16 [16384, 2048], P('ctx', 'head'), may hold values from -6 to 6
- keys: bfloat16 [16384, 2048], P('ctx', 'head'), may hold values from -6 to 6
- values: bfloat16 [16384, 2048], P('ctx', 'head'), may hold values from -6 to 6
- out_weight: bfloat16 [2048, 2048], P('head'), may hold values from -0.125 to 0.125
- upstream: bfloat16 [16384, 2048], P('ctx', 'head'), may hold values from -6 to 6
- rand_round: int32 [256, 3], P('ctx'), may hold values from 0 to 3, as said below
- rand_block: int32 [256, 3], P('ctx'), may hold values from 0 to 3
Outputs:
- mixed: bfloat16 [16384, 2048], P('ctx', 'head')
- grad_queries: bfloat16 [16384, 2048], P('ctx', 'head')
- grad_keys: bfloat16 [16384, 2048], P('ctx', 'head')
- grad_values: bfloat16 [16384, 2048], P('ctx', 'head')
Inputs may be any that keep to these rules, and one draw needn't show every extreme that they name: `rand_round`: the three entries of one query block name three different rounds.
All inputs are finite; a program needn't handle non-finite values.
Results may differ from a plain program's by a relative error of at most 0.023.
Values may be sent and summed in bfloat16 or wider, within the bound.
A program may use at most 64 MiB of HBM per device.

v0:
```python
import math

import jax
import jax.numpy as jnp
from jax import lax
from jax.sharding import PartitionSpec as P

HDIM = 128
BS = 64


def padded_2(block, sides, width):
    for axis, dim in sides:
        count = lax.axis_size(axis)
        forward = [(i, i + 1) for i in range(count - 1)]
        backward = [(target, source) for source, target in forward]
        low = lax.ppermute(
            lax.slice_in_dim(block, block.shape[dim] - width, None, axis=dim), axis, forward
        )
        high = lax.ppermute(lax.slice_in_dim(block, 0, width, axis=dim), axis, backward)
        block = jnp.concatenate([low, block, high], axis=dim)
    return block


def spread_2(value, axis, source):
    kept = jnp.where(lax.axis_index(axis) == source, value, 0).astype(value.dtype)
    return lax.psum(kept, axis)


def from_behind(block, axis, distance):
    devices = range(lax.axis_size(axis))
    route = [((i - distance) % len(devices), i) for i in devices]
    return lax.ppermute(block, axis, route)


def shifted(block, axis, distance):
    devices = range(lax.axis_size(axis))
    route = [(i - distance, i) for i in devices if i - distance in devices]
    return lax.ppermute(block, axis, route)


def body(queries, keys, values, out_weight, upstream, rand_round, rand_block):
    row_count, width_here = queries.shape
    head_dim = HDIM
    heads_here = width_here // head_dim
    block_rows = BS
    run_blocks = row_count // block_rows
    axis_count = lax.axis_size("ctx")
    position = lax.axis_index("ctx")
    logit_scale = 1.0 / math.sqrt(head_dim)
    offsets = [axis_count * factor // 8 for factor in (4, 2, 3, 5)]
    total_blocks = axis_count * run_blocks
    blocks = position * run_blocks + jnp.arange(run_blocks, dtype=jnp.int32)
    always = jnp.ones((run_blocks,), jnp.bool_)
    allowed = jnp.stack(
        [blocks >= 1, always, blocks <= total_blocks - 2, blocks >= 2, always, always, always],
        axis=1,
    )
    key_value = jnp.stack([keys, values])
    padded = padded_2(key_value, (("ctx", 1),), block_rows)
    framed = padded.reshape(2, run_blocks + 2, block_rows, width_here)
    window = jnp.stack(
        [framed[:, :run_blocks], framed[:, 1 : run_blocks + 1], framed[:, 2:]], axis=2
    )
    anchor = spread_2(key_value[:, :block_rows], "ctx", 0)
    anchor_slot = jnp.broadcast_to(
        anchor[:, None, None], (2, run_blocks, 1, block_rows, width_here)
    )
    picks = (rand_round * run_blocks + rand_block).reshape(-1)

    def assemble(arrivals):
        pool = jnp.stack(arrivals, axis=1).reshape(2, 4 * run_blocks, block_rows, width_here)
        chosen = jnp.take(pool, picks, axis=1).reshape(2, run_blocks, 3, block_rows, width_here)
        return jnp.concatenate([window, anchor_slot, chosen], axis=2)

    arrivals = [from_behind(key_value, "ctx", offset) for offset in offsets]
    gathered = assemble(arrivals)
    q_blocks = queries.reshape(run_blocks, block_rows, heads_here, head_dim)
    key_bundle = gathered[0].reshape(run_blocks, 7, block_rows, heads_here, head_dim)
    value_bundle = gathered[1].reshape(run_blocks, 7, block_rows, heads_here, head_dim)
    attention_logits = (
        jnp.einsum("bqhd,bjkhd->bhqjk", q_blocks, key_bundle, preferred_element_type=jnp.float32)
        * logit_scale
    )
    attention_logits = jnp.where(allowed[:, None, None, :, None], attention_logits, -jnp.inf)
    row_max = jnp.max(attention_logits, axis=(3, 4), keepdims=True)
    raw = jnp.exp(attention_logits - row_max)
    row_total = jnp.sum(raw, axis=(3, 4), keepdims=True)
    probs = raw / row_total
    probabilities_blocked = probs.astype(jnp.bfloat16)
    attn_blocks = jnp.einsum(
        "bhqjk,bjkhd->bqhd", probabilities_blocked, value_bundle, preferred_element_type=jnp.float32
    ).astype(jnp.bfloat16)
    attention = attn_blocks.reshape(row_count, width_here)
    partial_out = jnp.dot(attention, out_weight, preferred_element_type=jnp.float32)
    mixed = lax.psum_scatter(
        partial_out.astype(jnp.bfloat16), "head", scatter_dimension=1, tiled=True
    )
    grad_attention = lax.dot_general(
        lax.all_gather(upstream, "head", axis=1, tiled=True),
        out_weight,
        (((1,), (1,)), ((), ())),
        preferred_element_type=jnp.float32,
    ).astype(jnp.bfloat16)
    fresh = [from_behind(key_value, "ctx", offset) for offset in offsets]
    gathered = assemble(fresh)
    key_bundle = gathered[0].reshape(run_blocks, 7, block_rows, heads_here, head_dim)
    value_bundle = gathered[1].reshape(run_blocks, 7, block_rows, heads_here, head_dim)
    grad_blocks = grad_attention.reshape(run_blocks, block_rows, heads_here, head_dim)
    delta = jnp.sum(grad_blocks.astype(jnp.float32) * attn_blocks.astype(jnp.float32), axis=-1)
    grad_probabilities = jnp.einsum(
        "bqhd,bjkhd->bhqjk", grad_blocks, value_bundle, preferred_element_type=jnp.float32
    )
    grad_logits = (probs * (grad_probabilities - delta.transpose(0, 2, 1)[..., None, None])).astype(
        jnp.bfloat16
    )
    grad_query_rows = logit_scale * jnp.einsum(
        "bhqjk,bjkhd->bqhd", grad_logits, key_bundle, preferred_element_type=jnp.float32
    )
    grad_queries = grad_query_rows.astype(jnp.bfloat16).reshape(row_count, width_here)
    slot_count = 7
    partial_keys = logit_scale * jnp.einsum(
        "bhqjk,bqhd->bjkhd", grad_logits, q_blocks, preferred_element_type=jnp.float32
    )
    partial_values = jnp.einsum(
        "bhqjk,bqhd->bjkhd", probabilities_blocked, grad_blocks, preferred_element_type=jnp.float32
    )
    parts = jnp.stack([partial_keys, partial_values]).reshape(
        2, run_blocks, slot_count, block_rows, width_here
    )
    framed_grad = jnp.zeros((2, run_blocks + 2, block_rows, width_here), jnp.float32)
    framed_grad = framed_grad.at[:, :run_blocks].add(parts[:, :, 0])
    framed_grad = framed_grad.at[:, 1 : run_blocks + 1].add(parts[:, :, 1])
    framed_grad = framed_grad.at[:, 2:].add(parts[:, :, 2])
    own_grad = framed_grad[:, 1 : run_blocks + 1]
    for step_by, rim_grad, slot_index in (
        (-1, framed_grad[:, 0], run_blocks - 1),
        (1, framed_grad[:, run_blocks + 1], 0),
    ):
        arrived = shifted(rim_grad.astype(jnp.bfloat16), "ctx", step_by).astype(rim_grad.dtype)
        own_grad = own_grad.at[:, slot_index].add(arrived)
    anchor_grad = lax.psum(jnp.sum(parts[:, :, 3], axis=1), "ctx")
    own_grad = own_grad.at[:, 0].add(jnp.where(position == 0, anchor_grad, 0.0))
    random_parts = parts[:, :, 4:].reshape(2, run_blocks * 3, block_rows, width_here)
    spread = (
        jnp.zeros((2, 4 * run_blocks, block_rows, width_here), jnp.float32)
        .at[:, picks]
        .add(random_parts)
    )
    spread = spread.reshape(2, 4, run_blocks, block_rows, width_here)
    for turn_index in range(4):
        returned = from_behind(
            spread[:, turn_index].astype(jnp.bfloat16), "ctx", -offsets[turn_index]
        ).astype(jnp.float32)
        own_grad = own_grad + returned
    grad_keys = own_grad[0].reshape(row_count, width_here).astype(jnp.bfloat16)
    grad_values = own_grad[1].reshape(row_count, width_here).astype(jnp.bfloat16)
    return (mixed, grad_queries, grad_keys, grad_values)


def solution(mesh):
    placed = (
        P("ctx", "head"),
        P("ctx", "head"),
        P("ctx", "head"),
        P("head", None),
        P("ctx", "head"),
        P("ctx", None),
        P("ctx", None),
    )
    return jax.shard_map(
        body,
        mesh=mesh,
        in_specs=placed,
        out_specs=(P("ctx", "head"), P("ctx", "head"), P("ctx", "head"), P("ctx", "head")),
        check_vma=False,
    )
```

profile of v0, /device:TPU:8, one launch (start us, length us, event | category | flops | bytes accessed | tf_op | source)
XLA Modules:
  0.0 1372.0 jit_solution(12532426596104420063)
XLA Ops:
  13.4 3.9 collective-permute-start.5
  17.4 5.4 collective-permute-start.3
  24.0 5.2 collective-permute-start
  34.3 19.1 %collective-permute-start.4 = (bf16[2,256,512]{2,1,0:T(8,128)(2,1)S(1)}, bf16[2,256,512]{2,1,0:T(8,128)(2,1)}, u32[]{:S(2)}, u32[]{:S(2)}) collective-permute-start(bf16[2,256,512]{2,1,0:T(8,128)(2,1)S(1)} %pad_maximum_fusion.2), channel_id=1, source_target_pairs={{160,0},{164,4},{168,8},{172,12},{176,16},{180,20},{184,24},{188,2... | collective-permute-start | bytes 1572872 | tf_op jit(solution)/shard_map/ppermute | solution.py:33
  57.2 579.5 %all-reduce.4.cloned.1.call-done = bf16[2,64,512]{2,1,0:T(8,128)(2,1)} async-done(((bf16[2,64,512]{2,1,0:T(8,128)(2,1)}), bf16[2,64,512]{2,1,0:T(8,128)(2,1)}) %all-reduce.4.cloned.1.call-update) | async-done | bytes 131088 | tf_op jit(solution)/shard_map/psum | solution.py:27
  638.5 3.0 pad_maximum_fusion
  641.5 3.5 gather_fusion
  647.8 4.3 fusion.57
  652.2 4.2 reshape_squeeze.4
  656.4 4.2 reshape_squeeze.5
  669.0 3.0 multiply_reduce_fusion
  672.2 3.0 multiply_convert_fusion
  680.2 6.9 copy.64
  687.1 5.4 reshape.370
  693.1 5.0 copy.65
  698.0 5.3 reshape.371
  703.3 2.6 constant_dynamic-update-slice_fusion.1
  707.1 2.9 copy-done.2
  725.5 2.5 broadcast_in_dim.49
  727.9 8.8 scatter_fusion
  736.8 2.5 convert.30
  742.9 3.8 collective-permute-start.9
  748.2 9.1 collective-permute-start.8
  758.4 602.4 %all-reduce.6.cloned.1.call-done = f32[2,64,512]{2,1,0:T(8,128)} async-done(((f32[2,64,512]{2,1,0:T(8,128)}), f32[2,64,512]{2,1,0:T(8,128)}) %all-reduce.6.cloned.1.call-update) | async-done | bytes 262160 | tf_op jit(solution)/shard_map/psum | solution.py:142
  (106 shorter events, 60.7 us)
Async XLA Ops:
  8.0 659.0 %copy-start = (bf16[512,2048]{1,0:T(8,128)(2,1)S(1)}, bf16[512,2048]{1,0:T(8,128)(2,1)}, u32[]{:S(2)}) copy-start(bf16[512,2048]{1,0:T(8,128)(2,1)} %param.24) | copy-start | bytes 6291460
  8.0 628.7 %all-reduce.4.cloned.1.call-start = ((), (), s32[]{:S(2)}) async-start(), calls=%async_computation.1 | async-start | bytes 262144 | tf_op jit(solution)/shard_map/psum | solution.py:27
  9.9 657.1 %all-gather.2.cloned.1.call-start = ((), (), s32[]{:S(2)}) async-start(), calls=%async_computation.3 | async-start | bytes 1310720 | tf_op jit(solution)/shard_map/all_gather | solution.py:100
  11.0 627.4 %collective-permute-start.2 = (bf16[2,256,512]{2,1,0:T(8,128)(2,1)S(1)}, bf16[2,256,512]{2,1,0:T(8,128)(2,1)S(1)}, u32[]{:S(2)}, u32[]{:S(2)}) collective-permute-start(bf16[2,256,512]{2,1,0:T(8,128)(2,1)S(1)} %pad_maximum_fusion.2), channel_id=1, source_target_pairs={{128,0},{132,4},{136,8},{140,12},{144,16},{148,20},{152,24},{156,2... | collective-permute-start | bytes 1572872 | tf_op jit(solution)/shard_map/ppermute | solution.py:33
  13.4 625.1 %collective-permute-start.5 = (bf16[2,256,512]{2,1,0:T(8,128)(2,1)S(1)}, bf16[2,256,512]{2,1,0:T(8,128)(2,1)}, u32[]{:S(2)}, u32[]{:S(2)}) collective-permute-start(bf16[2,256,512]{2,1,0:T(8,128)(2,1)S(1)} %pad_maximum_fusion.2), channel_id=1, source_target_pairs={{96,0},{100,4},{104,8},{108,12},{112,16},{116,20},{120,24},{124,28... | collective-permute-start | bytes 1572872 | tf_op jit(solution)/shard_map/ppermute | solution.py:33
  17.4 621.1 %collective-permute-start.3 = (bf16[2,256,512]{2,1,0:T(8,128)(2,1)S(1)}, bf16[2,256,512]{2,1,0:T(8,128)(2,1)}, u32[]{:S(2)}, u32[]{:S(2)}) collective-permute-start(bf16[2,256,512]{2,1,0:T(8,128)(2,1)S(1)} %pad_maximum_fusion.2), channel_id=1, source_target_pairs={{192,0},{196,4},{200,8},{204,12},{208,16},{212,20},{216,24},{220,2... | collective-permute-start | bytes 1572872 | tf_op jit(solution)/shard_map/ppermute | solution.py:33
  22.7 11.6 collective-permute-start.1
  24.0 29.4 %collective-permute-start = (bf16[2,64,512]{2,1,0:T(8,128)(2,1)S(1)}, bf16[2,64,512]{2,1,0:T(8,128)(2,1)}, u32[]{:S(2)}, u32[]{:S(2)}) collective-permute-start(bf16[2,64,512]{2,1,0:T(8,128)(2,1)S(1)} %get-tuple-element.89), channel_id=1, source_target_pairs={{0,4},{4,8},{8,12},{12,16},{16,20},{20,24},{24,28},{28,32},{32,36}... | collective-permute-start | bytes 393224 | tf_op jit(solution)/shard_map/ppermute | solution.py:17
  29.3 1331.5 %all-reduce.6.cloned.1.call-start = ((), (), s32[]{:S(2)}) async-start(), calls=%async_computation.4 | async-start | bytes 524288 | tf_op jit(solution)/shard_map/psum | solution.py:142
  34.3 604.2 %collective-permute-start.4 = (bf16[2,256,512]{2,1,0:T(8,128)(2,1)S(1)}, bf16[2,256,512]{2,1,0:T(8,128)(2,1)}, u32[]{:S(2)}, u32[]{:S(2)}) collective-permute-start(bf16[2,256,512]{2,1,0:T(8,128)(2,1)S(1)} %pad_maximum_fusion.2), channel_id=1, source_target_pairs={{160,0},{164,4},{168,8},{172,12},{176,16},{180,20},{184,24},{188,2... | collective-permute-start | bytes 1572872 | tf_op jit(solution)/shard_map/ppermute | solution.py:33
  638.5 6.5 copy-start.10
  669.0 3.1 copy-start.5
  672.2 3.0 copy-start.9
  687.1 5.4 copy-start.6
  703.3 3.1 copy-start.3
  710.9 653.6 %reduce-scatter.2.cloned.1.call-start = ((), (), s32[]{:S(2)}) async-start(), calls=%async_computation.2 | async-start | bytes 1310720 | tf_op jit(solution)/shard_map/reduce_scatter | solution.py:96
  721.1 37.2 %collective-permute-start.7 = (bf16[2,64,512]{2,1,0:T(8,128)(2,1)S(1)}, bf16[2,64,512]{2,1,0:T(8,128)(2,1)S(1)}, u32[]{:S(2)}, u32[]{:S(2)}) collective-permute-start(bf16[2,64,512]{2,1,0:T(8,128)(2,1)S(1)} %fusion.49), channel_id=1, source_target_pairs={{0,4},{4,8},{8,12},{12,16},{16,20},{20,24},{24,28},{28,32},{32,36}... | collective-permute-start | bytes 393224 | tf_op jit(solution)/shard_map/ppermute | solution.py:39
  724.2 24.0 %collective-permute-start.6 = (bf16[2,64,512]{2,1,0:T(8,128)(2,1)}, bf16[2,64,512]{2,1,0:T(8,128)(2,1)S(1)}, u32[]{:S(2)}, u32[]{:S(2)}) collective-permute-start(bf16[2,64,512]{2,1,0:T(8,128)(2,1)} %fusion.48), channel_id=1, source_target_pairs={{4,0},{8,4},{12,8},{16,12},{20,16},{24,20},{28,24},{32,28},{36,32}... | collective-permute-start | bytes 393224 | tf_op jit(solution)/shard_map/ppermute | solution.py:39
  739.4 17.9 %copy-start.7 = (f32[2,4,64,512]{3,2,0,1:T(8,128)S(1)}, f32[2,4,64,512]{3,2,0,1:T(8,128)}, u32[]{:S(2)}) copy-start(f32[2,4,64,512]{3,2,0,1:T(8,128)} %slice.280) | copy-start | bytes 3145732
  742.9 618.9 %collective-permute-start.11 = (bf16[2,4,64,512]{3,2,0,1:T(8,128)(2,1)}, bf16[2,4,64,512]{3,2,0,1:T(8,128)(2,1)}, u32[]{:S(2)}, u32[]{:S(2)}) collective-permute-start(bf16[2,4,64,512]{3,2,0,1:T(8,128)(2,1)} %bitcast.143), channel_id=1, source_target_pairs={{160,0},{164,4},{168,8},{172,12},{176,16},{180,20},{184,24},{188,2... | collective-permute-start | bytes 1572872 | tf_op jit(solution)/shard_map/ppermute | solution.py:33
  742.9 618.9 %collective-permute-start.9 = (bf16[2,4,64,512]{3,2,0,1:T(8,128)(2,1)}, bf16[2,4,64,512]{3,2,0,1:T(8,128)(2,1)}, u32[]{:S(2)}, u32[]{:S(2)}) collective-permute-start(bf16[2,4,64,512]{3,2,0,1:T(8,128)(2,1)} %bitcast.145), channel_id=1, source_target_pairs={{64,0},{68,4},{72,8},{76,12},{80,16},{84,20},{88,24},{92,28},{96,3... | collective-permute-start | bytes 1572872 | tf_op jit(solution)/shard_map/ppermute | solution.py:33
  746.7 615.2 %collective-permute-start.10 = (bf16[2,4,64,512]{3,2,0,1:T(8,128)(2,1)}, bf16[2,4,64,512]{3,2,0,1:T(8,128)(2,1)}, u32[]{:S(2)}, u32[]{:S(2)}) collective-permute-start(bf16[2,4,64,512]{3,2,0,1:T(8,128)(2,1)} %bitcast.144), channel_id=1, source_target_pairs={{96,0},{100,4},{104,8},{108,12},{112,16},{116,20},{120,24},{124,28... | collective-permute-start | bytes 1572872 | tf_op jit(solution)/shard_map/ppermute | solution.py:33
  748.2 613.6 %collective-permute-start.8 = (bf16[2,4,64,512]{3,2,0,1:T(8,128)(2,1)}, bf16[2,4,64,512]{3,2,0,1:T(8,128)(2,1)}, u32[]{:S(2)}, u32[]{:S(2)}) collective-permute-start(bf16[2,4,64,512]{3,2,0,1:T(8,128)(2,1)} %bitcast.146), channel_id=1, source_target_pairs={{128,0},{132,4},{136,8},{140,12},{144,16},{148,20},{152,24},{156,2... | collective-permute-start | bytes 1572872 | tf_op jit(solution)/shard_map/ppermute | solution.py:33
  757.3 607.2 %copy-start.1 = (bf16[512,2048]{1,0:T(8,128)(2,1)S(1)}, bf16[512,2048]{1,0:T(8,128)(2,1)}, u32[]{:S(2)}) copy-start(bf16[512,2048]{1,0:T(8,128)(2,1)} %param.24) | copy-start | bytes 6291460
  (3 other events, 5.7 us)
Sparse Core Ops, SparseCore 0:
  12.0 624.6 all-reduce.3
  711.1 649.6 all-reduce.5
Sparse Core Ops, SparseCore 1:
  29.3 35.1 all-gather.1
  714.7 17.9 reduce-scatter.1
where the time goes:
time: 1370 us
  waiting for transfers between devices  1180 us (86%)
  local copies, waits for them, and re-layouts  70.3 us (5%)
  starting transfers between devices  55.5 us (4%)
  other arithmetic  32.7 us (2%)
  between operations  15.8 us (1%)
  matrix products  15.7 us (1%)
    psum x1, waiting for transfers between devices, body(): anchor_grad = lax.psum(jnp.sum(parts[:, :, 3], axis=1), 'ctx')  602 us
    psum x1, waiting for transfers between devices, spread_2(): return lax.psum(kept, axis)  580 us
    ppermute x8, starting transfers between devices, from_behind(): return lax.ppermute(block, axis, route)  45.2 us
  transfers between devices with their start and end apart: 16, of which 2 were waited for; matrix products, arithmetic and copies ran while one was open for 5% of the time, Pallas kernels for 0%

commit v1 on v0

--- a/solution.py
+++ b/solution.py
@@ -22,9 +22,41 @@
     return block
 
 
-def spread_2(value, axis, source):
-    kept = jnp.where(lax.axis_index(axis) == source, value, 0).astype(value.dtype)
-    return lax.psum(kept, axis)
+def tree_strides(count, radix=4):
+    strides, stride = [], 1
+    while stride < count:
+        strides.append((stride, min(radix, count // stride)))
+        stride *= radix
+    return strides
+
+
+def spread_down(value, axis):
+    count = lax.axis_size(axis)
+    position = lax.axis_index(axis)
+    for stride, ways in reversed(tree_strides(count)):
+        digit = (position // stride) % ways
+        arrivals = [
+            lax.ppermute(
+                value, axis, [(i, i + turn * stride) for i in range(0, count, stride * ways)]
+            )
+            for turn in range(1, ways)
+        ]
+        holds = position % (stride * ways) == 0
+        fresh = arrivals[0]
+        for turn in range(2, ways):
+            fresh = jnp.where(digit == turn, arrivals[turn - 1], fresh)
+        value = jnp.where(holds, value, fresh)
+    return value
+
+
+def sum_up(value, axis):
+    count = lax.axis_size(axis)
+    for stride, ways in tree_strides(count):
+        sent = value.astype(jnp.bfloat16)
+        for turn in range(1, ways):
+            route = [(i + turn * stride, i) for i in range(0, count, stride * ways)]
+            value = value + lax.ppermute(sent, axis, route).astype(jnp.float32)
+    return value
 
 
 def from_behind(block, axis, distance):
@@ -62,7 +94,7 @@
     window = jnp.stack(
         [framed[:, :run_blocks], framed[:, 1 : run_blocks + 1], framed[:, 2:]], axis=2
     )
-    anchor = spread_2(key_value[:, :block_rows], "ctx", 0)
+    anchor = spread_down(key_value[:, :block_rows], "ctx")
     anchor_slot = jnp.broadcast_to(
         anchor[:, None, None], (2, run_blocks, 1, block_rows, width_here)
     )
@@ -102,10 +134,6 @@
         (((1,), (1,)), ((), ())),
         preferred_element_type=jnp.float32,
     ).astype(jnp.bfloat16)
-    fresh = [from_behind(key_value, "ctx", offset) for offset in offsets]
-    gathered = assemble(fresh)
-    key_bundle = gathered[0].reshape(run_blocks, 7, block_rows, heads_here, head_dim)
-    value_bundle = gathered[1].reshape(run_blocks, 7, block_rows, heads_here, head_dim)
     grad_blocks = grad_attention.reshape(run_blocks, block_rows, heads_here, head_dim)
     delta = jnp.sum(grad_blocks.astype(jnp.float32) * attn_blocks.astype(jnp.float32), axis=-1)
     grad_probabilities = jnp.einsum(
@@ -139,7 +167,7 @@
     ):
         arrived = shifted(rim_grad.astype(jnp.bfloat16), "ctx", step_by).astype(rim_grad.dtype)
         own_grad = own_grad.at[:, slot_index].add(arrived)
-    anchor_grad = lax.psum(jnp.sum(parts[:, :, 3], axis=1), "ctx")
+    anchor_grad = sum_up(jnp.sum(parts[:, :, 3], axis=1), "ctx")
     own_grad = own_grad.at[:, 0].add(jnp.where(position == 0, anchor_grad, 0.0))
     random_parts = parts[:, :, 4:].reshape(2, run_blocks * 3, block_rows, width_here)
     spread = (

time: 1370 us -> 296 us (0.22)
  waiting for transfers between devices: 1180 us -> 77 us
  starting transfers between devices: 55.5 us -> 88 us
    psum x2 -> x0, waiting for transfers between devices: 1180 us -> none  [the longest x1 602 us: body(): anchor_grad = lax.psum(jnp.sum(parts[:, :, 3], axis=1), 'ctx')]
    ppermute x0 -> x18, starting transfers between devices: none -> 56.8 us  [the longest x9 45.1 us: spread_down(): lax.ppermute(value, axis, [(i, i + turn * stride) for i in range(0, count...]
    ppermute x0 -> x18, waiting for transfers between devices: none -> 45.4 us  [the longest x9 41.7 us: sum_up(): value = value + lax.ppermute(sent, axis, route).astype(jnp.float32)]
    ppermute x8, waiting for transfers between devices: 0.02 us -> 31 us  [from_behind(): return lax.ppermute(block, axis, route)]
    ppermute x8, starting transfers between devices: 45.2 us -> 19.6 us  [from_behind(): return lax.ppermute(block, axis, route)]
  transfers between devices with their start and end apart: 16 -> 32, of which waited for: 2 -> 8; matrix products, arithmetic and copies ran while one was open for 5% -> 24% of each run, Pallas kernels for 0% -> 0%
where the time goes in v1:
time: 296 us; the launch traced here: 294 us
  starting transfers between devices  88 us (30%)
  waiting for transfers between devices  77 us (26%)
  local copies, waits for them, and re-layouts  61.4 us (21%)
  other arithmetic  36.4 us (12%)
  matrix products  16.8 us (6%)
  between operations  14.7 us (5%)
    ppermute x9, starting transfers between devices, spread_down(): lax.ppermute(value, axis, [(i, i + turn * stride) for i in range(0, count...  45.1 us
    ppermute x9, waiting for transfers between devices, sum_up(): value = value + lax.ppermute(sent, axis, route).astype(jnp.float32)  41.7 us
    ppermute x8, waiting for transfers between devices, from_behind(): return lax.ppermute(block, axis, route)  31 us
    ppermute x8, starting transfers between devices, from_behind(): return lax.ppermute(block, axis, route)  19.6 us
    unnamed x42, local copies, waits for them, and re-layouts  12 us
    ppermute x9, starting transfers between devices, sum_up(): value = value + lax.ppermute(sent, axis, route).astype(jnp.float32)  11.7 us
    another operation x3, local copies, waits for them, and re-layouts, body(): jnp.stack([partial_keys, partial_values])  11.1 us
    scatter-add x1, other arithmetic, body(): spread = jnp.zeros((2, 4 * run_blocks, block_rows, width_here), jnp.float...  8.97 us
  transfers between devices with their start and end apart: 32, of which 8 were waited for; matrix products, arithmetic and copies ran while one was open for 24% of the time, Pallas kernels for 0%

profile of v1, /device:TPU:8, one launch (start us, length us, event | category | flops | bytes accessed | tf_op | source)
XLA Modules:
  0.0 294.3 jit_solution(10679633411524188293)
XLA Ops:
  9.0 9.7 %collective-permute-start.4 = (bf16[2,64,512]{2,1,0:T(8,128)(2,1)S(1)}, bf16[2,64,512]{2,1,0:T(8,128)(2,1)}, u32[]{:S(2)}, u32[]{:S(2)}) collective-permute-start(bf16[2,64,512]{2,1,0:T(8,128)(2,1)S(1)} %get-tuple-element.94), channel_id=1, source_target_pairs={{0,64},{1,65},{2,66},{3,67}} | collective-permute-start | bytes 393224 | tf_op jit(solution)/shard_map/ppermute | solution.py:39
  31.5 3.1 %collective-permute-start = (bf16[2,64,512]{2,1,0:T(8,128)(2,1)}, bf16[2,64,512]{2,1,0:T(8,128)(2,1)S(1)}, u32[]{:S(2)}, u32[]{:S(2)}) collective-permute-start(bf16[2,64,512]{2,1,0:T(8,128)(2,1)} %get-tuple-element.93), channel_id=1, source_target_pairs={{0,4},{4,8},{8,12},{12,16},{16,20},{20,24},{24,28},{28,32},{32,36}... | collective-permute-start | bytes 393224 | tf_op jit(solution)/shard_map/ppermute | solution.py:17
  37.4 22.2 %collective-permute-start.6 = (bf16[2,64,512]{2,1,0:T(8,128)(2,1)S(1)}, bf16[2,64,512]{2,1,0:T(8,128)(2,1)S(1)}, u32[]{:S(2)}, u32[]{:S(2)}) collective-permute-start(bf16[2,64,512]{2,1,0:T(8,128)(2,1)S(1)} %select_select_fusion.2), channel_id=1, source_target_pairs={{0,32},{64,96},{128,160},{192,224},{1,33},{65,97},{129,161},{193,2... | collective-permute-start | bytes 393224 | tf_op jit(solution)/shard_map/ppermute | solution.py:39
  59.7 3.6 %collective-permute-start.5 = (bf16[2,64,512]{2,1,0:T(8,128)(2,1)S(1)}, bf16[2,64,512]{2,1,0:T(8,128)(2,1)S(1)}, u32[]{:S(2)}, u32[]{:S(2)}) collective-permute-start(bf16[2,64,512]{2,1,0:T(8,128)(2,1)S(1)} %select_select_fusion.2), channel_id=1, source_target_pairs={{0,48},{64,112},{128,176},{192,240},{1,49},{65,113},{129,177},{193... | collective-permute-start | bytes 393224 | tf_op jit(solution)/shard_map/ppermute | solution.py:39
  65.1 2.6 collective-permute-start.12
  78.7 16.9 %collective-permute-done.12 = bf16[2,256,512]{2,1,0:T(8,128)(2,1)S(1)} collective-permute-done((bf16[2,256,512]{2,1,0:T(8,128)(2,1)S(1)}, bf16[2,256,512]{2,1,0:T(8,128)(2,1)S(1)}, u32[]{:S(2)}, u32[]{:S(2)}) %collective-permute-start.12) | collective-permute-done | bytes 524320 | tf_op jit(solution)/shard_map/ppermute | solution.py:65
  95.6 14.2 %collective-permute-done.13 = bf16[2,256,512]{2,1,0:T(8,128)(2,1)S(1)} collective-permute-done((bf16[2,256,512]{2,1,0:T(8,128)(2,1)S(1)}, bf16[2,256,512]{2,1,0:T(8,128)(2,1)S(1)}, u32[]{:S(2)}, u32[]{:S(2)}) %collective-permute-start.13) | collective-permute-done | bytes 524320 | tf_op jit(solution)/shard_map/ppermute | solution.py:65
  112.4 3.4 %gather_fusion = bf16[12,2,64,512]{3,2,1,0:T(8,128)(2,1)} fusion(bf16[2,16,64,512]{3,2,1,0:T(8,128)(2,1)} %bitcast.152, s32[1024]{0:T(1024)S(1)} %pad_clamp_fusion), kind=kCustom, calls=%fused_computation | custom fusion | bytes 3145776 | tf_op jit(solution)/shard_map/jit(_take)/gather | solution.py:105
  115.8 3.1 %fusion.10 = bf16[2,4,7,64,512]{4,3,2,1,0:T(8,128)(2,1)} fusion(bf16[2,4,7,64,512]{4,3,2,1,0:T(8,128)(2,1)} %broadcast_dynamic-update-slice_fusion, bf16[2,4,3,64,512]{4,3,0,2,1:T(8,128)(2,1)} %bitcast.153, pred[4,3]{1,0:T(4,128)(4,1)S(1)} %get-tuple-element.78), kind=kLoop, calls=%fused_computation.20 | loop fusion | flops 786432 | bytes 3145740 | tf_op jit(solution)/shard_map/concatenate | solution.py:106
  118.9 4.3 %fusion.59 = (bf16[1,4,7,64,512]{4,3,2,1,0:T(8,128)(2,1)}, bf16[1,4,7,64,512]{4,3,2,1,0:T(8,128)(2,1)}) fusion(bf16[2,4,7,64,512]{4,3,2,1,0:T(8,128)(2,1)} %fusion.10), kind=kLoop, calls=%fused_computation.96 | loop fusion | bytes 7340032 | tf_op jit(solution)/shard_map/slice | solution.py:112
  123.2 4.2 %reshape_squeeze.8 = bf16[4,7,64,4,128]{4,3,2,1,0:T(4,128)(2,1)} reshape(bf16[1,4,7,64,512]{4,3,2,1,0:T(8,128)(2,1)} %get-tuple-element.83) | data formatting | bytes 3670016 | tf_op jit(solution)/shard_map/reshape;squeeze | solution.py:112
  127.4 4.2 %reshape_squeeze.9 = bf16[4,7,64,4,128]{4,3,2,1,0:T(4,128)(2,1)} reshape(bf16[1,4,7,64,512]{4,3,2,1,0:T(8,128)(2,1)} %get-tuple-element.84) | data formatting | bytes 3670016 | tf_op jit(solution)/shard_map/reshape;squeeze | solution.py:111
  140.2 3.6 %multiply_reduce_fusion = (f32[4,64,4]{1,2,0:T(4,128)S(1)}, bf16[4,64,4,128]{3,1,2,0:T(8,128)(2,1)}) fusion(bf16[4,64,4,128]{3,2,1,0:T(4,128)(2,1)S(1)} %reshape.327, bf16[4,4,64,7,64]{2,4,3,1,0:T(8,128)(2,1)} %fusion.35, bf16[4,7,64,4,128]{4,3,2,1,0:T(4,128)(2,1)} %reshape_squeeze.8), kind=kOutput, calls=%fused_computation.54 | convolution fusion | flops 118094848 | bytes 3280896 | tf_op jit(solution)/shard_map/bhqjk,bjkhd->bqhd/dot_general | solution.py:123
  143.8 3.0 %multiply_convert_fusion = bf16[4,4,64,7,64]{2,4,3,1,0:T(8,128)(2,1)S(1)} fusion(f32[4,4,64]{2,1,0:T(4,128)S(1)} %bitcast.176, bf16[4,7,64,4,128]{4,3,2,1,0:T(4,128)(2,1)} %reshape_squeeze.8, f32[4,4,64]{2,1,0:T(4,128)S(1)} %fusion.2, f32[4,4,64]{2,1,0:T(4,128)S(1)} %get-tuple-element.95, f32[4,4,7,64,64]{4,3,2,1,0:T(8,128)S(1)} %copy-done.6, ...), kind=kOutput, calls=%fused_computation.6 | convolution fusion | flops 120651776 | bytes 4861980 | tf_op jit(solution)/shard_map/bqhd,bjkhd->bhqjk/dot_general | solution.py:139
  148.9 4.9 %copy.72 = f32[4,7,64,4,128]{4,3,2,1,0:T(4,128)} copy(f32[4,7,64,4,128]{4,2,1,3,0:T(8,128)S(1)} %multiply_bitcast_fusion) | data formatting | bytes 7340032 | tf_op jit(solution)/shard_map/mul | solution.py:150
  153.7 5.2 %stack.60 = f32[1,4,7,64,512]{4,3,2,1,0:T(8,128)} reshape(f32[4,7,64,4,128]{4,3,2,1,0:T(4,128)} %copy.72) | data formatting | bytes 7340032 | tf_op jit(solution)/shard_map/stack | solution.py:156
  161.1 5.0 %copy.74 = f32[4,7,64,4,128]{4,3,2,1,0:T(4,128)} copy(f32[4,7,64,4,128]{4,2,1,3,0:T(8,128)S(1)} %bitcast.145) | data formatting | bytes 7340032 | tf_op jit(solution)/shard_map/bhqjk,bqhd->bjkhd/transpose | solution.py:153
  166.0 5.2 %stack.61 = f32[1,4,7,64,512]{4,3,2,1,0:T(8,128)} reshape(f32[4,7,64,4,128]{4,3,2,1,0:T(4,128)} %copy.74) | data formatting | bytes 7340032 | tf_op jit(solution)/shard_map/stack | solution.py:156
  201.3 5.8 %collective-permute-start.16 = (bf16[2,64,512]{2,1,0:T(8,128)(2,1)}, bf16[2,64,512]{2,1,0:T(8,128)(2,1)S(1)}, u32[]{:S(2)}, u32[]{:S(2)}) collective-permute-start(bf16[2,64,512]{2,1,0:T(8,128)(2,1)} %fusion.50), channel_id=1, source_target_pairs={{0,4},{4,8},{8,12},{12,16},{16,20},{20,24},{24,28},{28,32},{32,36}... | collective-permute-start | bytes 393224 | tf_op jit(solution)/shard_map/ppermute | solution.py:71
  209.7 9.0 %scatter_fusion = f32[2,16,64,512]{3,2,1,0:T(8,128)} fusion(f32[2,16,64,512]{3,2,1,0:T(8,128)} %broadcast_in_dim.47, s32[12]{0:T(128)S(1)} %fusion.57, f32[12,2,64,512]{3,2,1,0:T(8,128)} %copy.80), kind=kCustom, calls=%fused_computation.1 | custom fusion | flops 786432 | bytes 9437232 | tf_op jit(solution)/shard_map/scatter-add | solution.py:176
  226.0 6.8 %collective-permute-start.29 = (bf16[2,4,64,512]{3,2,0,1:T(8,128)(2,1)S(1)}, bf16[2,4,64,512]{3,2,0,1:T(8,128)(2,1)S(1)}, u32[]{:S(2)}, u32[]{:S(2)}) collective-permute-start(bf16[2,4,64,512]{3,2,0,1:T(8,128)(2,1)S(1)} %bitcast.169), channel_id=1, source_target_pairs={{160,0},{164,4},{168,8},{172,12},{176,16},{180,20},{184,24},{188,2... | collective-permute-start | bytes 1572872 | tf_op jit(solution)/shard_map/ppermute | solution.py:65
  235.4 5.2 %collective-permute-start.28 = (bf16[2,4,64,512]{3,2,0,1:T(8,128)(2,1)S(1)}, bf16[2,4,64,512]{3,2,0,1:T(8,128)(2,1)S(1)}, u32[]{:S(2)}, u32[]{:S(2)}) collective-permute-start(bf16[2,4,64,512]{3,2,0,1:T(8,128)(2,1)S(1)} %bitcast.167), channel_id=1, source_target_pairs={{96,0},{100,4},{104,8},{108,12},{112,16},{116,20},{120,24},{124,28... | collective-permute-start | bytes 1572872 | tf_op jit(solution)/shard_map/ppermute | solution.py:65
  243.0 19.3 %collective-permute-done.24 = bf16[2,64,512]{2,1,0:T(8,128)(2,1)S(1)} collective-permute-done((bf16[2,64,512]{2,1,0:T(8,128)(2,1)S(1)}, bf16[2,64,512]{2,1,0:T(8,128)(2,1)S(1)}, u32[]{:S(2)}, u32[]{:S(2)}) %collective-permute-start.24) | collective-permute-done | bytes 131104 | tf_op jit(solution)/shard_map/ppermute | solution.py:58
  263.6 22.4 %collective-permute-done.23 = bf16[2,64,512]{2,1,0:T(8,128)(2,1)S(1)} collective-permute-done((bf16[2,64,512]{2,1,0:T(8,128)(2,1)S(1)}, bf16[2,64,512]{2,1,0:T(8,128)(2,1)S(1)}, u32[]{:S(2)}, u32[]{:S(2)}) %collective-permute-start.23) | collective-permute-done | bytes 131104 | tf_op jit(solution)/shard_map/ppermute | solution.py:58
  (146 shorter events, 92.5 us)
Async XLA Ops:
  7.2 130.9 %all-gather.2.cloned.1.call-start = ((), (), s32[]{:S(2)}) async-start(), calls=%async_computation.2 | async-start | bytes 1310720 | tf_op jit(solution)/shard_map/all_gather | solution.py:132
  9.0 22.4 %collective-permute-start.4 = (bf16[2,64,512]{2,1,0:T(8,128)(2,1)S(1)}, bf16[2,64,512]{2,1,0:T(8,128)(2,1)}, u32[]{:S(2)}, u32[]{:S(2)}) collective-permute-start(bf16[2,64,512]{2,1,0:T(8,128)(2,1)S(1)} %get-tuple-element.94), channel_id=1, source_target_pairs={{0,64},{1,65},{2,66},{3,67}} | collective-permute-start | bytes 393224 | tf_op jit(solution)/shard_map/ppermute | solution.py:39
  23.1 36.5 %collective-permute-start.1 = (bf16[2,64,512]{2,1,0:T(8,128)(2,1)S(1)}, bf16[2,64,512]{2,1,0:T(8,128)(2,1)}, u32[]{:S(2)}, u32[]{:S(2)}) collective-permute-start(bf16[2,64,512]{2,1,0:T(8,128)(2,1)S(1)} %get-tuple-element.94), channel_id=1, source_target_pairs={{4,0},{8,4},{12,8},{16,12},{20,16},{24,20},{28,24},{32,28},{36,32}... | collective-permute-start | bytes 393224 | tf_op jit(solution)/shard_map/ppermute | solution.py:20
  24.4 263.0 %reduce-scatter.2.cloned.1.call-start = ((), (), s32[]{:S(2)}) async-start(), calls=%async_computation.1 | async-start | bytes 1310720 | tf_op jit(solution)/shard_map/reduce_scatter | solution.py:128
  25.6 53.1 %collective-permute-start.11 = (bf16[2,256,512]{2,1,0:T(8,128)(2,1)S(1)}, bf16[2,256,512]{2,1,0:T(8,128)(2,1)}, u32[]{:S(2)}, u32[]{:S(2)}) collective-permute-start(bf16[2,256,512]{2,1,0:T(8,128)(2,1)S(1)} %pad_maximum_fusion.2), channel_id=1, source_target_pairs={{128,0},{132,4},{136,8},{140,12},{144,16},{148,20},{152,24},{156,2... | collective-permute-start | bytes 1572872 | tf_op jit(solution)/shard_map/ppermute | solution.py:65
  31.4 47.3 %collective-permute-start.14 = (bf16[2,256,512]{2,1,0:T(8,128)(2,1)S(1)}, bf16[2,256,512]{2,1,0:T(8,128)(2,1)S(1)}, u32[]{:S(2)}, u32[]{:S(2)}) collective-permute-start(bf16[2,256,512]{2,1,0:T(8,128)(2,1)S(1)} %pad_maximum_fusion.2), channel_id=1, source_target_pairs={{96,0},{100,4},{104,8},{108,12},{112,16},{116,20},{120,24},{124,28... | collective-permute-start | bytes 1572872 | tf_op jit(solution)/shard_map/ppermute | solution.py:65
  35.6 29.6 %collective-permute-start.7 = (bf16[2,64,512]{2,1,0:T(8,128)(2,1)S(1)}, bf16[2,64,512]{2,1,0:T(8,128)(2,1)S(1)}, u32[]{:S(2)}, u32[]{:S(2)}) collective-permute-start(bf16[2,64,512]{2,1,0:T(8,128)(2,1)S(1)} %select_select_fusion.2), channel_id=1, source_target_pairs={{0,16},{64,80},{128,144},{192,208},{1,17},{65,81},{129,145},{193,2... | collective-permute-start | bytes 393224 | tf_op jit(solution)/shard_map/ppermute | solution.py:39
  37.4 30.4 %collective-permute-start.6 = (bf16[2,64,512]{2,1,0:T(8,128)(2,1)S(1)}, bf16[2,64,512]{2,1,0:T(8,128)(2,1)S(1)}, u32[]{:S(2)}, u32[]{:S(2)}) collective-permute-start(bf16[2,64,512]{2,1,0:T(8,128)(2,1)S(1)} %select_select_fusion.2), channel_id=1, source_target_pairs={{0,32},{64,96},{128,160},{192,224},{1,33},{65,97},{129,161},{193,2... | collective-permute-start | bytes 393224 | tf_op jit(solution)/shard_map/ppermute | solution.py:39
  65.1 30.4 %collective-permute-start.12 = (bf16[2,256,512]{2,1,0:T(8,128)(2,1)S(1)}, bf16[2,256,512]{2,1,0:T(8,128)(2,1)S(1)}, u32[]{:S(2)}, u32[]{:S(2)}) collective-permute-start(bf16[2,256,512]{2,1,0:T(8,128)(2,1)S(1)} %pad_maximum_fusion.2), channel_id=1, source_target_pairs={{192,0},{196,4},{200,8},{204,12},{208,16},{212,20},{216,24},{220,2... | collective-permute-start | bytes 1572872 | tf_op jit(solution)/shard_map/ppermute | solution.py:65
  72.6 37.1 %collective-permute-start.13 = (bf16[2,256,512]{2,1,0:T(8,128)(2,1)S(1)}, bf16[2,256,512]{2,1,0:T(8,128)(2,1)S(1)}, u32[]{:S(2)}, u32[]{:S(2)}) collective-permute-start(bf16[2,256,512]{2,1,0:T(8,128)(2,1)S(1)} %pad_maximum_fusion.2), channel_id=1, source_target_pairs={{160,0},{164,4},{168,8},{172,12},{176,16},{180,20},{184,24},{188,2... | collective-permute-start | bytes 1572872 | tf_op jit(solution)/shard_map/ppermute | solution.py:65
  177.8 17.1 %collective-permute-start.19 = (bf16[2,64,512]{2,1,0:T(8,128)(2,1)}, bf16[2,64,512]{2,1,0:T(8,128)(2,1)S(1)}, u32[]{:S(2)}, u32[]{:S(2)}) collective-permute-start(bf16[2,64,512]{2,1,0:T(8,128)(2,1)} %convert_element_type.124), channel_id=1, source_target_pairs={{12,0},{28,16},{44,32},{60,48},{76,64},{92,80},{108,96},{124,112},... | collective-permute-start | bytes 393224 | tf_op jit(solution)/shard_map/ppermute | solution.py:58
  179.3 15.7 %collective-permute-start.18 = (bf16[2,64,512]{2,1,0:T(8,128)(2,1)}, bf16[2,64,512]{2,1,0:T(8,128)(2,1)}, u32[]{:S(2)}, u32[]{:S(2)}) collective-permute-start(bf16[2,64,512]{2,1,0:T(8,128)(2,1)} %convert_element_type.124), channel_id=1, source_target_pairs={{8,0},{24,16},{40,32},{56,48},{72,64},{88,80},{104,96},{120,112},{... | collective-permute-start | bytes 393224 | tf_op jit(solution)/shard_map/ppermute | solution.py:58
  193.7 41.7 %collective-permute-start.15 = (bf16[2,64,512]{2,1,0:T(8,128)(2,1)}, bf16[2,64,512]{2,1,0:T(8,128)(2,1)}, u32[]{:S(2)}, u32[]{:S(2)}) collective-permute-start(bf16[2,64,512]{2,1,0:T(8,128)(2,1)} %fusion.49), channel_id=1, source_target_pairs={{4,0},{8,4},{12,8},{16,12},{20,16},{24,20},{28,24},{32,28},{36,32}... | collective-permute-start | bytes 393224 | tf_op jit(solution)/shard_map/ppermute | solution.py:71
  196.7 24.5 %collective-permute-start.22 = (bf16[2,64,512]{2,1,0:T(8,128)(2,1)}, bf16[2,64,512]{2,1,0:T(8,128)(2,1)}, u32[]{:S(2)}, u32[]{:S(2)}) collective-permute-start(bf16[2,64,512]{2,1,0:T(8,128)(2,1)} %fusion.53), channel_id=1, source_target_pairs={{48,0},{112,64},{176,128},{240,192},{49,1},{113,65},{177,129},{241... | collective-permute-start | bytes 393224 | tf_op jit(solution)/shard_map/ppermute | solution.py:58
  198.0 23.2 %collective-permute-start.21 = (bf16[2,64,512]{2,1,0:T(8,128)(2,1)}, bf16[2,64,512]{2,1,0:T(8,128)(2,1)}, u32[]{:S(2)}, u32[]{:S(2)}) collective-permute-start(bf16[2,64,512]{2,1,0:T(8,128)(2,1)} %fusion.53), channel_id=1, source_target_pairs={{32,0},{96,64},{160,128},{224,192},{33,1},{97,65},{161,129},{225,1... | collective-permute-start | bytes 393224 | tf_op jit(solution)/shard_map/ppermute | solution.py:58
  199.3 21.9 %collective-permute-start.20 = (bf16[2,64,512]{2,1,0:T(8,128)(2,1)}, bf16[2,64,512]{2,1,0:T(8,128)(2,1)}, u32[]{:S(2)}, u32[]{:S(2)}) collective-permute-start(bf16[2,64,512]{2,1,0:T(8,128)(2,1)} %fusion.53), channel_id=1, source_target_pairs={{16,0},{80,64},{144,128},{208,192},{17,1},{81,65},{145,129},{209,1... | collective-permute-start | bytes 393224 | tf_op jit(solution)/shard_map/ppermute | solution.py:58
  201.3 39.3 %collective-permute-start.16 = (bf16[2,64,512]{2,1,0:T(8,128)(2,1)}, bf16[2,64,512]{2,1,0:T(8,128)(2,1)S(1)}, u32[]{:S(2)}, u32[]{:S(2)}) collective-permute-start(bf16[2,64,512]{2,1,0:T(8,128)(2,1)} %fusion.50), channel_id=1, source_target_pairs={{0,4},{4,8},{8,12},{12,16},{16,20},{20,24},{24,28},{28,32},{32,36}... | collective-permute-start | bytes 393224 | tf_op jit(solution)/shard_map/ppermute | solution.py:71
  222.6 18.1 %collective-permute-start.25 = (bf16[2,64,512]{2,1,0:T(8,128)(2,1)S(1)}, bf16[2,64,512]{2,1,0:T(8,128)(2,1)S(1)}, u32[]{:S(2)}, u32[]{:S(2)}) collective-permute-start(bf16[2,64,512]{2,1,0:T(8,128)(2,1)S(1)} %get-tuple-element.76), channel_id=1, source_target_pairs={{192,0},{193,1},{194,2},{195,3}} | collective-permute-start | bytes 393224 | tf_op jit(solution)/shard_map/ppermute | solution.py:58
  226.0 60.2 %collective-permute-start.29 = (bf16[2,4,64,512]{3,2,0,1:T(8,128)(2,1)S(1)}, bf16[2,4,64,512]{3,2,0,1:T(8,128)(2,1)S(1)}, u32[]{:S(2)}, u32[]{:S(2)}) collective-permute-start(bf16[2,4,64,512]{3,2,0,1:T(8,128)(2,1)S(1)} %bitcast.169), channel_id=1, source_target_pairs={{160,0},{164,4},{168,8},{172,12},{176,16},{180,20},{184,24},{188,2... | collective-permute-start | bytes 1572872 | tf_op jit(solution)/shard_map/ppermute | solution.py:65
  232.8 53.4 %collective-permute-start.27 = (bf16[2,4,64,512]{3,2,0,1:T(8,128)(2,1)S(1)}, bf16[2,4,64,512]{3,2,0,1:T(8,128)(2,1)S(1)}, u32[]{:S(2)}, u32[]{:S(2)}) collective-permute-start(bf16[2,4,64,512]{3,2,0,1:T(8,128)(2,1)S(1)} %bitcast.168), channel_id=1, source_target_pairs={{64,0},{68,4},{72,8},{76,12},{80,16},{84,20},{88,24},{92,28},{96,3... | collective-permute-start | bytes 1572872 | tf_op jit(solution)/shard_map/ppermute | solution.py:65
  235.4 50.8 %collective-permute-start.28 = (bf16[2,4,64,512]{3,2,0,1:T(8,128)(2,1)S(1)}, bf16[2,4,64,512]{3,2,0,1:T(8,128)(2,1)S(1)}, u32[]{:S(2)}, u32[]{:S(2)}) collective-permute-start(bf16[2,4,64,512]{3,2,0,1:T(8,128)(2,1)S(1)} %bitcast.167), channel_id=1, source_target_pairs={{96,0},{100,4},{104,8},{108,12},{112,16},{116,20},{120,24},{124,28... | collective-permute-start | bytes 1572872 | tf_op jit(solution)/shard_map/ppermute | solution.py:65
  240.6 45.6 %collective-permute-start.26 = (bf16[2,4,64,512]{3,2,0,1:T(8,128)(2,1)S(1)}, bf16[2,4,64,512]{3,2,0,1:T(8,128)(2,1)S(1)}, u32[]{:S(2)}, u32[]{:S(2)}) collective-permute-start(bf16[2,4,64,512]{3,2,0,1:T(8,128)(2,1)S(1)} %bitcast.166), channel_id=1, source_target_pairs={{128,0},{132,4},{136,8},{140,12},{144,16},{148,20},{152,24},{156,2... | collective-permute-start | bytes 1572872 | tf_op jit(solution)/shard_map/ppermute | solution.py:65
  240.7 21.6 %collective-permute-start.24 = (bf16[2,64,512]{2,1,0:T(8,128)(2,1)S(1)}, bf16[2,64,512]{2,1,0:T(8,128)(2,1)S(1)}, u32[]{:S(2)}, u32[]{:S(2)}) collective-permute-start(bf16[2,64,512]{2,1,0:T(8,128)(2,1)S(1)} %get-tuple-element.76), channel_id=1, source_target_pairs={{128,0},{129,1},{130,2},{131,3}} | collective-permute-start | bytes 393224 | tf_op jit(solution)/shard_map/ppermute | solution.py:58
  262.3 23.8 %collective-permute-start.23 = (bf16[2,64,512]{2,1,0:T(8,128)(2,1)S(1)}, bf16[2,64,512]{2,1,0:T(8,128)(2,1)S(1)}, u32[]{:S(2)}, u32[]{:S(2)}) collective-permute-start(bf16[2,64,512]{2,1,0:T(8,128)(2,1)S(1)} %get-tuple-element.76), channel_id=1, source_target_pairs={{64,0},{65,1},{66,2},{67,3}} | collective-permute-start | bytes 393224 | tf_op jit(solution)/shard_map/ppermute | solution.py:58
  (23 other events, 354.0 us)
Sparse Core Ops, SparseCore 0:
  24.5 22.8 all-gather.1
  186.0 24.5 reduce-scatter.1

commit v2 on v1

v2 whole, which is shorter than its diff:
```python
import functools
import math

import jax
import jax.numpy as jnp
from jax import lax
from jax.experimental import pallas as pl
from jax.experimental.pallas import tpu as pltpu
from jax.sharding import PartitionSpec as P

HDIM = 128
BS = 64


def tree_strides(count, radix=4):
    strides, stride = [], 1
    while stride < count:
        strides.append((stride, min(radix, count // stride)))
        stride *= radix
    return strides


def spread_down(value, axis):
    count = lax.axis_size(axis)
    position = lax.axis_index(axis)
    for stride, ways in reversed(tree_strides(count)):
        digit = (position // stride) % ways
        arrivals = [
            lax.ppermute(
                value, axis, [(i, i + turn * stride) for i in range(0, count, stride * ways)]
            )
            for turn in range(1, ways)
        ]
        holds = position % (stride * ways) == 0
        fresh = arrivals[0]
        for turn in range(2, ways):
            fresh = jnp.where(digit == turn, arrivals[turn - 1], fresh)
        value = jnp.where(holds, value, fresh)
    return value


def sum_up(value, axis):
    count = lax.axis_size(axis)
    for stride, ways in tree_strides(count):
        sent = value.astype(jnp.bfloat16)
        for turn in range(1, ways):
            route = [(i + turn * stride, i) for i in range(0, count, stride * ways)]
            value = value + lax.ppermute(sent, axis, route).astype(jnp.float32)
    return value


def from_behind(block, axis, distance):
    devices = range(lax.axis_size(axis))
    route = [((i - distance) % len(devices), i) for i in devices]
    return lax.ppermute(block, axis, route)


def shifted(block, axis, distance):
    devices = range(lax.axis_size(axis))
    route = [(i - distance, i) for i in devices if i - distance in devices]
    return lax.ppermute(block, axis, route)


def rows_at(index):
    return pl.ds(pl.multiple_of(index * BS, BS), BS)


def attend(
    run_blocks,
    scale,
    picks,
    bias_ref,
    q_ref,
    g_ref,
    own_ref,
    low_ref,
    high_ref,
    anchor_ref,
    r0_ref,
    r1_ref,
    r2_ref,
    r3_ref,
    attn_ref,
    dq_ref,
    down_ref,
    dlow_ref,
    dhigh_ref,
    danchor_ref,
    s0_ref,
    s1_ref,
    s2_ref,
    s3_ref,
    frame,
    pool,
    frame_sum,
    anchor_sum,
    pool_sum,
):
    run_rows = run_blocks * BS
    frame[:, :BS] = low_ref[...]
    frame[:, BS : BS + run_rows] = own_ref[...]
    frame[:, BS + run_rows :] = high_ref[...]
    for turn, ref in enumerate((r0_ref, r1_ref, r2_ref, r3_ref)):
        pool[:, turn * run_rows : (turn + 1) * run_rows] = ref[...]
    frame_sum[...] = jnp.zeros_like(frame_sum)
    anchor_sum[...] = jnp.zeros_like(anchor_sum)
    pool_sum[...] = jnp.zeros_like(pool_sum)

    for b in range(run_blocks):
        rows = slice(b * BS, (b + 1) * BS)
        q = q_ref[rows, :]
        g = g_ref[rows, :]
        chosen = [rows_at(picks[b * 3 + slot]) for slot in range(3)]
        k_list, v_list = (
            jnp.concatenate(
                [frame[which, b * BS : (b + 3) * BS, :], anchor_ref[which]]
                + [pool[which, at, :] for at in chosen],
                axis=0,
            )
            for which in (0, 1)
        )
        across = (((1,), (1,)), ((), ()))
        along = (((0,), (0,)), ((), ()))
        logits = lax.dot_general(q, k_list, across, preferred_element_type=jnp.float32)
        grad_probs = lax.dot_general(g, v_list, across, preferred_element_type=jnp.float32)
        logits = logits * scale + bias_ref[b : b + 1, :]
        raw = jnp.exp(logits - jnp.max(logits, axis=1, keepdims=True))
        probs = raw * (1.0 / jnp.sum(raw, axis=1, keepdims=True))
        probs_b = probs.astype(jnp.bfloat16)
        attn = jnp.dot(probs_b, v_list, preferred_element_type=jnp.float32).astype(jnp.bfloat16)
        attn_ref[rows, :] = attn
        delta = jnp.sum(g.astype(jnp.float32) * attn.astype(jnp.float32), axis=1, keepdims=True)
        grad_logits = (probs * (grad_probs - delta)).astype(jnp.bfloat16)
        dq = jnp.dot(grad_logits, k_list, preferred_element_type=jnp.float32)
        dq_ref[rows, :] = (dq * scale).astype(jnp.bfloat16)
        for which, left, right in ((0, grad_logits, q), (1, probs_b, g)):
            parts = lax.dot_general(left, right, along, preferred_element_type=jnp.float32)
            frame_sum[which, b * BS : (b + 3) * BS, :] += parts[: 3 * BS]
            anchor_sum[which] += parts[3 * BS : 4 * BS]
            for slot, at in enumerate(chosen):
                pool_sum[which, at, :] += parts[(4 + slot) * BS : (5 + slot) * BS]

    for which, factor in ((0, scale), (1, 1.0)):
        down_ref[which] = frame_sum[which, BS : BS + run_rows, :] * factor
        dlow_ref[which] = (frame_sum[which, :BS, :] * factor).astype(jnp.bfloat16)
        dhigh_ref[which] = (frame_sum[which, BS + run_rows :, :] * factor).astype(jnp.bfloat16)
        danchor_ref[which] = anchor_sum[which] * factor
        for turn, ref in enumerate((s0_ref, s1_ref, s2_ref, s3_ref)):
            ref[which] = (
                pool_sum[which, turn * run_rows : (turn + 1) * run_rows, :] * factor
            ).astype(jnp.bfloat16)


def attention_both_ways(picks, bias, queries, grad_attention, own, low, high, anchor, arrivals):
    row_count, width_here = queries.shape
    heads_here = width_here // HDIM
    run_blocks = row_count // BS
    flat = pl.BlockSpec((row_count, HDIM), lambda h, p: (0, h))
    run = pl.BlockSpec((2, row_count, HDIM), lambda h, p: (0, 0, h))
    edge = pl.BlockSpec((2, BS, HDIM), lambda h, p: (0, 0, h))
    shape = jax.ShapeDtypeStruct
    flat_shape = shape((row_count, width_here), jnp.bfloat16)
    run_shape = shape((2, row_count, width_here), jnp.bfloat16)
    edge_shape = shape((2, BS, width_here), jnp.bfloat16)
    pairs = row_count * 7 * BS * width_here
    return pl.pallas_call(
        functools.partial(attend, run_blocks, 1.0 / math.sqrt(HDIM)),
        grid_spec=pltpu.PrefetchScalarGridSpec(
            num_scalar_prefetch=1,
            grid=(heads_here,),
            in_specs=[pl.BlockSpec(bias.shape, lambda h, p: (0, 0)), flat, flat, run]
            + [edge] * 3
            + [run] * 4,
            out_specs=[flat, flat, run, edge, edge, edge] + [run] * 4,
            scratch_shapes=[
                pltpu.VMEM((2, row_count + 2 * BS, HDIM), jnp.bfloat16),
                pltpu.VMEM((2, 4 * row_count, HDIM), jnp.bfloat16),
                pltpu.VMEM((2, row_count + 2 * BS, HDIM), jnp.float32),
                pltpu.VMEM((2, BS, HDIM), jnp.float32),
                pltpu.VMEM((2, 4 * row_count, HDIM), jnp.float32),
            ],
        ),
        out_shape=[
            flat_shape,
            flat_shape,
            shape((2, row_count, width_here), jnp.float32),
            edge_shape,
            edge_shape,
            shape((2, BS, width_here), jnp.float32),
        ]
        + [run_shape] * 4,
        cost_estimate=pl.CostEstimate(
            flops=10 * pairs, bytes_accessed=8 * 2**20, transcendentals=pairs // HDIM
        ),
        name="attention_both_ways",
    )(picks, bias, queries, grad_attention, own, low, high, anchor, *arrivals)


def body(queries, keys, values, out_weight, upstream, rand_round, rand_block):
    row_count, width_here = queries.shape
    run_blocks = row_count // BS
    axis_count = lax.axis_size("ctx")
    position = lax.axis_index("ctx")
    offsets = [axis_count * factor // 8 for factor in (4, 2, 3, 5)]
    total_blocks = axis_count * run_blocks
    blocks = position * run_blocks + jnp.arange(run_blocks, dtype=jnp.int32)
    always = jnp.ones((run_blocks,), jnp.bool_)
    allowed = jnp.stack(
        [blocks >= 1, always, blocks <= total_blocks - 2, blocks >= 2, always, always, always],
        axis=1,
    )
    bias = jnp.repeat(jnp.where(allowed, 0.0, -jnp.inf).astype(jnp.float32), BS, axis=1)
    picks = (rand_round * run_blocks + rand_block).reshape(-1)
    key_value = jnp.stack([keys, values])
    low = shifted(key_value[:, -BS:], "ctx", 1)
    high = shifted(key_value[:, :BS], "ctx", -1)
    anchor = spread_down(key_value[:, :BS], "ctx")
    arrivals = [from_behind(key_value, "ctx", offset) for offset in offsets]
    grad_attention = lax.dot_general(
        lax.all_gather(upstream, "head", axis=1, tiled=True),
        out_weight,
        (((1,), (1,)), ((), ())),
        preferred_element_type=jnp.float32,
    ).astype(jnp.bfloat16)
    attention, grad_queries, own_grad, low_grad, high_grad, anchor_grad, *spread = (
        attention_both_ways(
            picks, bias, queries, grad_attention, key_value, low, high, anchor, arrivals
        )
    )
    partial_out = jnp.dot(attention, out_weight, preferred_element_type=jnp.float32)
    mixed = lax.psum_scatter(
        partial_out.astype(jnp.bfloat16), "head", scatter_dimension=1, tiled=True
    )
    anchor_grad = sum_up(anchor_grad, "ctx")
    from_high = shifted(low_grad, "ctx", -1).astype(jnp.float32)
    from_low = shifted(high_grad, "ctx", 1).astype(jnp.float32)
    first = from_low + jnp.where(position == 0, anchor_grad, 0.0)
    for sent, offset in zip(spread, offsets):
        own_grad = own_grad + from_behind(sent, "ctx", -offset).astype(jnp.float32)
    own_grad = jnp.concatenate(
        [
            own_grad[:, :BS] + first,
            own_grad[:, BS:-BS],
            own_grad[:, -BS:] + from_high,
        ],
        axis=1,
    ).astype(jnp.bfloat16)
    return (mixed, grad_queries, own_grad[0], own_grad[1])


def solution(mesh):
    placed = (
        P("ctx", "head"),
        P("ctx", "head"),
        P("ctx", "head"),
        P("head", None),
        P("ctx", "head"),
        P("ctx", None),
        P("ctx", None),
    )
    return jax.shard_map(
        body,
        mesh=mesh,
        in_specs=placed,
        out_specs=(P("ctx", "head"), P("ctx", "head"), P("ctx", "head"), P("ctx", "head")),
        check_vma=False,
    )
```

time: 296 us -> 220 us (0.74)
  local copies, waits for them, and re-layouts: 61.4 us -> 4.87 us
  other arithmetic: 36.4 us -> 9.92 us
  waiting for transfers between devices: 77 us -> 98.9 us
  starting transfers between devices: 88 us -> 70 us
  Pallas kernels: 0 us -> 14.9 us
  matrix products: 16.8 us -> 5.38 us
    ppermute x8, waiting for transfers between devices: 31 us -> 0.24 us  [from_behind(): return lax.ppermute(block, axis, route)]
    ppermute x9, waiting for transfers between devices: 41.7 us -> 68.9 us  [sum_up(): value = value + lax.ppermute(sent, axis, route).astype(jnp.float32)]
    ppermute x9, starting transfers between devices: 45.1 us -> 23.7 us  [spread_down(): lax.ppermute(value, axis, [(i, i + turn * stride) for i in range(0, count...]
    ppermute x9, waiting for transfers between devices: 3.71 us -> 24.2 us  [spread_down(): lax.ppermute(value, axis, [(i, i + turn * stride) for i in range(0, count...]
    another operation x7 -> x2, local copies, waits for them, and re-layouts: 20.1 us -> 0.52 us  [the longest x3 11.1 us: body(): jnp.stack([partial_keys, partial_values])]
    pallas_call x0 -> x1, Pallas kernels: none -> 14.9 us  [attention_both_ways(): pl.pallas_call(functools.partial(attend, run_blocks, 1.0 / math.sqrt(HDIM...]
    dot_general x5 -> x0, matrix products: 11 us -> none  [the longest x1 3.63 us: body(): jnp.einsum('bhqjk,bjkhd->bqhd', probabilities_blocked, value_bundle, pref...]
    unnamed x42 -> x20, local copies, waits for them, and re-layouts: 12 us -> 1.32 us
  transfers between devices with their start and end apart: 32 -> 32, of which waited for: 8 -> 14; matrix products, arithmetic and copies ran while one was open for 24% -> 7% of each run, Pallas kernels for 0% -> 0%
where the time goes in v2:
time: 220 us; the launch traced here: 218 us
  waiting for transfers between devices  98.9 us (45%)
  starting transfers between devices  70 us (32%)
  Pallas kernels  14.9 us (7%)
  between operations  14.5 us (7%)
  other arithmetic  9.92 us (5%)
  matrix products  5.38 us (2%)
  local copies, waits for them, and re-layouts  4.87 us (2%)
    ppermute x9, waiting for transfers between devices, sum_up(): value = value + lax.ppermute(sent, axis, route).astype(jnp.float32)  68.9 us
    ppermute x8, starting transfers between devices, from_behind(): return lax.ppermute(block, axis, route)  27.3 us
    ppermute x9, waiting for transfers between devices, spread_down(): lax.ppermute(value, axis, [(i, i + turn * stride) for i in range(0, count...  24.2 us
    ppermute x9, starting transfers between devices, spread_down(): lax.ppermute(value, axis, [(i, i + turn * stride) for i in range(0, count...  23.7 us
    pallas_call x1, Pallas kernels, attention_both_ways(): pl.pallas_call(functools.partial(attend, run_blocks, 1.0 / math.sqrt(HDIM...  14.9 us
    ppermute x9, starting transfers between devices, sum_up(): value = value + lax.ppermute(sent, axis, route).astype(jnp.float32)  11.7 us
    ppermute x4, starting transfers between devices, shifted(): return lax.ppermute(block, axis, route)  7.11 us
    ppermute x4, waiting for transfers between devices, shifted(): return lax.ppermute(block, axis, route)  4.77 us
  transfers between devices with their start and end apart: 32, of which 14 were waited for; matrix products, arithmetic and copies ran while one was open for 7% of the time, Pallas kernels for 0%

profile of v2, /device:TPU:8, one launch (start us, length us, event | category | flops | bytes accessed | tf_op | source)
XLA Modules:
  0.0 218.4 jit_solution(15890977693418151785)
XLA Ops:
  9.6 9.1 %collective-permute-start.4 = (bf16[2,64,512]{2,1,0:T(8,128)(2,1)S(1)}, bf16[2,64,512]{2,1,0:T(8,128)(2,1)S(1)}, u32[]{:S(2)}, u32[]{:S(2)}) collective-permute-start(bf16[2,64,512]{2,1,0:T(8,128)(2,1)S(1)} %get-tuple-element.30), channel_id=1, source_target_pairs={{0,64},{1,65},{2,66},{3,67}} | collective-permute-start | bytes 393224 | tf_op jit(solution)/shard_map/ppermute | solution.py:29
  20.0 2.4 %collective-permute-start.2 = (bf16[2,64,512]{2,1,0:T(8,128)(2,1)S(1)}, bf16[2,64,512]{2,1,0:T(8,128)(2,1)}, u32[]{:S(2)}, u32[]{:S(2)}) collective-permute-start(bf16[2,64,512]{2,1,0:T(8,128)(2,1)S(1)} %get-tuple-element.30), channel_id=1, source_target_pairs={{0,192},{1,193},{2,194},{3,195}} | collective-permute-start | bytes 393224 | tf_op jit(solution)/shard_map/ppermute | solution.py:29
  26.7 2.5 %collective-permute-start.6 = (bf16[2,64,512]{2,1,0:T(8,128)(2,1)S(1)}, bf16[2,64,512]{2,1,0:T(8,128)(2,1)}, u32[]{:S(2)}, u32[]{:S(2)}) collective-permute-start(bf16[2,64,512]{2,1,0:T(8,128)(2,1)S(1)} %select_select_fusion.2), channel_id=1, source_target_pairs={{0,32},{64,96},{128,160},{192,224},{1,33},{65,97},{129,161},{193,2... | collective-permute-start | bytes 393224 | tf_op jit(solution)/shard_map/ppermute | solution.py:29
  29.2 1.9 collective-permute-start.5
  33.6 18.0 %collective-permute-done.7 = bf16[2,64,512]{2,1,0:T(8,128)(2,1)S(1)} collective-permute-done((bf16[2,64,512]{2,1,0:T(8,128)(2,1)S(1)}, bf16[2,64,512]{2,1,0:T(8,128)(2,1)S(1)}, u32[]{:S(2)}, u32[]{:S(2)}) %collective-permute-start.7) | collective-permute-done | bytes 131104 | tf_op jit(solution)/shard_map/ppermute | solution.py:29
  51.6 2.8 %collective-permute-done.6 = bf16[2,64,512]{2,1,0:T(8,128)(2,1)} collective-permute-done((bf16[2,64,512]{2,1,0:T(8,128)(2,1)S(1)}, bf16[2,64,512]{2,1,0:T(8,128)(2,1)}, u32[]{:S(2)}, u32[]{:S(2)}) %collective-permute-start.6) | collective-permute-done | bytes 131104 | tf_op jit(solution)/shard_map/ppermute | solution.py:29
  54.4 1.9 collective-permute-done.5
  58.6 1.9 collective-permute-start.9
  60.5 1.9 collective-permute-start.8
  63.8 4.0 %collective-permute-start.14 = (bf16[2,256,512]{2,1,0:T(8,128)(2,1)S(1)}, bf16[2,256,512]{2,1,0:T(8,128)(2,1)}, u32[]{:S(2)}, u32[]{:S(2)}) collective-permute-start(bf16[2,256,512]{2,1,0:T(8,128)(2,1)S(1)} %pad_maximum_fusion.own_ref), channel_id=1, source_target_pairs={{96,0},{100,4},{104,8},{108,12},{112,16},{116,20},{120,24},{124,28... | collective-permute-start | bytes 1572872 | tf_op jit(solution)/shard_map/ppermute | solution.py:55
  67.8 3.3 %collective-permute-start = (bf16[2,64,512]{2,1,0:T(8,128)(2,1)}, bf16[2,64,512]{2,1,0:T(8,128)(2,1)}, u32[]{:S(2)}, u32[]{:S(2)}) collective-permute-start(bf16[2,64,512]{2,1,0:T(8,128)(2,1)} %get-tuple-element.31), channel_id=1, source_target_pairs={{0,4},{4,8},{8,12},{12,16},{16,20},{20,24},{24,28},{28,32},{32,36}... | collective-permute-start | bytes 393224 | tf_op jit(solution)/shard_map/ppermute | solution.py:61
  74.6 2.7 %convolution_convert_fusion.1.g_ref = bf16[256,512]{1,0:T(8,128)(2,1)} fusion(bf16[256,2048]{1,0:T(8,128)(2,1)} %all-gather.2.cloned.1.call-done, bf16[512,2048]{1,0:T(8,128)(2,1)S(1)} %copy-done), kind=kOutput, calls=%fused_computation.1 | convolution fusion | flops 537001984 | bytes 3407872 | tf_op jit(solution)/shard_map/dot_general | solution.py:219
  77.2 3.3 %collective-permute-done.1.high_ref = bf16[2,64,512]{2,1,0:T(8,128)(2,1)S(1)} collective-permute-done((bf16[2,64,512]{2,1,0:T(8,128)(2,1)S(1)}, bf16[2,64,512]{2,1,0:T(8,128)(2,1)S(1)}, u32[]{:S(2)}, u32[]{:S(2)}) %collective-permute-start.1) | collective-permute-done | bytes 131104 | tf_op jit(solution)/shard_map/ppermute | solution.py:61
  81.4 14.9 %attention_both_ways.1 = (bf16[256,512]{1,0:T(8,128)(2,1)}, bf16[256,512]{1,0:T(8,128)(2,1)}, f32[2,256,512]{2,1,0:T(8,128)}, bf16[2,64,512]{2,1,0:T(8,128)(2,1)...) custom-call(s32[12]{0:T(128)} %reshape.32.picks, ...), custom_call_target="tpu_custom_call" | custom-call | flops 587202560 | bytes 8388608 | tf_op jit(solution)/shard_map/attention_both_ways/pallas_call | solution.py:166
  96.3 2.7 %convolution_convert_fusion = bf16[256,2048]{1,0:T(8,128)(2,1)} fusion(bf16[256,512]{1,0:T(8,128)(2,1)} %get-tuple-element.14, bf16[512,2048]{1,0:T(8,128)(2,1)S(1)} %copy-done), kind=kOutput, calls=%fused_computation | convolution fusion | flops 537395200 | bytes 3407872 | tf_op jit(solution)/shard_map/dot_general | solution.py:230
  103.1 8.5 %collective-permute-done.22 = bf16[2,64,512]{2,1,0:T(8,128)(2,1)S(1)} collective-permute-done((bf16[2,64,512]{2,1,0:T(8,128)(2,1)S(1)}, bf16[2,64,512]{2,1,0:T(8,128)(2,1)S(1)}, u32[]{:S(2)}, u32[]{:S(2)}) %collective-permute-start.22) | collective-permute-done | bytes 131104 | tf_op jit(solution)/shard_map/ppermute | solution.py:48
  114.6 6.6 %collective-permute-start.15 = (bf16[2,256,512]{2,1,0:T(8,128)(2,1)}, bf16[2,256,512]{2,1,0:T(8,128)(2,1)}, u32[]{:S(2)}, u32[]{:S(2)}) collective-permute-start(bf16[2,256,512]{2,1,0:T(8,128)(2,1)} %get-tuple-element.17), channel_id=1, source_target_pairs={{128,0},{132,4},{136,8},{140,12},{144,16},{148,20},{152,24},{156,2... | collective-permute-start | bytes 1572872 | tf_op jit(solution)/shard_map/ppermute | solution.py:55
  121.2 12.4 %collective-permute-start.16 = (bf16[2,256,512]{2,1,0:T(8,128)(2,1)}, bf16[2,256,512]{2,1,0:T(8,128)(2,1)}, u32[]{:S(2)}, u32[]{:S(2)}) collective-permute-start(bf16[2,256,512]{2,1,0:T(8,128)(2,1)} %get-tuple-element.18), channel_id=1, source_target_pairs={{64,0},{68,4},{72,8},{76,12},{80,16},{84,20},{88,24},{92,28},{96,3... | collective-permute-start | bytes 1572872 | tf_op jit(solution)/shard_map/ppermute | solution.py:55
  133.7 4.0 %collective-permute-start.18 = (bf16[2,256,512]{2,1,0:T(8,128)(2,1)}, bf16[2,256,512]{2,1,0:T(8,128)(2,1)}, u32[]{:S(2)}, u32[]{:S(2)}) collective-permute-start(bf16[2,256,512]{2,1,0:T(8,128)(2,1)} %get-tuple-element.20), channel_id=1, source_target_pairs={{160,0},{164,4},{168,8},{172,12},{176,16},{180,20},{184,24},{188,2... | collective-permute-start | bytes 1572872 | tf_op jit(solution)/shard_map/ppermute | solution.py:55
  139.0 43.8 %collective-permute-done.24 = bf16[2,64,512]{2,1,0:T(8,128)(2,1)} collective-permute-done((bf16[2,64,512]{2,1,0:T(8,128)(2,1)}, bf16[2,64,512]{2,1,0:T(8,128)(2,1)}, u32[]{:S(2)}, u32[]{:S(2)}) %collective-permute-start.24) | collective-permute-done | bytes 131104 | tf_op jit(solution)/shard_map/ppermute | solution.py:48
  184.1 6.3 %collective-permute-done.23 = bf16[2,64,512]{2,1,0:T(8,128)(2,1)} collective-permute-done((bf16[2,64,512]{2,1,0:T(8,128)(2,1)}, bf16[2,64,512]{2,1,0:T(8,128)(2,1)}, u32[]{:S(2)}, u32[]{:S(2)}) %collective-permute-start.23) | collective-permute-done | bytes 131104 | tf_op jit(solution)/shard_map/ppermute | solution.py:48
  198.2 1.9 convert_add_fusion
  200.2 8.4 %collective-permute-done.28 = bf16[2,64,512]{2,1,0:T(8,128)(2,1)S(1)} collective-permute-done((bf16[2,64,512]{2,1,0:T(8,128)(2,1)S(1)}, bf16[2,64,512]{2,1,0:T(8,128)(2,1)S(1)}, u32[]{:S(2)}, u32[]{:S(2)}) %collective-permute-start.28) | collective-permute-done | bytes 131104 | tf_op jit(solution)/shard_map/ppermute | solution.py:48
  208.5 2.0 collective-permute-done.27
  (88 shorter events, 36.7 us)
Async XLA Ops:
  7.2 67.3 %all-gather.2.cloned.1.call-start = ((), (), s32[]{:S(2)}) async-start(), calls=%async_computation.1 | async-start | bytes 1310720 | tf_op jit(solution)/shard_map/all_gather | solution.py:220
  7.9 203.6 %reduce-scatter.2.cloned.1.call-start = ((), (), s32[]{:S(2)}) async-start(), calls=%async_computation.2 | async-start | bytes 1310720 | tf_op jit(solution)/shard_map/reduce_scatter | solution.py:231
  9.6 14.2 %collective-permute-start.4 = (bf16[2,64,512]{2,1,0:T(8,128)(2,1)S(1)}, bf16[2,64,512]{2,1,0:T(8,128)(2,1)S(1)}, u32[]{:S(2)}, u32[]{:S(2)}) collective-permute-start(bf16[2,64,512]{2,1,0:T(8,128)(2,1)S(1)} %get-tuple-element.30), channel_id=1, source_target_pairs={{0,64},{1,65},{2,66},{3,67}} | collective-permute-start | bytes 393224 | tf_op jit(solution)/shard_map/ppermute | solution.py:29
  23.5 57.0 %collective-permute-start.13 = (bf16[2,256,512]{2,1,0:T(8,128)(2,1)S(1)}, bf16[2,256,512]{2,1,0:T(8,128)(2,1)S(1)}, u32[]{:S(2)}, u32[]{:S(2)}) collective-permute-start(bf16[2,256,512]{2,1,0:T(8,128)(2,1)S(1)} %pad_maximum_fusion.own_ref), channel_id=1, source_target_pairs={{160,0},{164,4},{168,8},{172,12},{176,16},{180,20},{184,24},{188,2... | collective-permute-start | bytes 1572872 | tf_op jit(solution)/shard_map/ppermute | solution.py:55
  23.6 56.9 %collective-permute-start.12 = (bf16[2,256,512]{2,1,0:T(8,128)(2,1)S(1)}, bf16[2,256,512]{2,1,0:T(8,128)(2,1)}, u32[]{:S(2)}, u32[]{:S(2)}) collective-permute-start(bf16[2,256,512]{2,1,0:T(8,128)(2,1)S(1)} %pad_maximum_fusion.own_ref), channel_id=1, source_target_pairs={{192,0},{196,4},{200,8},{204,12},{208,16},{212,20},{216,24},{220,2... | collective-permute-start | bytes 1572872 | tf_op jit(solution)/shard_map/ppermute | solution.py:55
  25.4 26.2 %collective-permute-start.7 = (bf16[2,64,512]{2,1,0:T(8,128)(2,1)S(1)}, bf16[2,64,512]{2,1,0:T(8,128)(2,1)S(1)}, u32[]{:S(2)}, u32[]{:S(2)}) collective-permute-start(bf16[2,64,512]{2,1,0:T(8,128)(2,1)S(1)} %select_select_fusion.2), channel_id=1, source_target_pairs={{0,16},{64,80},{128,144},{192,208},{1,17},{65,81},{129,145},{193,2... | collective-permute-start | bytes 393224 | tf_op jit(solution)/shard_map/ppermute | solution.py:29
  26.7 27.7 %collective-permute-start.6 = (bf16[2,64,512]{2,1,0:T(8,128)(2,1)S(1)}, bf16[2,64,512]{2,1,0:T(8,128)(2,1)}, u32[]{:S(2)}, u32[]{:S(2)}) collective-permute-start(bf16[2,64,512]{2,1,0:T(8,128)(2,1)S(1)} %select_select_fusion.2), channel_id=1, source_target_pairs={{0,32},{64,96},{128,160},{192,224},{1,33},{65,97},{129,161},{193,2... | collective-permute-start | bytes 393224 | tf_op jit(solution)/shard_map/ppermute | solution.py:29
  29.2 27.1 %collective-permute-start.5 = (bf16[2,64,512]{2,1,0:T(8,128)(2,1)S(1)}, bf16[2,64,512]{2,1,0:T(8,128)(2,1)}, u32[]{:S(2)}, u32[]{:S(2)}) collective-permute-start(bf16[2,64,512]{2,1,0:T(8,128)(2,1)S(1)} %select_select_fusion.2), channel_id=1, source_target_pairs={{0,48},{64,112},{128,176},{192,240},{1,49},{65,113},{129,177},{193... | collective-permute-start | bytes 393224 | tf_op jit(solution)/shard_map/ppermute | solution.py:29
  63.2 17.3 %collective-permute-start.11 = (bf16[2,256,512]{2,1,0:T(8,128)(2,1)S(1)}, bf16[2,256,512]{2,1,0:T(8,128)(2,1)}, u32[]{:S(2)}, u32[]{:S(2)}) collective-permute-start(bf16[2,256,512]{2,1,0:T(8,128)(2,1)S(1)} %pad_maximum_fusion.own_ref), channel_id=1, source_target_pairs={{128,0},{132,4},{136,8},{140,12},{144,16},{148,20},{152,24},{156,2... | collective-permute-start | bytes 1572872 | tf_op jit(solution)/shard_map/ppermute | solution.py:55
  63.8 17.0 %collective-permute-start.14 = (bf16[2,256,512]{2,1,0:T(8,128)(2,1)S(1)}, bf16[2,256,512]{2,1,0:T(8,128)(2,1)}, u32[]{:S(2)}, u32[]{:S(2)}) collective-permute-start(bf16[2,256,512]{2,1,0:T(8,128)(2,1)S(1)} %pad_maximum_fusion.own_ref), channel_id=1, source_target_pairs={{96,0},{100,4},{104,8},{108,12},{112,16},{116,20},{120,24},{124,28... | collective-permute-start | bytes 1572872 | tf_op jit(solution)/shard_map/ppermute | solution.py:55
  99.1 12.5 %collective-permute-start.22 = (bf16[2,64,512]{2,1,0:T(8,128)(2,1)S(1)}, bf16[2,64,512]{2,1,0:T(8,128)(2,1)S(1)}, u32[]{:S(2)}, u32[]{:S(2)}) collective-permute-start(bf16[2,64,512]{2,1,0:T(8,128)(2,1)S(1)} %convert_element_type.68), channel_id=1, source_target_pairs={{12,0},{28,16},{44,32},{60,48},{76,64},{92,80},{108,96},{124,112},... | collective-permute-start | bytes 393224 | tf_op jit(solution)/shard_map/ppermute | solution.py:48
  100.5 11.1 %collective-permute-start.21 = (bf16[2,64,512]{2,1,0:T(8,128)(2,1)S(1)}, bf16[2,64,512]{2,1,0:T(8,128)(2,1)}, u32[]{:S(2)}, u32[]{:S(2)}) collective-permute-start(bf16[2,64,512]{2,1,0:T(8,128)(2,1)S(1)} %convert_element_type.68), channel_id=1, source_target_pairs={{8,0},{24,16},{40,32},{56,48},{72,64},{88,80},{104,96},{120,112},{... | collective-permute-start | bytes 393224 | tf_op jit(solution)/shard_map/ppermute | solution.py:48
  101.8 9.8 %collective-permute-start.20 = (bf16[2,64,512]{2,1,0:T(8,128)(2,1)S(1)}, bf16[2,64,512]{2,1,0:T(8,128)(2,1)}, u32[]{:S(2)}, u32[]{:S(2)}) collective-permute-start(bf16[2,64,512]{2,1,0:T(8,128)(2,1)S(1)} %convert_element_type.68), channel_id=1, source_target_pairs={{4,0},{20,16},{36,32},{52,48},{68,64},{84,80},{100,96},{116,112},{... | collective-permute-start | bytes 393224 | tf_op jit(solution)/shard_map/ppermute | solution.py:48
  113.3 24.4 %collective-permute-start.25 = (bf16[2,64,512]{2,1,0:T(8,128)(2,1)}, bf16[2,64,512]{2,1,0:T(8,128)(2,1)}, u32[]{:S(2)}, u32[]{:S(2)}) collective-permute-start(bf16[2,64,512]{2,1,0:T(8,128)(2,1)} %fusion.4), channel_id=1, source_target_pairs={{48,0},{112,64},{176,128},{240,192},{49,1},{113,65},{177,129},{241... | collective-permute-start | bytes 393224 | tf_op jit(solution)/shard_map/ppermute | solution.py:48
  114.6 78.4 %collective-permute-start.15 = (bf16[2,256,512]{2,1,0:T(8,128)(2,1)}, bf16[2,256,512]{2,1,0:T(8,128)(2,1)}, u32[]{:S(2)}, u32[]{:S(2)}) collective-permute-start(bf16[2,256,512]{2,1,0:T(8,128)(2,1)} %get-tuple-element.17), channel_id=1, source_target_pairs={{128,0},{132,4},{136,8},{140,12},{144,16},{148,20},{152,24},{156,2... | collective-permute-start | bytes 1572872 | tf_op jit(solution)/shard_map/ppermute | solution.py:55
  121.2 73.1 %collective-permute-start.16 = (bf16[2,256,512]{2,1,0:T(8,128)(2,1)}, bf16[2,256,512]{2,1,0:T(8,128)(2,1)}, u32[]{:S(2)}, u32[]{:S(2)}) collective-permute-start(bf16[2,256,512]{2,1,0:T(8,128)(2,1)} %get-tuple-element.18), channel_id=1, source_target_pairs={{64,0},{68,4},{72,8},{76,12},{80,16},{84,20},{88,24},{92,28},{96,3... | collective-permute-start | bytes 1572872 | tf_op jit(solution)/shard_map/ppermute | solution.py:55
  133.6 62.0 %collective-permute-start.17 = (bf16[2,256,512]{2,1,0:T(8,128)(2,1)}, bf16[2,256,512]{2,1,0:T(8,128)(2,1)}, u32[]{:S(2)}, u32[]{:S(2)}) collective-permute-start(bf16[2,256,512]{2,1,0:T(8,128)(2,1)} %get-tuple-element.19), channel_id=1, source_target_pairs={{96,0},{100,4},{104,8},{108,12},{112,16},{116,20},{120,24},{124,28... | collective-permute-start | bytes 1572872 | tf_op jit(solution)/shard_map/ppermute | solution.py:55
  133.7 63.3 %collective-permute-start.18 = (bf16[2,256,512]{2,1,0:T(8,128)(2,1)}, bf16[2,256,512]{2,1,0:T(8,128)(2,1)}, u32[]{:S(2)}, u32[]{:S(2)}) collective-permute-start(bf16[2,256,512]{2,1,0:T(8,128)(2,1)} %get-tuple-element.20), channel_id=1, source_target_pairs={{160,0},{164,4},{168,8},{172,12},{176,16},{180,20},{184,24},{188,2... | collective-permute-start | bytes 1572872 | tf_op jit(solution)/shard_map/ppermute | solution.py:55
  137.7 45.1 %collective-permute-start.24 = (bf16[2,64,512]{2,1,0:T(8,128)(2,1)}, bf16[2,64,512]{2,1,0:T(8,128)(2,1)}, u32[]{:S(2)}, u32[]{:S(2)}) collective-permute-start(bf16[2,64,512]{2,1,0:T(8,128)(2,1)} %fusion.4), channel_id=1, source_target_pairs={{32,0},{96,64},{160,128},{224,192},{33,1},{97,65},{161,129},{225,1... | collective-permute-start | bytes 393224 | tf_op jit(solution)/shard_map/ppermute | solution.py:48
  182.8 7.6 %collective-permute-start.23 = (bf16[2,64,512]{2,1,0:T(8,128)(2,1)}, bf16[2,64,512]{2,1,0:T(8,128)(2,1)}, u32[]{:S(2)}, u32[]{:S(2)}) collective-permute-start(bf16[2,64,512]{2,1,0:T(8,128)(2,1)} %fusion.4), channel_id=1, source_target_pairs={{16,0},{80,64},{144,128},{208,192},{17,1},{81,65},{145,129},{209,1... | collective-permute-start | bytes 393224 | tf_op jit(solution)/shard_map/ppermute | solution.py:48
  190.4 9.7 %collective-permute-start.19 = (bf16[2,64,512]{2,1,0:T(8,128)(2,1)}, bf16[2,64,512]{2,1,0:T(8,128)(2,1)S(1)}, u32[]{:S(2)}, u32[]{:S(2)}) collective-permute-start(bf16[2,64,512]{2,1,0:T(8,128)(2,1)} %get-tuple-element.21), channel_id=1, source_target_pairs={{0,4},{4,8},{8,12},{12,16},{16,20},{20,24},{24,28},{28,32},{32,36}... | collective-permute-start | bytes 393224 | tf_op jit(solution)/shard_map/ppermute | solution.py:61
  194.3 14.2 %collective-permute-start.28 = (bf16[2,64,512]{2,1,0:T(8,128)(2,1)S(1)}, bf16[2,64,512]{2,1,0:T(8,128)(2,1)S(1)}, u32[]{:S(2)}, u32[]{:S(2)}) collective-permute-start(bf16[2,64,512]{2,1,0:T(8,128)(2,1)S(1)} %get-tuple-element.24), channel_id=1, source_target_pairs={{192,0},{193,1},{194,2},{195,3}} | collective-permute-start | bytes 393224 | tf_op jit(solution)/shard_map/ppermute | solution.py:48
  195.6 14.9 %collective-permute-start.27 = (bf16[2,64,512]{2,1,0:T(8,128)(2,1)S(1)}, bf16[2,64,512]{2,1,0:T(8,128)(2,1)S(1)}, u32[]{:S(2)}, u32[]{:S(2)}) collective-permute-start(bf16[2,64,512]{2,1,0:T(8,128)(2,1)S(1)} %get-tuple-element.24), channel_id=1, source_target_pairs={{128,0},{129,1},{130,2},{131,3}} | collective-permute-start | bytes 393224 | tf_op jit(solution)/shard_map/ppermute | solution.py:48
  196.9 13.6 %collective-permute-start.26 = (bf16[2,64,512]{2,1,0:T(8,128)(2,1)S(1)}, bf16[2,64,512]{2,1,0:T(8,128)(2,1)S(1)}, u32[]{:S(2)}, u32[]{:S(2)}) collective-permute-start(bf16[2,64,512]{2,1,0:T(8,128)(2,1)S(1)} %get-tuple-element.24), channel_id=1, source_target_pairs={{64,0},{65,1},{66,2},{67,3}} | collective-permute-start | bytes 393224 | tf_op jit(solution)/shard_map/ppermute | solution.py:48
  (18 other events, 310.4 us)
Sparse Core Ops, SparseCore 0:
  9.8 39.3 all-gather.1
  99.1 42.5 reduce-scatter.1

commit v3 on v2

--- a/solution.py
+++ b/solution.py
@@ -39,14 +39,28 @@
     return value
 
 
-def sum_up(value, axis):
+def sum_stage(value, axis, stride, ways, left):
+    sent = value.astype(jnp.bfloat16)
     count = lax.axis_size(axis)
-    for stride, ways in tree_strides(count):
-        sent = value.astype(jnp.bfloat16)
-        for turn in range(1, ways):
-            route = [(i + turn * stride, i) for i in range(0, count, stride * ways)]
-            value = value + lax.ppermute(sent, axis, route).astype(jnp.float32)
+    bases = [i for i in range(count) if (i // stride) % ways == 0 and left(i)]
+    for turn in range(1, ways):
+        route = [(i + turn * stride, i) for i in bases]
+        value = value + lax.ppermute(sent, axis, route).astype(jnp.float32)
     return value
+
+
+def sum_up(value, axis, held):
+    done = []
+    strides = tree_strides(lax.axis_size(axis))
+    for stride, ways in reversed(strides):
+        above = list(done)
+        value = sum_stage(
+            value, axis, stride, ways, lambda i: all((i // s) % w == 0 for s, w in above)
+        )
+        done.append((stride, ways))
+        if len(done) == len(strides) - 1:
+            value, held = lax.optimization_barrier((value, held))
+    return value, held
 
 
 def from_behind(block, axis, distance):
@@ -231,7 +245,8 @@
     mixed = lax.psum_scatter(
         partial_out.astype(jnp.bfloat16), "head", scatter_dimension=1, tiled=True
     )
-    anchor_grad = sum_up(anchor_grad, "ctx")
+    anchor_grad, held = sum_up(anchor_grad, "ctx", spread[1:])
+    spread = [spread[0], *held]
     from_high = shifted(low_grad, "ctx", -1).astype(jnp.float32)
     from_low = shifted(high_grad, "ctx", 1).astype(jnp.float32)
     first = from_low + jnp.where(position == 0, anchor_grad, 0.0)

time: 220 us -> 218 us (level)
  waiting for transfers between devices: 98.9 us -> 118 us
  starting transfers between devices: 70 us -> 52.4 us
    ppermute x8, waiting for transfers between devices: 0.24 us -> 26.8 us  [from_behind(): return lax.ppermute(block, axis, route)]
    ppermute x8, starting transfers between devices: 27.3 us -> 8.58 us  [from_behind(): return lax.ppermute(block, axis, route)]
    ppermute x9, waiting for transfers between devices: 68.9 us -> 61.3 us  [sum_stage(): value = value + lax.ppermute(sent, axis, route).astype(jnp.float32)]
  transfers between devices with their start and end apart: 32 -> 32, of which waited for: 14 -> 16; matrix products, arithmetic and copies ran while one was open for 7% -> 7% of each run, Pallas kernels for 0% -> 0%
where the time goes in v3:
time: 218 us
  waiting for transfers between devices  118 us (54%)
  starting transfers between devices  52.4 us (24%)
  Pallas kernels  14.9 us (7%)
  between operations  14.5 us (7%)
  other arithmetic  8.31 us (4%)
  matrix products  5.38 us (2%)
  local copies, waits for them, and re-layouts  4.7 us (2%)
    ppermute x9, waiting for transfers between devices, sum_stage(): value = value + lax.ppermute(sent, axis, route).astype(jnp.float32)  61.3 us
    ppermute x8, waiting for transfers between devices, from_behind(): return lax.ppermute(block, axis, route)  26.8 us
    ppermute x9, waiting for transfers between devices, spread_down(): lax.ppermute(value, axis, [(i, i + turn * stride) for i in range(0, count...  24.1 us
    ppermute x9, starting transfers between devices, spread_down(): lax.ppermute(value, axis, [(i, i + turn * stride) for i in range(0, count...  23.7 us
    pallas_call x1, Pallas kernels, attention_both_ways(): pl.pallas_call(functools.partial(attend, run_blocks, 1.0 / math.sqrt(HDIM...  14.9 us
    ppermute x9, starting transfers between devices, sum_stage(): value = value + lax.ppermute(sent, axis, route).astype(jnp.float32)  11.6 us
    ppermute x8, starting transfers between devices, from_behind(): return lax.ppermute(block, axis, route)  8.58 us
    ppermute x4, starting transfers between devices, shifted(): return lax.ppermute(block, axis, route)  8.41 us
  transfers between devices with their start and end apart: 32, of which 16 were waited for; matrix products, arithmetic and copies ran while one was open for 7% of the time, Pallas kernels for 0%

profile of v3, /device:TPU:8, one launch (start us, length us, event | category | flops | bytes accessed | tf_op | source)
XLA Modules:
  0.0 217.8 jit_solution(10724280099072263934)
XLA Ops:
  9.6 9.1 %collective-permute-start.4 = (bf16[2,64,512]{2,1,0:T(8,128)(2,1)S(1)}, bf16[2,64,512]{2,1,0:T(8,128)(2,1)S(1)}, u32[]{:S(2)}, u32[]{:S(2)}) collective-permute-start(bf16[2,64,512]{2,1,0:T(8,128)(2,1)S(1)} %get-tuple-element.36), channel_id=1, source_target_pairs={{0,64},{1,65},{2,66},{3,67}} | collective-permute-start | bytes 393224 | tf_op jit(solution)/shard_map/ppermute | solution.py:29
  20.0 2.4 %collective-permute-start.2 = (bf16[2,64,512]{2,1,0:T(8,128)(2,1)S(1)}, bf16[2,64,512]{2,1,0:T(8,128)(2,1)}, u32[]{:S(2)}, u32[]{:S(2)}) collective-permute-start(bf16[2,64,512]{2,1,0:T(8,128)(2,1)S(1)} %get-tuple-element.36), channel_id=1, source_target_pairs={{0,192},{1,193},{2,194},{3,195}} | collective-permute-start | bytes 393224 | tf_op jit(solution)/shard_map/ppermute | solution.py:29
  26.8 2.5 %collective-permute-start.6 = (bf16[2,64,512]{2,1,0:T(8,128)(2,1)S(1)}, bf16[2,64,512]{2,1,0:T(8,128)(2,1)}, u32[]{:S(2)}, u32[]{:S(2)}) collective-permute-start(bf16[2,64,512]{2,1,0:T(8,128)(2,1)S(1)} %select_select_fusion.2), channel_id=1, source_target_pairs={{0,32},{64,96},{128,160},{192,224},{1,33},{65,97},{129,161},{193,2... | collective-permute-start | bytes 393224 | tf_op jit(solution)/shard_map/ppermute | solution.py:29
  29.2 1.9 collective-permute-start.5
  33.6 17.9 %collective-permute-done.7 = bf16[2,64,512]{2,1,0:T(8,128)(2,1)S(1)} collective-permute-done((bf16[2,64,512]{2,1,0:T(8,128)(2,1)S(1)}, bf16[2,64,512]{2,1,0:T(8,128)(2,1)S(1)}, u32[]{:S(2)}, u32[]{:S(2)}) %collective-permute-start.7) | collective-permute-done | bytes 131104 | tf_op jit(solution)/shard_map/ppermute | solution.py:29
  51.5 2.8 %collective-permute-done.6 = bf16[2,64,512]{2,1,0:T(8,128)(2,1)} collective-permute-done((bf16[2,64,512]{2,1,0:T(8,128)(2,1)S(1)}, bf16[2,64,512]{2,1,0:T(8,128)(2,1)}, u32[]{:S(2)}, u32[]{:S(2)}) %collective-permute-start.6) | collective-permute-done | bytes 131104 | tf_op jit(solution)/shard_map/ppermute | solution.py:29
  54.3 1.9 collective-permute-done.5
  58.4 1.9 collective-permute-start.9
  60.4 1.9 collective-permute-start.8
  63.6 4.0 %collective-permute-start.14 = (bf16[2,256,512]{2,1,0:T(8,128)(2,1)S(1)}, bf16[2,256,512]{2,1,0:T(8,128)(2,1)}, u32[]{:S(2)}, u32[]{:S(2)}) collective-permute-start(bf16[2,256,512]{2,1,0:T(8,128)(2,1)S(1)} %pad_maximum_fusion.own_ref), channel_id=1, source_target_pairs={{96,0},{100,4},{104,8},{108,12},{112,16},{116,20},{120,24},{124,28... | collective-permute-start | bytes 1572872 | tf_op jit(solution)/shard_map/ppermute | solution.py:69
  67.6 3.3 %collective-permute-start = (bf16[2,64,512]{2,1,0:T(8,128)(2,1)}, bf16[2,64,512]{2,1,0:T(8,128)(2,1)}, u32[]{:S(2)}, u32[]{:S(2)}) collective-permute-start(bf16[2,64,512]{2,1,0:T(8,128)(2,1)} %get-tuple-element.37), channel_id=1, source_target_pairs={{0,4},{4,8},{8,12},{12,16},{16,20},{20,24},{24,28},{28,32},{32,36}... | collective-permute-start | bytes 393224 | tf_op jit(solution)/shard_map/ppermute | solution.py:75
  74.4 2.7 %convolution_convert_fusion.1.g_ref = bf16[256,512]{1,0:T(8,128)(2,1)} fusion(bf16[256,2048]{1,0:T(8,128)(2,1)} %all-gather.2.cloned.1.call-done, bf16[512,2048]{1,0:T(8,128)(2,1)S(1)} %copy-done), kind=kOutput, calls=%fused_computation.1 | convolution fusion | flops 537001984 | bytes 3407872 | tf_op jit(solution)/shard_map/dot_general | solution.py:233
  77.1 3.3 %collective-permute-done.1.high_ref = bf16[2,64,512]{2,1,0:T(8,128)(2,1)S(1)} collective-permute-done((bf16[2,64,512]{2,1,0:T(8,128)(2,1)S(1)}, bf16[2,64,512]{2,1,0:T(8,128)(2,1)S(1)}, u32[]{:S(2)}, u32[]{:S(2)}) %collective-permute-start.1) | collective-permute-done | bytes 131104 | tf_op jit(solution)/shard_map/ppermute | solution.py:75
  81.2 14.9 %attention_both_ways.1 = (bf16[256,512]{1,0:T(8,128)(2,1)}, bf16[256,512]{1,0:T(8,128)(2,1)}, f32[2,256,512]{2,1,0:T(8,128)}, bf16[2,64,512]{2,1,0:T(8,128)(2,1)...) custom-call(s32[12]{0:T(128)} %reshape.32.picks, ...), custom_call_target="tpu_custom_call" | custom-call | flops 587202560 | bytes 8388608 | tf_op jit(solution)/shard_map/attention_both_ways/pallas_call | solution.py:180
  101.0 2.7 %convolution_convert_fusion = bf16[256,2048]{1,0:T(8,128)(2,1)} fusion(bf16[256,512]{1,0:T(8,128)(2,1)} %get-tuple-element.18, bf16[512,2048]{1,0:T(8,128)(2,1)S(1)} %copy-done), kind=kOutput, calls=%fused_computation | convolution fusion | flops 537395200 | bytes 3407872 | tf_op jit(solution)/shard_map/dot_general | solution.py:244
  103.7 16.4 %collective-permute-done.18 = bf16[2,64,512]{2,1,0:T(8,128)(2,1)S(1)} collective-permute-done((bf16[2,64,512]{2,1,0:T(8,128)(2,1)S(1)}, bf16[2,64,512]{2,1,0:T(8,128)(2,1)S(1)}, u32[]{:S(2)}, u32[]{:S(2)}) %collective-permute-start.18) | collective-permute-done | bytes 131104 | tf_op jit(solution)/shard_map/ppermute | solution.py:48
  124.8 4.9 %collective-permute-done.21 = bf16[2,64,512]{2,1,0:T(8,128)(2,1)S(1)} collective-permute-done((bf16[2,64,512]{2,1,0:T(8,128)(2,1)S(1)}, bf16[2,64,512]{2,1,0:T(8,128)(2,1)S(1)}, u32[]{:S(2)}, u32[]{:S(2)}) %collective-permute-start.21) | collective-permute-done | bytes 131104 | tf_op jit(solution)/shard_map/ppermute | solution.py:48
  129.7 35.7 %collective-permute-done.20 = bf16[2,64,512]{2,1,0:T(8,128)(2,1)S(1)} collective-permute-done((bf16[2,64,512]{2,1,0:T(8,128)(2,1)S(1)}, bf16[2,64,512]{2,1,0:T(8,128)(2,1)S(1)}, u32[]{:S(2)}, u32[]{:S(2)}) %collective-permute-start.20) | collective-permute-done | bytes 131104 | tf_op jit(solution)/shard_map/ppermute | solution.py:48
  165.7 4.1 %collective-permute-start.24 = (bf16[2,256,512]{2,1,0:T(8,128)(2,1)}, bf16[2,256,512]{2,1,0:T(8,128)(2,1)}, u32[]{:S(2)}, u32[]{:S(2)}) collective-permute-start(bf16[2,256,512]{2,1,0:T(8,128)(2,1)} %get-tuple-element.28), channel_id=1, source_target_pairs={{160,0},{164,4},{168,8},{172,12},{176,16},{180,20},{184,24},{188,2... | collective-permute-start | bytes 1572872 | tf_op jit(solution)/shard_map/ppermute | solution.py:69
  169.9 2.6 %collective-permute-start.25 = (bf16[2,64,512]{2,1,0:T(8,128)(2,1)}, bf16[2,64,512]{2,1,0:T(8,128)(2,1)S(1)}, u32[]{:S(2)}, u32[]{:S(2)}) collective-permute-start(bf16[2,64,512]{2,1,0:T(8,128)(2,1)} %get-tuple-element.29), channel_id=1, source_target_pairs={{0,4},{4,8},{8,12},{12,16},{16,20},{20,24},{24,28},{28,32},{32,36}... | collective-permute-start | bytes 393224 | tf_op jit(solution)/shard_map/ppermute | solution.py:75
  173.8 17.2 %collective-permute-done.22 = bf16[2,256,512]{2,1,0:T(8,128)(2,1)} collective-permute-done((bf16[2,256,512]{2,1,0:T(8,128)(2,1)}, bf16[2,256,512]{2,1,0:T(8,128)(2,1)}, u32[]{:S(2)}, u32[]{:S(2)}) %collective-permute-start.22) | collective-permute-done | bytes 524320 | tf_op jit(solution)/shard_map/ppermute | solution.py:69
  192.3 9.2 %collective-permute-done.23 = bf16[2,256,512]{2,1,0:T(8,128)(2,1)} collective-permute-done((bf16[2,256,512]{2,1,0:T(8,128)(2,1)}, bf16[2,256,512]{2,1,0:T(8,128)(2,1)}, u32[]{:S(2)}, u32[]{:S(2)}) %collective-permute-start.23) | collective-permute-done | bytes 524320 | tf_op jit(solution)/shard_map/ppermute | solution.py:69
  204.1 2.0 convert_add_fusion
  206.3 3.6 %collective-permute-done.27 = bf16[2,64,512]{2,1,0:T(8,128)(2,1)S(1)} collective-permute-done((bf16[2,64,512]{2,1,0:T(8,128)(2,1)S(1)}, bf16[2,64,512]{2,1,0:T(8,128)(2,1)S(1)}, u32[]{:S(2)}, u32[]{:S(2)}) %collective-permute-start.27) | collective-permute-done | bytes 131104 | tf_op jit(solution)/shard_map/ppermute | solution.py:48
  (87 shorter events, 34.3 us)
Async XLA Ops:
  7.2 67.2 %all-gather.2.cloned.1.call-start = ((), (), s32[]{:S(2)}) async-start(), calls=%async_computation.1 | async-start | bytes 1310720 | tf_op jit(solution)/shard_map/all_gather | solution.py:234
  7.9 203.0 %reduce-scatter.2.cloned.1.call-start = ((), (), s32[]{:S(2)}) async-start(), calls=%async_computation.2 | async-start | bytes 1310720 | tf_op jit(solution)/shard_map/reduce_scatter | solution.py:245
  9.6 14.2 %collective-permute-start.4 = (bf16[2,64,512]{2,1,0:T(8,128)(2,1)S(1)}, bf16[2,64,512]{2,1,0:T(8,128)(2,1)S(1)}, u32[]{:S(2)}, u32[]{:S(2)}) collective-permute-start(bf16[2,64,512]{2,1,0:T(8,128)(2,1)S(1)} %get-tuple-element.36), channel_id=1, source_target_pairs={{0,64},{1,65},{2,66},{3,67}} | collective-permute-start | bytes 393224 | tf_op jit(solution)/shard_map/ppermute | solution.py:29
  23.5 56.9 %collective-permute-start.13 = (bf16[2,256,512]{2,1,0:T(8,128)(2,1)S(1)}, bf16[2,256,512]{2,1,0:T(8,128)(2,1)S(1)}, u32[]{:S(2)}, u32[]{:S(2)}) collective-permute-start(bf16[2,256,512]{2,1,0:T(8,128)(2,1)S(1)} %pad_maximum_fusion.own_ref), channel_id=1, source_target_pairs={{160,0},{164,4},{168,8},{172,12},{176,16},{180,20},{184,24},{188,2... | collective-permute-start | bytes 1572872 | tf_op jit(solution)/shard_map/ppermute | solution.py:69
  23.6 56.8 %collective-permute-start.12 = (bf16[2,256,512]{2,1,0:T(8,128)(2,1)S(1)}, bf16[2,256,512]{2,1,0:T(8,128)(2,1)}, u32[]{:S(2)}, u32[]{:S(2)}) collective-permute-start(bf16[2,256,512]{2,1,0:T(8,128)(2,1)S(1)} %pad_maximum_fusion.own_ref), channel_id=1, source_target_pairs={{192,0},{196,4},{200,8},{204,12},{208,16},{212,20},{216,24},{220,2... | collective-permute-start | bytes 1572872 | tf_op jit(solution)/shard_map/ppermute | solution.py:69
  25.5 26.0 %collective-permute-start.7 = (bf16[2,64,512]{2,1,0:T(8,128)(2,1)S(1)}, bf16[2,64,512]{2,1,0:T(8,128)(2,1)S(1)}, u32[]{:S(2)}, u32[]{:S(2)}) collective-permute-start(bf16[2,64,512]{2,1,0:T(8,128)(2,1)S(1)} %select_select_fusion.2), channel_id=1, source_target_pairs={{0,16},{64,80},{128,144},{192,208},{1,17},{65,81},{129,145},{193,2... | collective-permute-start | bytes 393224 | tf_op jit(solution)/shard_map/ppermute | solution.py:29
  26.8 27.5 %collective-permute-start.6 = (bf16[2,64,512]{2,1,0:T(8,128)(2,1)S(1)}, bf16[2,64,512]{2,1,0:T(8,128)(2,1)}, u32[]{:S(2)}, u32[]{:S(2)}) collective-permute-start(bf16[2,64,512]{2,1,0:T(8,128)(2,1)S(1)} %select_select_fusion.2), channel_id=1, source_target_pairs={{0,32},{64,96},{128,160},{192,224},{1,33},{65,97},{129,161},{193,2... | collective-permute-start | bytes 393224 | tf_op jit(solution)/shard_map/ppermute | solution.py:29
  29.2 27.0 %collective-permute-start.5 = (bf16[2,64,512]{2,1,0:T(8,128)(2,1)S(1)}, bf16[2,64,512]{2,1,0:T(8,128)(2,1)}, u32[]{:S(2)}, u32[]{:S(2)}) collective-permute-start(bf16[2,64,512]{2,1,0:T(8,128)(2,1)S(1)} %select_select_fusion.2), channel_id=1, source_target_pairs={{0,48},{64,112},{128,176},{192,240},{1,49},{65,113},{129,177},{193... | collective-permute-start | bytes 393224 | tf_op jit(solution)/shard_map/ppermute | solution.py:29
  63.1 17.3 %collective-permute-start.11 = (bf16[2,256,512]{2,1,0:T(8,128)(2,1)S(1)}, bf16[2,256,512]{2,1,0:T(8,128)(2,1)}, u32[]{:S(2)}, u32[]{:S(2)}) collective-permute-start(bf16[2,256,512]{2,1,0:T(8,128)(2,1)S(1)} %pad_maximum_fusion.own_ref), channel_id=1, source_target_pairs={{128,0},{132,4},{136,8},{140,12},{144,16},{148,20},{152,24},{156,2... | collective-permute-start | bytes 1572872 | tf_op jit(solution)/shard_map/ppermute | solution.py:69
  63.6 17.1 %collective-permute-start.14 = (bf16[2,256,512]{2,1,0:T(8,128)(2,1)S(1)}, bf16[2,256,512]{2,1,0:T(8,128)(2,1)}, u32[]{:S(2)}, u32[]{:S(2)}) collective-permute-start(bf16[2,256,512]{2,1,0:T(8,128)(2,1)S(1)} %pad_maximum_fusion.own_ref), channel_id=1, source_target_pairs={{96,0},{100,4},{104,8},{108,12},{112,16},{116,20},{120,24},{124,28... | collective-permute-start | bytes 1572872 | tf_op jit(solution)/shard_map/ppermute | solution.py:69
  97.1 23.0 %collective-permute-start.18 = (bf16[2,64,512]{2,1,0:T(8,128)(2,1)S(1)}, bf16[2,64,512]{2,1,0:T(8,128)(2,1)S(1)}, u32[]{:S(2)}, u32[]{:S(2)}) collective-permute-start(bf16[2,64,512]{2,1,0:T(8,128)(2,1)S(1)} %convert_element_type.64), channel_id=1, source_target_pairs={{192,0},{196,4},{200,8},{204,12},{208,16},{212,20},{216,24},{220,2... | collective-permute-start | bytes 393224 | tf_op jit(solution)/shard_map/ppermute | solution.py:48
  98.4 21.7 %collective-permute-start.17 = (bf16[2,64,512]{2,1,0:T(8,128)(2,1)S(1)}, bf16[2,64,512]{2,1,0:T(8,128)(2,1)S(1)}, u32[]{:S(2)}, u32[]{:S(2)}) collective-permute-start(bf16[2,64,512]{2,1,0:T(8,128)(2,1)S(1)} %convert_element_type.64), channel_id=1, source_target_pairs={{128,0},{132,4},{136,8},{140,12},{144,16},{148,20},{152,24},{156,2... | collective-permute-start | bytes 393224 | tf_op jit(solution)/shard_map/ppermute | solution.py:48
  99.7 21.1 %collective-permute-start.16 = (bf16[2,64,512]{2,1,0:T(8,128)(2,1)S(1)}, bf16[2,64,512]{2,1,0:T(8,128)(2,1)S(1)}, u32[]{:S(2)}, u32[]{:S(2)}) collective-permute-start(bf16[2,64,512]{2,1,0:T(8,128)(2,1)S(1)} %convert_element_type.64), channel_id=1, source_target_pairs={{64,0},{68,4},{72,8},{76,12},{80,16},{84,20},{88,24},{92,28},{96,3... | collective-permute-start | bytes 393224 | tf_op jit(solution)/shard_map/ppermute | solution.py:48
  120.8 8.9 %collective-permute-start.21 = (bf16[2,64,512]{2,1,0:T(8,128)(2,1)S(1)}, bf16[2,64,512]{2,1,0:T(8,128)(2,1)S(1)}, u32[]{:S(2)}, u32[]{:S(2)}) collective-permute-start(bf16[2,64,512]{2,1,0:T(8,128)(2,1)S(1)} %fusion.4), channel_id=1, source_target_pairs={{48,0},{52,4},{56,8},{60,12},{49,1},{53,5},{57,9},{61,13},{50,2},{... | collective-permute-start | bytes 393224 | tf_op jit(solution)/shard_map/ppermute | solution.py:48
  122.1 43.3 %collective-permute-start.20 = (bf16[2,64,512]{2,1,0:T(8,128)(2,1)S(1)}, bf16[2,64,512]{2,1,0:T(8,128)(2,1)S(1)}, u32[]{:S(2)}, u32[]{:S(2)}) collective-permute-start(bf16[2,64,512]{2,1,0:T(8,128)(2,1)S(1)} %fusion.4), channel_id=1, source_target_pairs={{32,0},{36,4},{40,8},{44,12},{33,1},{37,5},{41,9},{45,13},{34,2},{... | collective-permute-start | bytes 393224 | tf_op jit(solution)/shard_map/ppermute | solution.py:48
  123.4 42.0 %collective-permute-start.19 = (bf16[2,64,512]{2,1,0:T(8,128)(2,1)S(1)}, bf16[2,64,512]{2,1,0:T(8,128)(2,1)S(1)}, u32[]{:S(2)}, u32[]{:S(2)}) collective-permute-start(bf16[2,64,512]{2,1,0:T(8,128)(2,1)S(1)} %fusion.4), channel_id=1, source_target_pairs={{16,0},{20,4},{24,8},{28,12},{17,1},{21,5},{25,9},{29,13},{18,2},{... | collective-permute-start | bytes 393224 | tf_op jit(solution)/shard_map/ppermute | solution.py:48
  124.7 47.8 %collective-permute-start.15 = (bf16[2,256,512]{2,1,0:T(8,128)(2,1)}, bf16[2,256,512]{2,1,0:T(8,128)(2,1)S(1)}, u32[]{:S(2)}, u32[]{:S(2)}) collective-permute-start(bf16[2,256,512]{2,1,0:T(8,128)(2,1)} %get-tuple-element.21), channel_id=1, source_target_pairs={{128,0},{132,4},{136,8},{140,12},{144,16},{148,20},{152,24},{156,2... | collective-permute-start | bytes 1572872 | tf_op jit(solution)/shard_map/ppermute | solution.py:69
  165.6 25.5 %collective-permute-start.22 = (bf16[2,256,512]{2,1,0:T(8,128)(2,1)}, bf16[2,256,512]{2,1,0:T(8,128)(2,1)}, u32[]{:S(2)}, u32[]{:S(2)}) collective-permute-start(bf16[2,256,512]{2,1,0:T(8,128)(2,1)} %get-tuple-element.26), channel_id=1, source_target_pairs={{64,0},{68,4},{72,8},{76,12},{80,16},{84,20},{88,24},{92,28},{96,3... | collective-permute-start | bytes 1572872 | tf_op jit(solution)/shard_map/ppermute | solution.py:69
  165.7 35.9 %collective-permute-start.23 = (bf16[2,256,512]{2,1,0:T(8,128)(2,1)}, bf16[2,256,512]{2,1,0:T(8,128)(2,1)}, u32[]{:S(2)}, u32[]{:S(2)}) collective-permute-start(bf16[2,256,512]{2,1,0:T(8,128)(2,1)} %get-tuple-element.27), channel_id=1, source_target_pairs={{96,0},{100,4},{104,8},{108,12},{112,16},{116,20},{120,24},{124,28... | collective-permute-start | bytes 1572872 | tf_op jit(solution)/shard_map/ppermute | solution.py:69
  165.7 37.1 %collective-permute-start.24 = (bf16[2,256,512]{2,1,0:T(8,128)(2,1)}, bf16[2,256,512]{2,1,0:T(8,128)(2,1)}, u32[]{:S(2)}, u32[]{:S(2)}) collective-permute-start(bf16[2,256,512]{2,1,0:T(8,128)(2,1)} %get-tuple-element.28), channel_id=1, source_target_pairs={{160,0},{164,4},{168,8},{172,12},{176,16},{180,20},{184,24},{188,2... | collective-permute-start | bytes 1572872 | tf_op jit(solution)/shard_map/ppermute | solution.py:69
  169.9 36.4 %collective-permute-start.25 = (bf16[2,64,512]{2,1,0:T(8,128)(2,1)}, bf16[2,64,512]{2,1,0:T(8,128)(2,1)S(1)}, u32[]{:S(2)}, u32[]{:S(2)}) collective-permute-start(bf16[2,64,512]{2,1,0:T(8,128)(2,1)} %get-tuple-element.29), channel_id=1, source_target_pairs={{0,4},{4,8},{8,12},{12,16},{16,20},{20,24},{24,28},{28,32},{32,36}... | collective-permute-start | bytes 393224 | tf_op jit(solution)/shard_map/ppermute | solution.py:75
  172.5 33.7 %collective-permute-start.29 = (bf16[2,64,512]{2,1,0:T(8,128)(2,1)}, bf16[2,64,512]{2,1,0:T(8,128)(2,1)S(1)}, u32[]{:S(2)}, u32[]{:S(2)}) collective-permute-start(bf16[2,64,512]{2,1,0:T(8,128)(2,1)} %get-tuple-element.31), channel_id=1, source_target_pairs={{4,0},{8,4},{12,8},{16,12},{20,16},{24,20},{28,24},{32,28},{36,32}... | collective-permute-start | bytes 393224 | tf_op jit(solution)/shard_map/ppermute | solution.py:75
  191.0 15.2 %collective-permute-start.28 = (bf16[2,64,512]{2,1,0:T(8,128)(2,1)S(1)}, bf16[2,64,512]{2,1,0:T(8,128)(2,1)S(1)}, u32[]{:S(2)}, u32[]{:S(2)}) collective-permute-start(bf16[2,64,512]{2,1,0:T(8,128)(2,1)S(1)} %convert_element_type.76), channel_id=1, source_target_pairs={{12,0},{13,1},{14,2},{15,3}} | collective-permute-start | bytes 393224 | tf_op jit(solution)/shard_map/ppermute | solution.py:48
  201.5 8.4 %collective-permute-start.27 = (bf16[2,64,512]{2,1,0:T(8,128)(2,1)S(1)}, bf16[2,64,512]{2,1,0:T(8,128)(2,1)S(1)}, u32[]{:S(2)}, u32[]{:S(2)}) collective-permute-start(bf16[2,64,512]{2,1,0:T(8,128)(2,1)S(1)} %convert_element_type.76), channel_id=1, source_target_pairs={{8,0},{9,1},{10,2},{11,3}} | collective-permute-start | bytes 393224 | tf_op jit(solution)/shard_map/ppermute | solution.py:48
  (17 other events, 227.8 us)
Sparse Core Ops, SparseCore 0:
  9.8 38.6 all-gather.1
  103.8 40.7 reduce-scatter.1

commit v4 on v2

--- a/solution.py
+++ b/solution.py
@@ -39,9 +39,9 @@
     return value
 
 
-def sum_up(value, axis):
+def sum_up(value, axis, stages):
     count = lax.axis_size(axis)
-    for stride, ways in tree_strides(count):
+    for stride, ways in stages:
         sent = value.astype(jnp.bfloat16)
         for turn in range(1, ways):
             route = [(i + turn * stride, i) for i in range(0, count, stride * ways)]
@@ -215,7 +215,9 @@
     low = shifted(key_value[:, -BS:], "ctx", 1)
     high = shifted(key_value[:, :BS], "ctx", -1)
     anchor = spread_down(key_value[:, :BS], "ctx")
-    arrivals = [from_behind(key_value, "ctx", offset) for offset in offsets]
+    arrivals = [from_behind(key_value, "ctx", offsets[0])]
+    anchor, held = lax.optimization_barrier((anchor, key_value))
+    arrivals += [from_behind(held, "ctx", offset) for offset in offsets[1:]]
     grad_attention = lax.dot_general(
         lax.all_gather(upstream, "head", axis=1, tiled=True),
         out_weight,
@@ -231,12 +233,15 @@
     mixed = lax.psum_scatter(
         partial_out.astype(jnp.bfloat16), "head", scatter_dimension=1, tiled=True
     )
-    anchor_grad = sum_up(anchor_grad, "ctx")
+    returned = [from_behind(sent, "ctx", -offset) for sent, offset in zip(spread, offsets)]
+    anchor_grad = sum_up(anchor_grad, "ctx", [(1, 2), (2, 2)])
+    anchor_grad, returned = lax.optimization_barrier((anchor_grad, returned))
+    anchor_grad = sum_up(anchor_grad, "ctx", tree_strides(axis_count)[1:])
     from_high = shifted(low_grad, "ctx", -1).astype(jnp.float32)
     from_low = shifted(high_grad, "ctx", 1).astype(jnp.float32)
     first = from_low + jnp.where(position == 0, anchor_grad, 0.0)
-    for sent, offset in zip(spread, offsets):
-        own_grad = own_grad + from_behind(sent, "ctx", -offset).astype(jnp.float32)
+    for arrived in returned:
+        own_grad = own_grad + arrived.astype(jnp.float32)
     own_grad = jnp.concatenate(
         [
             own_grad[:, :BS] + first,

time: 220 us -> 211 us (0.959)
  waiting for transfers between devices: 98.9 us -> 93.9 us
  other arithmetic: 9.92 us -> 6.75 us
    ppermute x8, waiting for transfers between devices: 0.24 us -> 62.7 us  [from_behind(): return lax.ppermute(block, axis, route)]
    ppermute x9 -> x8, waiting for transfers between devices: 68.9 us -> 21.9 us  [sum_up(): value = value + lax.ppermute(sent, axis, route).astype(jnp.float32)]
    ppermute x9, waiting for transfers between devices: 24.2 us -> 5.71 us  [spread_down(): lax.ppermute(value, axis, [(i, i + turn * stride) for i in range(0, count...]
    ppermute x8, starting transfers between devices: 27.3 us -> 30.3 us  [from_behind(): return lax.ppermute(block, axis, route)]
    convert_element_type x3 -> x4, other arithmetic: 2.99 us -> 0.13 us  [sum_up(): sent = value.astype(jnp.bfloat16)]
    ppermute x9 -> x8, starting transfers between devices: 11.7 us -> 10.3 us  [sum_up(): value = value + lax.ppermute(sent, axis, route).astype(jnp.float32)]
  transfers between devices with their start and end apart: 32 -> 31, of which waited for: 14 -> 16; matrix products, arithmetic and copies ran while one was open for 7% -> 6% of each run, Pallas kernels for 0% -> 0%
where the time goes in v4:
time: 211 us; the launch traced here: 210 us
  waiting for transfers between devices  93.9 us (45%)
  starting transfers between devices  70.8 us (34%)
  Pallas kernels  14.9 us (7%)
  between operations  14.5 us (7%)
  other arithmetic  6.75 us (3%)
  matrix products  5.39 us (3%)
  local copies, waits for them, and re-layouts  3.56 us (2%)
    ppermute x8, waiting for transfers between devices, from_behind(): return lax.ppermute(block, axis, route)  62.7 us
    ppermute x8, starting transfers between devices, from_behind(): return lax.ppermute(block, axis, route)  30.3 us
    ppermute x9, starting transfers between devices, spread_down(): lax.ppermute(value, axis, [(i, i + turn * stride) for i in range(0, count...  23.2 us
    ppermute x8, waiting for transfers between devices, sum_up(): value = value + lax.ppermute(sent, axis, route).astype(jnp.float32)  21.9 us
    pallas_call x1, Pallas kernels, attention_both_ways(): pl.pallas_call(functools.partial(attend, run_blocks, 1.0 / math.sqrt(HDIM...  14.9 us
    ppermute x8, starting transfers between devices, sum_up(): value = value + lax.ppermute(sent, axis, route).astype(jnp.float32)  10.3 us
    ppermute x4, starting transfers between devices, shifted(): return lax.ppermute(block, axis, route)  6.96 us
    ppermute x9, waiting for transfers between devices, spread_down(): lax.ppermute(value, axis, [(i, i + turn * stride) for i in range(0, count...  5.71 us
  transfers between devices with their start and end apart: 31, of which 16 were waited for; matrix products, arithmetic and copies ran while one was open for 6% of the time, Pallas kernels for 0%

profile of v4, /device:TPU:8, one launch (start us, length us, event | category | flops | bytes accessed | tf_op | source)
XLA Modules:
  0.0 209.8 jit_solution(16937065917009191157)
XLA Ops:
  8.9 9.1 %collective-permute-start.4 = (bf16[2,64,512]{2,1,0:T(8,128)(2,1)S(1)}, bf16[2,64,512]{2,1,0:T(8,128)(2,1)S(1)}, u32[]{:S(2)}, u32[]{:S(2)}) collective-permute-start(bf16[2,64,512]{2,1,0:T(8,128)(2,1)S(1)} %get-tuple-element.42), channel_id=1, source_target_pairs={{0,64},{1,65},{2,66},{3,67}} | collective-permute-start | bytes 393224 | tf_op jit(solution)/shard_map/ppermute | solution.py:29
  20.0 2.4 %collective-permute-start.2 = (bf16[2,64,512]{2,1,0:T(8,128)(2,1)S(1)}, bf16[2,64,512]{2,1,0:T(8,128)(2,1)}, u32[]{:S(2)}, u32[]{:S(2)}) collective-permute-start(bf16[2,64,512]{2,1,0:T(8,128)(2,1)S(1)} %get-tuple-element.42), channel_id=1, source_target_pairs={{0,192},{1,193},{2,194},{3,195}} | collective-permute-start | bytes 393224 | tf_op jit(solution)/shard_map/ppermute | solution.py:29
  30.9 2.8 %collective-permute-done.6 = bf16[2,64,512]{2,1,0:T(8,128)(2,1)S(1)} collective-permute-done((bf16[2,64,512]{2,1,0:T(8,128)(2,1)S(1)}, bf16[2,64,512]{2,1,0:T(8,128)(2,1)S(1)}, u32[]{:S(2)}, u32[]{:S(2)}) %collective-permute-start.6) | collective-permute-done | bytes 131104 | tf_op jit(solution)/shard_map/ppermute | solution.py:29
  45.3 5.5 %collective-permute-start.14 = (bf16[2,256,512]{2,1,0:T(8,128)(2,1)S(1)}, bf16[2,256,512]{2,1,0:T(8,128)(2,1)}, u32[]{:S(2)}, u32[]{:S(2)}) collective-permute-start(bf16[2,256,512]{2,1,0:T(8,128)(2,1)S(1)} %pad_maximum_fusion.own_ref), channel_id=1, source_target_pairs={{96,0},{100,4},{104,8},{108,12},{112,16},{116,20},{120,24},{124,28... | collective-permute-start | bytes 1572872 | tf_op jit(solution)/shard_map/ppermute | solution.py:55
  50.8 4.6 %collective-permute-start.12 = (bf16[2,256,512]{2,1,0:T(8,128)(2,1)S(1)}, bf16[2,256,512]{2,1,0:T(8,128)(2,1)}, u32[]{:S(2)}, u32[]{:S(2)}) collective-permute-start(bf16[2,256,512]{2,1,0:T(8,128)(2,1)S(1)} %pad_maximum_fusion.own_ref), channel_id=1, source_target_pairs={{192,0},{196,4},{200,8},{204,12},{208,16},{212,20},{216,24},{220,2... | collective-permute-start | bytes 1572872 | tf_op jit(solution)/shard_map/ppermute | solution.py:55
  57.4 2.7 %convolution_convert_fusion.1.g_ref = bf16[256,512]{1,0:T(8,128)(2,1)} fusion(bf16[256,2048]{1,0:T(8,128)(2,1)} %all-gather.2.cloned.1.call-done, bf16[512,2048]{1,0:T(8,128)(2,1)S(1)} %copy-done), kind=kOutput, calls=%fused_computation.1 | convolution fusion | flops 537001984 | bytes 3407872 | tf_op jit(solution)/shard_map/dot_general | solution.py:221
  60.1 2.8 %collective-permute-done.1.high_ref = bf16[2,64,512]{2,1,0:T(8,128)(2,1)S(1)} collective-permute-done((bf16[2,64,512]{2,1,0:T(8,128)(2,1)S(1)}, bf16[2,64,512]{2,1,0:T(8,128)(2,1)S(1)}, u32[]{:S(2)}, u32[]{:S(2)}) %collective-permute-start.1) | collective-permute-done | bytes 131104 | tf_op jit(solution)/shard_map/ppermute | solution.py:61
  63.0 22.4 %collective-permute-done.14.r3_ref = bf16[2,256,512]{2,1,0:T(8,128)(2,1)} collective-permute-done((bf16[2,256,512]{2,1,0:T(8,128)(2,1)S(1)}, bf16[2,256,512]{2,1,0:T(8,128)(2,1)}, u32[]{:S(2)}, u32[]{:S(2)}) %collective-permute-start.14) | collective-permute-done | bytes 524320 | tf_op jit(solution)/shard_map/ppermute | solution.py:55
  85.4 4.4 %collective-permute-done.13.r2_ref = bf16[2,256,512]{2,1,0:T(8,128)(2,1)} collective-permute-done((bf16[2,256,512]{2,1,0:T(8,128)(2,1)S(1)}, bf16[2,256,512]{2,1,0:T(8,128)(2,1)}, u32[]{:S(2)}, u32[]{:S(2)}) %collective-permute-start.13) | collective-permute-done | bytes 524320 | tf_op jit(solution)/shard_map/ppermute | solution.py:55
  89.8 3.2 %collective-permute-done.12.r1_ref = bf16[2,256,512]{2,1,0:T(8,128)(2,1)} collective-permute-done((bf16[2,256,512]{2,1,0:T(8,128)(2,1)S(1)}, bf16[2,256,512]{2,1,0:T(8,128)(2,1)}, u32[]{:S(2)}, u32[]{:S(2)}) %collective-permute-start.12) | collective-permute-done | bytes 524320 | tf_op jit(solution)/shard_map/ppermute | solution.py:55
  93.0 14.9 %attention_both_ways.1 = (bf16[256,512]{1,0:T(8,128)(2,1)}, bf16[256,512]{1,0:T(8,128)(2,1)}, f32[2,256,512]{2,1,0:T(8,128)}, bf16[2,64,512]{2,1,0:T(8,128)(2,1)...) custom-call(s32[12]{0:T(128)} %reshape.32.picks, ...), custom_call_target="tpu_custom_call" | custom-call | flops 587202560 | bytes 8388608 | tf_op jit(solution)/shard_map/attention_both_ways/pallas_call | solution.py:166
  107.9 2.7 %convolution_convert_fusion = bf16[256,2048]{1,0:T(8,128)(2,1)} fusion(bf16[256,512]{1,0:T(8,128)(2,1)} %get-tuple-element.23, bf16[512,2048]{1,0:T(8,128)(2,1)S(1)} %copy-done), kind=kOutput, calls=%fused_computation | convolution fusion | flops 537395200 | bytes 3407872 | tf_op jit(solution)/shard_map/dot_general | solution.py:232
  112.0 8.0 %collective-permute-start.17 = (bf16[2,256,512]{2,1,0:T(8,128)(2,1)}, bf16[2,256,512]{2,1,0:T(8,128)(2,1)S(1)}, u32[]{:S(2)}, u32[]{:S(2)}) collective-permute-start(bf16[2,256,512]{2,1,0:T(8,128)(2,1)} %get-tuple-element.27), channel_id=1, source_target_pairs={{128,0},{132,4},{136,8},{140,12},{144,16},{148,20},{152,24},{156,2... | collective-permute-start | bytes 1572872 | tf_op jit(solution)/shard_map/ppermute | solution.py:55
  120.0 8.0 %collective-permute-start.18 = (bf16[2,256,512]{2,1,0:T(8,128)(2,1)}, bf16[2,256,512]{2,1,0:T(8,128)(2,1)S(1)}, u32[]{:S(2)}, u32[]{:S(2)}) collective-permute-start(bf16[2,256,512]{2,1,0:T(8,128)(2,1)} %get-tuple-element.28), channel_id=1, source_target_pairs={{64,0},{68,4},{72,8},{76,12},{80,16},{84,20},{88,24},{92,28},{96,3... | collective-permute-start | bytes 1572872 | tf_op jit(solution)/shard_map/ppermute | solution.py:55
  129.7 2.4 %collective-permute-start.20 = (bf16[2,256,512]{2,1,0:T(8,128)(2,1)}, bf16[2,256,512]{2,1,0:T(8,128)(2,1)S(1)}, u32[]{:S(2)}, u32[]{:S(2)}) collective-permute-start(bf16[2,256,512]{2,1,0:T(8,128)(2,1)} %get-tuple-element.30), channel_id=1, source_target_pairs={{160,0},{164,4},{168,8},{172,12},{176,16},{180,20},{184,24},{188,2... | collective-permute-start | bytes 1572872 | tf_op jit(solution)/shard_map/ppermute | solution.py:55
  133.5 7.1 %collective-permute-done.16 = bf16[2,64,512]{2,1,0:T(8,128)(2,1)S(1)} collective-permute-done((bf16[2,64,512]{2,1,0:T(8,128)(2,1)S(1)}, bf16[2,64,512]{2,1,0:T(8,128)(2,1)S(1)}, u32[]{:S(2)}, u32[]{:S(2)}) %collective-permute-start.16) | collective-permute-done | bytes 131104 | tf_op jit(solution)/shard_map/ppermute | solution.py:48
  140.6 8.9 %collective-permute-done.18 = bf16[2,256,512]{2,1,0:T(8,128)(2,1)S(1)} collective-permute-done((bf16[2,256,512]{2,1,0:T(8,128)(2,1)}, bf16[2,256,512]{2,1,0:T(8,128)(2,1)S(1)}, u32[]{:S(2)}, u32[]{:S(2)}) %collective-permute-start.18) | collective-permute-done | bytes 524320 | tf_op jit(solution)/shard_map/ppermute | solution.py:55
  149.5 6.1 %collective-permute-done.19 = bf16[2,256,512]{2,1,0:T(8,128)(2,1)S(1)} collective-permute-done((bf16[2,256,512]{2,1,0:T(8,128)(2,1)}, bf16[2,256,512]{2,1,0:T(8,128)(2,1)S(1)}, u32[]{:S(2)}, u32[]{:S(2)}) %collective-permute-start.19) | collective-permute-done | bytes 524320 | tf_op jit(solution)/shard_map/ppermute | solution.py:55
  155.7 17.6 %collective-permute-done.20 = bf16[2,256,512]{2,1,0:T(8,128)(2,1)S(1)} collective-permute-done((bf16[2,256,512]{2,1,0:T(8,128)(2,1)}, bf16[2,256,512]{2,1,0:T(8,128)(2,1)S(1)}, u32[]{:S(2)}, u32[]{:S(2)}) %collective-permute-start.20) | collective-permute-done | bytes 524320 | tf_op jit(solution)/shard_map/ppermute | solution.py:55
  177.2 2.5 %collective-permute-start.21 = (bf16[2,64,512]{2,1,0:T(8,128)(2,1)}, bf16[2,64,512]{2,1,0:T(8,128)(2,1)S(1)}, u32[]{:S(2)}, u32[]{:S(2)}) collective-permute-start(bf16[2,64,512]{2,1,0:T(8,128)(2,1)} %get-tuple-element.35), channel_id=1, source_target_pairs={{0,4},{4,8},{8,12},{12,16},{16,20},{20,24},{24,28},{28,32},{32,36}... | collective-permute-start | bytes 393224 | tf_op jit(solution)/shard_map/ppermute | solution.py:61
  182.6 2.7 %collective-permute-done.23 = bf16[2,64,512]{2,1,0:T(8,128)(2,1)S(1)} collective-permute-done((bf16[2,64,512]{2,1,0:T(8,128)(2,1)S(1)}, bf16[2,64,512]{2,1,0:T(8,128)(2,1)S(1)}, u32[]{:S(2)}, u32[]{:S(2)}) %collective-permute-start.23) | collective-permute-done | bytes 131104 | tf_op jit(solution)/shard_map/ppermute | solution.py:48
  185.3 2.8 %collective-permute-done.22 = bf16[2,64,512]{2,1,0:T(8,128)(2,1)S(1)} collective-permute-done((bf16[2,64,512]{2,1,0:T(8,128)(2,1)S(1)}, bf16[2,64,512]{2,1,0:T(8,128)(2,1)S(1)}, u32[]{:S(2)}, u32[]{:S(2)}) %collective-permute-start.22) | collective-permute-done | bytes 131104 | tf_op jit(solution)/shard_map/ppermute | solution.py:48
  192.0 2.0 convert_add_fusion
  194.2 7.5 %collective-permute-done.27 = bf16[2,64,512]{2,1,0:T(8,128)(2,1)S(1)} collective-permute-done((bf16[2,64,512]{2,1,0:T(8,128)(2,1)S(1)}, bf16[2,64,512]{2,1,0:T(8,128)(2,1)S(1)}, u32[]{:S(2)}, u32[]{:S(2)}) %collective-permute-start.27) | collective-permute-done | bytes 131104 | tf_op jit(solution)/shard_map/ppermute | solution.py:48
  (90 shorter events, 42.1 us)
Async XLA Ops:
  7.2 50.2 %all-gather.2.cloned.1.call-start = ((), (), s32[]{:S(2)}) async-start(), calls=%async_computation.1 | async-start | bytes 1310720 | tf_op jit(solution)/shard_map/all_gather | solution.py:222
  7.9 195.0 %reduce-scatter.2.cloned.1.call-start = ((), (), s32[]{:S(2)}) async-start(), calls=%async_computation.2 | async-start | bytes 1310720 | tf_op jit(solution)/shard_map/reduce_scatter | solution.py:233
  8.9 16.7 %collective-permute-start.4 = (bf16[2,64,512]{2,1,0:T(8,128)(2,1)S(1)}, bf16[2,64,512]{2,1,0:T(8,128)(2,1)S(1)}, u32[]{:S(2)}, u32[]{:S(2)}) collective-permute-start(bf16[2,64,512]{2,1,0:T(8,128)(2,1)S(1)} %get-tuple-element.42), channel_id=1, source_target_pairs={{0,64},{1,65},{2,66},{3,67}} | collective-permute-start | bytes 393224 | tf_op jit(solution)/shard_map/ppermute | solution.py:29
  18.1 7.6 %collective-permute-start.3 = (bf16[2,64,512]{2,1,0:T(8,128)(2,1)S(1)}, bf16[2,64,512]{2,1,0:T(8,128)(2,1)}, u32[]{:S(2)}, u32[]{:S(2)}) collective-permute-start(bf16[2,64,512]{2,1,0:T(8,128)(2,1)S(1)} %get-tuple-element.42), channel_id=1, source_target_pairs={{0,128},{1,129},{2,130},{3,131}} | collective-permute-start | bytes 393224 | tf_op jit(solution)/shard_map/ppermute | solution.py:29
  22.4 33.7 %collective-permute-start = (bf16[2,64,512]{2,1,0:T(8,128)(2,1)S(1)}, bf16[2,64,512]{2,1,0:T(8,128)(2,1)}, u32[]{:S(2)}, u32[]{:S(2)}) collective-permute-start(bf16[2,64,512]{2,1,0:T(8,128)(2,1)S(1)} %get-tuple-element.43), channel_id=1, source_target_pairs={{0,4},{4,8},{8,12},{12,16},{16,20},{20,24},{24,28},{28,32},{32,36}... | collective-permute-start | bytes 393224 | tf_op jit(solution)/shard_map/ppermute | solution.py:61
  25.5 37.5 %collective-permute-start.11 = (bf16[2,256,512]{2,1,0:T(8,128)(2,1)S(1)}, bf16[2,256,512]{2,1,0:T(8,128)(2,1)S(1)}, u32[]{:S(2)}, u32[]{:S(2)}) collective-permute-start(bf16[2,256,512]{2,1,0:T(8,128)(2,1)S(1)} %pad_maximum_fusion.own_ref), channel_id=1, source_target_pairs={{128,0},{132,4},{136,8},{140,12},{144,16},{148,20},{152,24},{156,2... | collective-permute-start | bytes 1572872 | tf_op jit(solution)/shard_map/ppermute | solution.py:55
  35.4 8.3 %collective-permute-start.10 = (bf16[2,64,512]{2,1,0:T(8,128)(2,1)S(1)}, bf16[2,64,512]{2,1,0:T(8,128)(2,1)}, u32[]{:S(2)}, u32[]{:S(2)}) collective-permute-start(bf16[2,64,512]{2,1,0:T(8,128)(2,1)S(1)} %select_select_fusion.1), channel_id=1, source_target_pairs={{0,4},{16,20},{32,36},{48,52},{64,68},{80,84},{96,100},{112,116},{... | collective-permute-start | bytes 393224 | tf_op jit(solution)/shard_map/ppermute | solution.py:29
  45.3 40.0 %collective-permute-start.14 = (bf16[2,256,512]{2,1,0:T(8,128)(2,1)S(1)}, bf16[2,256,512]{2,1,0:T(8,128)(2,1)}, u32[]{:S(2)}, u32[]{:S(2)}) collective-permute-start(bf16[2,256,512]{2,1,0:T(8,128)(2,1)S(1)} %pad_maximum_fusion.own_ref), channel_id=1, source_target_pairs={{96,0},{100,4},{104,8},{108,12},{112,16},{116,20},{120,24},{124,28... | collective-permute-start | bytes 1572872 | tf_op jit(solution)/shard_map/ppermute | solution.py:55
  50.8 39.0 %collective-permute-start.13 = (bf16[2,256,512]{2,1,0:T(8,128)(2,1)S(1)}, bf16[2,256,512]{2,1,0:T(8,128)(2,1)}, u32[]{:S(2)}, u32[]{:S(2)}) collective-permute-start(bf16[2,256,512]{2,1,0:T(8,128)(2,1)S(1)} %pad_maximum_fusion.own_ref), channel_id=1, source_target_pairs={{160,0},{164,4},{168,8},{172,12},{176,16},{180,20},{184,24},{188,2... | collective-permute-start | bytes 1572872 | tf_op jit(solution)/shard_map/ppermute | solution.py:55
  50.8 42.2 %collective-permute-start.12 = (bf16[2,256,512]{2,1,0:T(8,128)(2,1)S(1)}, bf16[2,256,512]{2,1,0:T(8,128)(2,1)}, u32[]{:S(2)}, u32[]{:S(2)}) collective-permute-start(bf16[2,256,512]{2,1,0:T(8,128)(2,1)S(1)} %pad_maximum_fusion.own_ref), channel_id=1, source_target_pairs={{192,0},{196,4},{200,8},{204,12},{208,16},{212,20},{216,24},{220,2... | collective-permute-start | bytes 1572872 | tf_op jit(solution)/shard_map/ppermute | solution.py:55
  110.7 21.5 %collective-permute-start.15 = (bf16[2,64,512]{2,1,0:T(8,128)(2,1)S(1)}, bf16[2,64,512]{2,1,0:T(8,128)(2,1)S(1)}, u32[]{:S(2)}, u32[]{:S(2)}) collective-permute-start(bf16[2,64,512]{2,1,0:T(8,128)(2,1)S(1)} %convert_element_type.63), channel_id=1, source_target_pairs={{4,0},{12,8},{20,16},{28,24},{36,32},{44,40},{52,48},{60,56},{68,6... | collective-permute-start | bytes 393224 | tf_op jit(solution)/shard_map/ppermute | solution.py:48
  112.0 28.6 %collective-permute-start.17 = (bf16[2,256,512]{2,1,0:T(8,128)(2,1)}, bf16[2,256,512]{2,1,0:T(8,128)(2,1)S(1)}, u32[]{:S(2)}, u32[]{:S(2)}) collective-permute-start(bf16[2,256,512]{2,1,0:T(8,128)(2,1)} %get-tuple-element.27), channel_id=1, source_target_pairs={{128,0},{132,4},{136,8},{140,12},{144,16},{148,20},{152,24},{156,2... | collective-permute-start | bytes 1572872 | tf_op jit(solution)/shard_map/ppermute | solution.py:55
  120.0 29.5 %collective-permute-start.18 = (bf16[2,256,512]{2,1,0:T(8,128)(2,1)}, bf16[2,256,512]{2,1,0:T(8,128)(2,1)S(1)}, u32[]{:S(2)}, u32[]{:S(2)}) collective-permute-start(bf16[2,256,512]{2,1,0:T(8,128)(2,1)} %get-tuple-element.28), channel_id=1, source_target_pairs={{64,0},{68,4},{72,8},{76,12},{80,16},{84,20},{88,24},{92,28},{96,3... | collective-permute-start | bytes 1572872 | tf_op jit(solution)/shard_map/ppermute | solution.py:55
  128.0 27.7 %collective-permute-start.19 = (bf16[2,256,512]{2,1,0:T(8,128)(2,1)}, bf16[2,256,512]{2,1,0:T(8,128)(2,1)S(1)}, u32[]{:S(2)}, u32[]{:S(2)}) collective-permute-start(bf16[2,256,512]{2,1,0:T(8,128)(2,1)} %get-tuple-element.29), channel_id=1, source_target_pairs={{96,0},{100,4},{104,8},{108,12},{112,16},{116,20},{120,24},{124,28... | collective-permute-start | bytes 1572872 | tf_op jit(solution)/shard_map/ppermute | solution.py:55
  129.7 43.6 %collective-permute-start.20 = (bf16[2,256,512]{2,1,0:T(8,128)(2,1)}, bf16[2,256,512]{2,1,0:T(8,128)(2,1)S(1)}, u32[]{:S(2)}, u32[]{:S(2)}) collective-permute-start(bf16[2,256,512]{2,1,0:T(8,128)(2,1)} %get-tuple-element.30), channel_id=1, source_target_pairs={{160,0},{164,4},{168,8},{172,12},{176,16},{180,20},{184,24},{188,2... | collective-permute-start | bytes 1572872 | tf_op jit(solution)/shard_map/ppermute | solution.py:55
  132.2 8.4 %collective-permute-start.16 = (bf16[2,64,512]{2,1,0:T(8,128)(2,1)S(1)}, bf16[2,64,512]{2,1,0:T(8,128)(2,1)S(1)}, u32[]{:S(2)}, u32[]{:S(2)}) collective-permute-start(bf16[2,64,512]{2,1,0:T(8,128)(2,1)S(1)} %fusion.2), channel_id=1, source_target_pairs={{8,0},{24,16},{40,32},{56,48},{72,64},{88,80},{104,96},{120,112},{... | collective-permute-start | bytes 393224 | tf_op jit(solution)/shard_map/ppermute | solution.py:48
  173.3 9.3 %collective-permute-start.24 = (bf16[2,64,512]{2,1,0:T(8,128)(2,1)S(1)}, bf16[2,64,512]{2,1,0:T(8,128)(2,1)S(1)}, u32[]{:S(2)}, u32[]{:S(2)}) collective-permute-start(bf16[2,64,512]{2,1,0:T(8,128)(2,1)S(1)} %convert_element_type.72), channel_id=1, source_target_pairs={{48,0},{112,64},{176,128},{240,192},{49,1},{113,65},{177,129},{241... | collective-permute-start | bytes 393224 | tf_op jit(solution)/shard_map/ppermute | solution.py:48
  174.6 10.7 %collective-permute-start.23 = (bf16[2,64,512]{2,1,0:T(8,128)(2,1)S(1)}, bf16[2,64,512]{2,1,0:T(8,128)(2,1)S(1)}, u32[]{:S(2)}, u32[]{:S(2)}) collective-permute-start(bf16[2,64,512]{2,1,0:T(8,128)(2,1)S(1)} %convert_element_type.72), channel_id=1, source_target_pairs={{32,0},{96,64},{160,128},{224,192},{33,1},{97,65},{161,129},{225,1... | collective-permute-start | bytes 393224 | tf_op jit(solution)/shard_map/ppermute | solution.py:48
  175.9 12.2 %collective-permute-start.22 = (bf16[2,64,512]{2,1,0:T(8,128)(2,1)S(1)}, bf16[2,64,512]{2,1,0:T(8,128)(2,1)S(1)}, u32[]{:S(2)}, u32[]{:S(2)}) collective-permute-start(bf16[2,64,512]{2,1,0:T(8,128)(2,1)S(1)} %convert_element_type.72), channel_id=1, source_target_pairs={{16,0},{80,64},{144,128},{208,192},{17,1},{81,65},{145,129},{209,1... | collective-permute-start | bytes 393224 | tf_op jit(solution)/shard_map/ppermute | solution.py:48
  177.2 16.9 %collective-permute-start.21 = (bf16[2,64,512]{2,1,0:T(8,128)(2,1)}, bf16[2,64,512]{2,1,0:T(8,128)(2,1)S(1)}, u32[]{:S(2)}, u32[]{:S(2)}) collective-permute-start(bf16[2,64,512]{2,1,0:T(8,128)(2,1)} %get-tuple-element.35), channel_id=1, source_target_pairs={{0,4},{4,8},{8,12},{12,16},{16,20},{20,24},{24,28},{28,32},{32,36}... | collective-permute-start | bytes 393224 | tf_op jit(solution)/shard_map/ppermute | solution.py:61
  179.7 14.5 %collective-permute-start.28 = (bf16[2,64,512]{2,1,0:T(8,128)(2,1)S(1)}, bf16[2,64,512]{2,1,0:T(8,128)(2,1)S(1)}, u32[]{:S(2)}, u32[]{:S(2)}) collective-permute-start(bf16[2,64,512]{2,1,0:T(8,128)(2,1)S(1)} %copy-done.10), channel_id=1, source_target_pairs={{4,0},{8,4},{12,8},{16,12},{20,16},{24,20},{28,24},{32,28},{36,32}... | collective-permute-start | bytes 393224 | tf_op jit(solution)/shard_map/ppermute | solution.py:61
  188.1 13.5 %collective-permute-start.27 = (bf16[2,64,512]{2,1,0:T(8,128)(2,1)S(1)}, bf16[2,64,512]{2,1,0:T(8,128)(2,1)S(1)}, u32[]{:S(2)}, u32[]{:S(2)}) collective-permute-start(bf16[2,64,512]{2,1,0:T(8,128)(2,1)S(1)} %fusion.5), channel_id=1, source_target_pairs={{192,0},{193,1},{194,2},{195,3}} | collective-permute-start | bytes 393224 | tf_op jit(solution)/shard_map/ppermute | solution.py:48
  189.4 12.2 %collective-permute-start.26 = (bf16[2,64,512]{2,1,0:T(8,128)(2,1)S(1)}, bf16[2,64,512]{2,1,0:T(8,128)(2,1)S(1)}, u32[]{:S(2)}, u32[]{:S(2)}) collective-permute-start(bf16[2,64,512]{2,1,0:T(8,128)(2,1)S(1)} %fusion.5), channel_id=1, source_target_pairs={{128,0},{129,1},{130,2},{131,3}} | collective-permute-start | bytes 393224 | tf_op jit(solution)/shard_map/ppermute | solution.py:48
  190.7 11.1 %collective-permute-start.25 = (bf16[2,64,512]{2,1,0:T(8,128)(2,1)S(1)}, bf16[2,64,512]{2,1,0:T(8,128)(2,1)S(1)}, u32[]{:S(2)}, u32[]{:S(2)}) collective-permute-start(bf16[2,64,512]{2,1,0:T(8,128)(2,1)S(1)} %fusion.5), channel_id=1, source_target_pairs={{64,0},{65,1},{66,2},{67,3}} | collective-permute-start | bytes 393224 | tf_op jit(solution)/shard_map/ppermute | solution.py:48
  (18 other events, 351.8 us)
Sparse Core Ops, SparseCore 0:
  9.8 32.5 all-gather.1
  110.8 29.6 reduce-scatter.1

commit v5 on v4

--- a/solution.py
+++ b/solution.py
@@ -215,9 +215,7 @@
     low = shifted(key_value[:, -BS:], "ctx", 1)
     high = shifted(key_value[:, :BS], "ctx", -1)
     anchor = spread_down(key_value[:, :BS], "ctx")
-    arrivals = [from_behind(key_value, "ctx", offsets[0])]
-    anchor, held = lax.optimization_barrier((anchor, key_value))
-    arrivals += [from_behind(held, "ctx", offset) for offset in offsets[1:]]
+    arrivals = [from_behind(key_value, "ctx", offset) for offset in offsets]
     grad_attention = lax.dot_general(
         lax.all_gather(upstream, "head", axis=1, tiled=True),
         out_weight,

time: 211 us -> 204 us (0.967)
  waiting for transfers between devices: 93.9 us -> 83.9 us
    ppermute x8, waiting for transfers between devices: 62.7 us -> 32.3 us  [from_behind(): return lax.ppermute(block, axis, route)]
    ppermute x9, waiting for transfers between devices: 5.71 us -> 24.2 us  [spread_down(): lax.ppermute(value, axis, [(i, i + turn * stride) for i in range(0, count...]
  transfers between devices with their start and end apart: 31 -> 31, of which waited for: 16 -> 18; matrix products, arithmetic and copies ran while one was open for 6% -> 7% of each run, Pallas kernels for 0% -> 0%
where the time goes in v5:
time: 204 us; the launch traced here: 203 us
  waiting for transfers between devices  83.9 us (41%)
  starting transfers between devices  71.7 us (35%)
  Pallas kernels  14.9 us (7%)
  between operations  14.5 us (7%)
  other arithmetic  7.35 us (4%)
  matrix products  5.37 us (3%)
  local copies, waits for them, and re-layouts  4.87 us (2%)
    ppermute x8, waiting for transfers between devices, from_behind(): return lax.ppermute(block, axis, route)  32.3 us
    ppermute x8, starting transfers between devices, from_behind(): return lax.ppermute(block, axis, route)  29.4 us
    ppermute x9, waiting for transfers between devices, spread_down(): lax.ppermute(value, axis, [(i, i + turn * stride) for i in range(0, count...  24.2 us
    ppermute x9, starting transfers between devices, spread_down(): lax.ppermute(value, axis, [(i, i + turn * stride) for i in range(0, count...  23.7 us
    ppermute x8, waiting for transfers between devices, sum_up(): value = value + lax.ppermute(sent, axis, route).astype(jnp.float32)  21.9 us
    pallas_call x1, Pallas kernels, attention_both_ways(): pl.pallas_call(functools.partial(attend, run_blocks, 1.0 / math.sqrt(HDIM...  14.9 us
    ppermute x8, starting transfers between devices, sum_up(): value = value + lax.ppermute(sent, axis, route).astype(jnp.float32)  10.3 us
    ppermute x4, starting transfers between devices, shifted(): return lax.ppermute(block, axis, route)  8.24 us
  transfers between devices with their start and end apart: 31, of which 18 were waited for; matrix products, arithmetic and copies ran while one was open for 7% of the time, Pallas kernels for 0%

profile of v5, /device:TPU:8, one launch (start us, length us, event | category | flops | bytes accessed | tf_op | source)
XLA Modules:
  0.0 202.6 jit_solution(6888034291758770996)
XLA Ops:
  9.6 9.1 %collective-permute-start.4 = (bf16[2,64,512]{2,1,0:T(8,128)(2,1)S(1)}, bf16[2,64,512]{2,1,0:T(8,128)(2,1)S(1)}, u32[]{:S(2)}, u32[]{:S(2)}) collective-permute-start(bf16[2,64,512]{2,1,0:T(8,128)(2,1)S(1)} %get-tuple-element.38), channel_id=1, source_target_pairs={{0,64},{1,65},{2,66},{3,67}} | collective-permute-start | bytes 393224 | tf_op jit(solution)/shard_map/ppermute | solution.py:29
  20.0 2.4 %collective-permute-start.2 = (bf16[2,64,512]{2,1,0:T(8,128)(2,1)S(1)}, bf16[2,64,512]{2,1,0:T(8,128)(2,1)}, u32[]{:S(2)}, u32[]{:S(2)}) collective-permute-start(bf16[2,64,512]{2,1,0:T(8,128)(2,1)S(1)} %get-tuple-element.38), channel_id=1, source_target_pairs={{0,192},{1,193},{2,194},{3,195}} | collective-permute-start | bytes 393224 | tf_op jit(solution)/shard_map/ppermute | solution.py:29
  26.8 2.5 %collective-permute-start.6 = (bf16[2,64,512]{2,1,0:T(8,128)(2,1)S(1)}, bf16[2,64,512]{2,1,0:T(8,128)(2,1)}, u32[]{:S(2)}, u32[]{:S(2)}) collective-permute-start(bf16[2,64,512]{2,1,0:T(8,128)(2,1)S(1)} %select_select_fusion.2), channel_id=1, source_target_pairs={{0,32},{64,96},{128,160},{192,224},{1,33},{65,97},{129,161},{193,2... | collective-permute-start | bytes 393224 | tf_op jit(solution)/shard_map/ppermute | solution.py:29
  33.6 18.0 %collective-permute-done.7 = bf16[2,64,512]{2,1,0:T(8,128)(2,1)S(1)} collective-permute-done((bf16[2,64,512]{2,1,0:T(8,128)(2,1)S(1)}, bf16[2,64,512]{2,1,0:T(8,128)(2,1)S(1)}, u32[]{:S(2)}, u32[]{:S(2)}) %collective-permute-start.7) | collective-permute-done | bytes 131104 | tf_op jit(solution)/shard_map/ppermute | solution.py:29
  51.6 2.8 %collective-permute-done.6 = bf16[2,64,512]{2,1,0:T(8,128)(2,1)} collective-permute-done((bf16[2,64,512]{2,1,0:T(8,128)(2,1)S(1)}, bf16[2,64,512]{2,1,0:T(8,128)(2,1)}, u32[]{:S(2)}, u32[]{:S(2)}) %collective-permute-start.6) | collective-permute-done | bytes 131104 | tf_op jit(solution)/shard_map/ppermute | solution.py:29
  58.6 2.0 collective-permute-start.9
  60.5 1.9 collective-permute-start.8
  63.8 4.0 %collective-permute-start.14 = (bf16[2,256,512]{2,1,0:T(8,128)(2,1)S(1)}, bf16[2,256,512]{2,1,0:T(8,128)(2,1)}, u32[]{:S(2)}, u32[]{:S(2)}) collective-permute-start(bf16[2,256,512]{2,1,0:T(8,128)(2,1)S(1)} %pad_maximum_fusion.own_ref), channel_id=1, source_target_pairs={{96,0},{100,4},{104,8},{108,12},{112,16},{116,20},{120,24},{124,28... | collective-permute-start | bytes 1572872 | tf_op jit(solution)/shard_map/ppermute | solution.py:55
  67.8 3.3 %collective-permute-start = (bf16[2,64,512]{2,1,0:T(8,128)(2,1)}, bf16[2,64,512]{2,1,0:T(8,128)(2,1)}, u32[]{:S(2)}, u32[]{:S(2)}) collective-permute-start(bf16[2,64,512]{2,1,0:T(8,128)(2,1)} %get-tuple-element.39), channel_id=1, source_target_pairs={{0,4},{4,8},{8,12},{12,16},{16,20},{20,24},{24,28},{28,32},{32,36}... | collective-permute-start | bytes 393224 | tf_op jit(solution)/shard_map/ppermute | solution.py:61
  74.6 2.7 %convolution_convert_fusion.1.g_ref = bf16[256,512]{1,0:T(8,128)(2,1)} fusion(bf16[256,2048]{1,0:T(8,128)(2,1)} %all-gather.2.cloned.1.call-done, bf16[512,2048]{1,0:T(8,128)(2,1)S(1)} %copy-done), kind=kOutput, calls=%fused_computation.1 | convolution fusion | flops 537001984 | bytes 3407872 | tf_op jit(solution)/shard_map/dot_general | solution.py:219
  77.2 3.3 %collective-permute-done.1.high_ref = bf16[2,64,512]{2,1,0:T(8,128)(2,1)S(1)} collective-permute-done((bf16[2,64,512]{2,1,0:T(8,128)(2,1)S(1)}, bf16[2,64,512]{2,1,0:T(8,128)(2,1)S(1)}, u32[]{:S(2)}, u32[]{:S(2)}) %collective-permute-start.1) | collective-permute-done | bytes 131104 | tf_op jit(solution)/shard_map/ppermute | solution.py:61
  81.4 14.9 %attention_both_ways.1 = (bf16[256,512]{1,0:T(8,128)(2,1)}, bf16[256,512]{1,0:T(8,128)(2,1)}, f32[2,256,512]{2,1,0:T(8,128)}, bf16[2,64,512]{2,1,0:T(8,128)(2,1)...) custom-call(s32[12]{0:T(128)} %reshape.32.picks, ...), custom_call_target="tpu_custom_call" | custom-call | flops 587202560 | bytes 8388608 | tf_op jit(solution)/shard_map/attention_both_ways/pallas_call | solution.py:166
  96.3 2.7 %convolution_convert_fusion = bf16[256,2048]{1,0:T(8,128)(2,1)} fusion(bf16[256,512]{1,0:T(8,128)(2,1)} %get-tuple-element.19, bf16[512,2048]{1,0:T(8,128)(2,1)S(1)} %copy-done), kind=kOutput, calls=%fused_computation | convolution fusion | flops 537395200 | bytes 3407872 | tf_op jit(solution)/shard_map/dot_general | solution.py:230
  100.4 7.2 %collective-permute-start.17 = (bf16[2,256,512]{2,1,0:T(8,128)(2,1)}, bf16[2,256,512]{2,1,0:T(8,128)(2,1)S(1)}, u32[]{:S(2)}, u32[]{:S(2)}) collective-permute-start(bf16[2,256,512]{2,1,0:T(8,128)(2,1)} %get-tuple-element.23), channel_id=1, source_target_pairs={{128,0},{132,4},{136,8},{140,12},{144,16},{148,20},{152,24},{156,2... | collective-permute-start | bytes 1572872 | tf_op jit(solution)/shard_map/ppermute | solution.py:55
  107.6 13.8 %collective-permute-start.18 = (bf16[2,256,512]{2,1,0:T(8,128)(2,1)}, bf16[2,256,512]{2,1,0:T(8,128)(2,1)S(1)}, u32[]{:S(2)}, u32[]{:S(2)}) collective-permute-start(bf16[2,256,512]{2,1,0:T(8,128)(2,1)} %get-tuple-element.24), channel_id=1, source_target_pairs={{64,0},{68,4},{72,8},{76,12},{80,16},{84,20},{88,24},{92,28},{96,3... | collective-permute-start | bytes 1572872 | tf_op jit(solution)/shard_map/ppermute | solution.py:55
  121.4 4.1 %collective-permute-start.20 = (bf16[2,256,512]{2,1,0:T(8,128)(2,1)}, bf16[2,256,512]{2,1,0:T(8,128)(2,1)S(1)}, u32[]{:S(2)}, u32[]{:S(2)}) collective-permute-start(bf16[2,256,512]{2,1,0:T(8,128)(2,1)} %get-tuple-element.26), channel_id=1, source_target_pairs={{160,0},{164,4},{168,8},{172,12},{176,16},{180,20},{184,24},{188,2... | collective-permute-start | bytes 1572872 | tf_op jit(solution)/shard_map/ppermute | solution.py:55
  126.8 7.1 %collective-permute-done.16 = bf16[2,64,512]{2,1,0:T(8,128)(2,1)S(1)} collective-permute-done((bf16[2,64,512]{2,1,0:T(8,128)(2,1)S(1)}, bf16[2,64,512]{2,1,0:T(8,128)(2,1)S(1)}, u32[]{:S(2)}, u32[]{:S(2)}) %collective-permute-start.16) | collective-permute-done | bytes 131104 | tf_op jit(solution)/shard_map/ppermute | solution.py:48
  134.0 10.2 %collective-permute-done.18 = bf16[2,256,512]{2,1,0:T(8,128)(2,1)S(1)} collective-permute-done((bf16[2,256,512]{2,1,0:T(8,128)(2,1)}, bf16[2,256,512]{2,1,0:T(8,128)(2,1)S(1)}, u32[]{:S(2)}, u32[]{:S(2)}) %collective-permute-start.18) | collective-permute-done | bytes 524320 | tf_op jit(solution)/shard_map/ppermute | solution.py:55
  144.2 20.0 %collective-permute-done.19 = bf16[2,256,512]{2,1,0:T(8,128)(2,1)S(1)} collective-permute-done((bf16[2,256,512]{2,1,0:T(8,128)(2,1)}, bf16[2,256,512]{2,1,0:T(8,128)(2,1)S(1)}, u32[]{:S(2)}, u32[]{:S(2)}) %collective-permute-start.19) | collective-permute-done | bytes 524320 | tf_op jit(solution)/shard_map/ppermute | solution.py:55
  170.0 2.4 %collective-permute-start.21 = (bf16[2,64,512]{2,1,0:T(8,128)(2,1)}, bf16[2,64,512]{2,1,0:T(8,128)(2,1)S(1)}, u32[]{:S(2)}, u32[]{:S(2)}) collective-permute-start(bf16[2,64,512]{2,1,0:T(8,128)(2,1)} %get-tuple-element.31), channel_id=1, source_target_pairs={{0,4},{4,8},{8,12},{12,16},{16,20},{20,24},{24,28},{28,32},{32,36}... | collective-permute-start | bytes 393224 | tf_op jit(solution)/shard_map/ppermute | solution.py:61
  175.3 2.7 %collective-permute-done.23 = bf16[2,64,512]{2,1,0:T(8,128)(2,1)S(1)} collective-permute-done((bf16[2,64,512]{2,1,0:T(8,128)(2,1)S(1)}, bf16[2,64,512]{2,1,0:T(8,128)(2,1)S(1)}, u32[]{:S(2)}, u32[]{:S(2)}) %collective-permute-start.23) | collective-permute-done | bytes 131104 | tf_op jit(solution)/shard_map/ppermute | solution.py:48
  178.1 2.7 %collective-permute-done.22 = bf16[2,64,512]{2,1,0:T(8,128)(2,1)S(1)} collective-permute-done((bf16[2,64,512]{2,1,0:T(8,128)(2,1)S(1)}, bf16[2,64,512]{2,1,0:T(8,128)(2,1)S(1)}, u32[]{:S(2)}, u32[]{:S(2)}) %collective-permute-start.22) | collective-permute-done | bytes 131104 | tf_op jit(solution)/shard_map/ppermute | solution.py:48
  184.7 2.0 %convert_add_fusion = f32[2,256,512]{2,1,0:T(8,128)S(1)} fusion(bf16[2,256,512]{2,1,0:T(8,128)(2,1)} %copy-done.6, bf16[2,256,512]{2,1,0:T(8,128)(2,1)} %copy-done.5, bf16[2,256,512]{2,1,0:T(8,128)(2,1)} %copy-done.4, f32[2,256,512]{2,1,0:T(8,128)} %get-tuple-element.21, bf16[2,256,512]{2,1,0:T(8,128)(2,1)S(1)} %collective-permute-done.17), kind=kLoop, calls=%fused_computation.2 | loop fusion | flops 2097152 | bytes 4194304 | tf_op jit(solution)/shard_map/add | solution.py:242
  186.8 7.6 %collective-permute-done.27 = bf16[2,64,512]{2,1,0:T(8,128)(2,1)S(1)} collective-permute-done((bf16[2,64,512]{2,1,0:T(8,128)(2,1)S(1)}, bf16[2,64,512]{2,1,0:T(8,128)(2,1)S(1)}, u32[]{:S(2)}, u32[]{:S(2)}) %collective-permute-start.27) | collective-permute-done | bytes 131104 | tf_op jit(solution)/shard_map/ppermute | solution.py:48
  (94 shorter events, 38.7 us)
Async XLA Ops:
  7.2 67.3 %all-gather.2.cloned.1.call-start = ((), (), s32[]{:S(2)}) async-start(), calls=%async_computation.1 | async-start | bytes 1310720 | tf_op jit(solution)/shard_map/all_gather | solution.py:220
  7.9 187.8 %reduce-scatter.2.cloned.1.call-start = ((), (), s32[]{:S(2)}) async-start(), calls=%async_computation.2 | async-start | bytes 1310720 | tf_op jit(solution)/shard_map/reduce_scatter | solution.py:231
  9.6 14.2 %collective-permute-start.4 = (bf16[2,64,512]{2,1,0:T(8,128)(2,1)S(1)}, bf16[2,64,512]{2,1,0:T(8,128)(2,1)S(1)}, u32[]{:S(2)}, u32[]{:S(2)}) collective-permute-start(bf16[2,64,512]{2,1,0:T(8,128)(2,1)S(1)} %get-tuple-element.38), channel_id=1, source_target_pairs={{0,64},{1,65},{2,66},{3,67}} | collective-permute-start | bytes 393224 | tf_op jit(solution)/shard_map/ppermute | solution.py:29
  23.5 57.0 %collective-permute-start.13 = (bf16[2,256,512]{2,1,0:T(8,128)(2,1)S(1)}, bf16[2,256,512]{2,1,0:T(8,128)(2,1)S(1)}, u32[]{:S(2)}, u32[]{:S(2)}) collective-permute-start(bf16[2,256,512]{2,1,0:T(8,128)(2,1)S(1)} %pad_maximum_fusion.own_ref), channel_id=1, source_target_pairs={{160,0},{164,4},{168,8},{172,12},{176,16},{180,20},{184,24},{188,2... | collective-permute-start | bytes 1572872 | tf_op jit(solution)/shard_map/ppermute | solution.py:55
  23.6 56.9 %collective-permute-start.12 = (bf16[2,256,512]{2,1,0:T(8,128)(2,1)S(1)}, bf16[2,256,512]{2,1,0:T(8,128)(2,1)}, u32[]{:S(2)}, u32[]{:S(2)}) collective-permute-start(bf16[2,256,512]{2,1,0:T(8,128)(2,1)S(1)} %pad_maximum_fusion.own_ref), channel_id=1, source_target_pairs={{192,0},{196,4},{200,8},{204,12},{208,16},{212,20},{216,24},{220,2... | collective-permute-start | bytes 1572872 | tf_op jit(solution)/shard_map/ppermute | solution.py:55
  25.5 26.2 %collective-permute-start.7 = (bf16[2,64,512]{2,1,0:T(8,128)(2,1)S(1)}, bf16[2,64,512]{2,1,0:T(8,128)(2,1)S(1)}, u32[]{:S(2)}, u32[]{:S(2)}) collective-permute-start(bf16[2,64,512]{2,1,0:T(8,128)(2,1)S(1)} %select_select_fusion.2), channel_id=1, source_target_pairs={{0,16},{64,80},{128,144},{192,208},{1,17},{65,81},{129,145},{193,2... | collective-permute-start | bytes 393224 | tf_op jit(solution)/shard_map/ppermute | solution.py:29
  26.8 27.7 %collective-permute-start.6 = (bf16[2,64,512]{2,1,0:T(8,128)(2,1)S(1)}, bf16[2,64,512]{2,1,0:T(8,128)(2,1)}, u32[]{:S(2)}, u32[]{:S(2)}) collective-permute-start(bf16[2,64,512]{2,1,0:T(8,128)(2,1)S(1)} %select_select_fusion.2), channel_id=1, source_target_pairs={{0,32},{64,96},{128,160},{192,224},{1,33},{65,97},{129,161},{193,2... | collective-permute-start | bytes 393224 | tf_op jit(solution)/shard_map/ppermute | solution.py:29
  29.2 27.1 %collective-permute-start.5 = (bf16[2,64,512]{2,1,0:T(8,128)(2,1)S(1)}, bf16[2,64,512]{2,1,0:T(8,128)(2,1)}, u32[]{:S(2)}, u32[]{:S(2)}) collective-permute-start(bf16[2,64,512]{2,1,0:T(8,128)(2,1)S(1)} %select_select_fusion.2), channel_id=1, source_target_pairs={{0,48},{64,112},{128,176},{192,240},{1,49},{65,113},{129,177},{193... | collective-permute-start | bytes 393224 | tf_op jit(solution)/shard_map/ppermute | solution.py:29
  63.3 17.3 %collective-permute-start.11 = (bf16[2,256,512]{2,1,0:T(8,128)(2,1)S(1)}, bf16[2,256,512]{2,1,0:T(8,128)(2,1)}, u32[]{:S(2)}, u32[]{:S(2)}) collective-permute-start(bf16[2,256,512]{2,1,0:T(8,128)(2,1)S(1)} %pad_maximum_fusion.own_ref), channel_id=1, source_target_pairs={{128,0},{132,4},{136,8},{140,12},{144,16},{148,20},{152,24},{156,2... | collective-permute-start | bytes 1572872 | tf_op jit(solution)/shard_map/ppermute | solution.py:55
  63.8 17.0 %collective-permute-start.14 = (bf16[2,256,512]{2,1,0:T(8,128)(2,1)S(1)}, bf16[2,256,512]{2,1,0:T(8,128)(2,1)}, u32[]{:S(2)}, u32[]{:S(2)}) collective-permute-start(bf16[2,256,512]{2,1,0:T(8,128)(2,1)S(1)} %pad_maximum_fusion.own_ref), channel_id=1, source_target_pairs={{96,0},{100,4},{104,8},{108,12},{112,16},{116,20},{120,24},{124,28... | collective-permute-start | bytes 1572872 | tf_op jit(solution)/shard_map/ppermute | solution.py:55
  99.1 26.4 %collective-permute-start.15 = (bf16[2,64,512]{2,1,0:T(8,128)(2,1)S(1)}, bf16[2,64,512]{2,1,0:T(8,128)(2,1)S(1)}, u32[]{:S(2)}, u32[]{:S(2)}) collective-permute-start(bf16[2,64,512]{2,1,0:T(8,128)(2,1)S(1)} %convert_element_type.63), channel_id=1, source_target_pairs={{4,0},{12,8},{20,16},{28,24},{36,32},{44,40},{52,48},{60,56},{68,6... | collective-permute-start | bytes 393224 | tf_op jit(solution)/shard_map/ppermute | solution.py:48
  100.4 33.6 %collective-permute-start.17 = (bf16[2,256,512]{2,1,0:T(8,128)(2,1)}, bf16[2,256,512]{2,1,0:T(8,128)(2,1)S(1)}, u32[]{:S(2)}, u32[]{:S(2)}) collective-permute-start(bf16[2,256,512]{2,1,0:T(8,128)(2,1)} %get-tuple-element.23), channel_id=1, source_target_pairs={{128,0},{132,4},{136,8},{140,12},{144,16},{148,20},{152,24},{156,2... | collective-permute-start | bytes 1572872 | tf_op jit(solution)/shard_map/ppermute | solution.py:55
  107.6 36.6 %collective-permute-start.18 = (bf16[2,256,512]{2,1,0:T(8,128)(2,1)}, bf16[2,256,512]{2,1,0:T(8,128)(2,1)S(1)}, u32[]{:S(2)}, u32[]{:S(2)}) collective-permute-start(bf16[2,256,512]{2,1,0:T(8,128)(2,1)} %get-tuple-element.24), channel_id=1, source_target_pairs={{64,0},{68,4},{72,8},{76,12},{80,16},{84,20},{88,24},{92,28},{96,3... | collective-permute-start | bytes 1572872 | tf_op jit(solution)/shard_map/ppermute | solution.py:55
  121.4 42.8 %collective-permute-start.19 = (bf16[2,256,512]{2,1,0:T(8,128)(2,1)}, bf16[2,256,512]{2,1,0:T(8,128)(2,1)S(1)}, u32[]{:S(2)}, u32[]{:S(2)}) collective-permute-start(bf16[2,256,512]{2,1,0:T(8,128)(2,1)} %get-tuple-element.25), channel_id=1, source_target_pairs={{96,0},{100,4},{104,8},{108,12},{112,16},{116,20},{120,24},{124,28... | collective-permute-start | bytes 1572872 | tf_op jit(solution)/shard_map/ppermute | solution.py:55
  121.4 44.6 %collective-permute-start.20 = (bf16[2,256,512]{2,1,0:T(8,128)(2,1)}, bf16[2,256,512]{2,1,0:T(8,128)(2,1)S(1)}, u32[]{:S(2)}, u32[]{:S(2)}) collective-permute-start(bf16[2,256,512]{2,1,0:T(8,128)(2,1)} %get-tuple-element.26), channel_id=1, source_target_pairs={{160,0},{164,4},{168,8},{172,12},{176,16},{180,20},{184,24},{188,2... | collective-permute-start | bytes 1572872 | tf_op jit(solution)/shard_map/ppermute | solution.py:55
  125.5 8.4 %collective-permute-start.16 = (bf16[2,64,512]{2,1,0:T(8,128)(2,1)S(1)}, bf16[2,64,512]{2,1,0:T(8,128)(2,1)S(1)}, u32[]{:S(2)}, u32[]{:S(2)}) collective-permute-start(bf16[2,64,512]{2,1,0:T(8,128)(2,1)S(1)} %fusion.2), channel_id=1, source_target_pairs={{8,0},{24,16},{40,32},{56,48},{72,64},{88,80},{104,96},{120,112},{... | collective-permute-start | bytes 393224 | tf_op jit(solution)/shard_map/ppermute | solution.py:48
  166.0 9.3 %collective-permute-start.24 = (bf16[2,64,512]{2,1,0:T(8,128)(2,1)S(1)}, bf16[2,64,512]{2,1,0:T(8,128)(2,1)S(1)}, u32[]{:S(2)}, u32[]{:S(2)}) collective-permute-start(bf16[2,64,512]{2,1,0:T(8,128)(2,1)S(1)} %convert_element_type.72), channel_id=1, source_target_pairs={{48,0},{112,64},{176,128},{240,192},{49,1},{113,65},{177,129},{241... | collective-permute-start | bytes 393224 | tf_op jit(solution)/shard_map/ppermute | solution.py:48
  167.4 10.7 %collective-permute-start.23 = (bf16[2,64,512]{2,1,0:T(8,128)(2,1)S(1)}, bf16[2,64,512]{2,1,0:T(8,128)(2,1)S(1)}, u32[]{:S(2)}, u32[]{:S(2)}) collective-permute-start(bf16[2,64,512]{2,1,0:T(8,128)(2,1)S(1)} %convert_element_type.72), channel_id=1, source_target_pairs={{32,0},{96,64},{160,128},{224,192},{33,1},{97,65},{161,129},{225,1... | collective-permute-start | bytes 393224 | tf_op jit(solution)/shard_map/ppermute | solution.py:48
  168.7 12.1 %collective-permute-start.22 = (bf16[2,64,512]{2,1,0:T(8,128)(2,1)S(1)}, bf16[2,64,512]{2,1,0:T(8,128)(2,1)S(1)}, u32[]{:S(2)}, u32[]{:S(2)}) collective-permute-start(bf16[2,64,512]{2,1,0:T(8,128)(2,1)S(1)} %convert_element_type.72), channel_id=1, source_target_pairs={{16,0},{80,64},{144,128},{208,192},{17,1},{81,65},{145,129},{209,1... | collective-permute-start | bytes 393224 | tf_op jit(solution)/shard_map/ppermute | solution.py:48
  170.0 16.8 %collective-permute-start.21 = (bf16[2,64,512]{2,1,0:T(8,128)(2,1)}, bf16[2,64,512]{2,1,0:T(8,128)(2,1)S(1)}, u32[]{:S(2)}, u32[]{:S(2)}) collective-permute-start(bf16[2,64,512]{2,1,0:T(8,128)(2,1)} %get-tuple-element.31), channel_id=1, source_target_pairs={{0,4},{4,8},{8,12},{12,16},{16,20},{20,24},{24,28},{28,32},{32,36}... | collective-permute-start | bytes 393224 | tf_op jit(solution)/shard_map/ppermute | solution.py:61
  172.4 14.4 %collective-permute-start.28 = (bf16[2,64,512]{2,1,0:T(8,128)(2,1)S(1)}, bf16[2,64,512]{2,1,0:T(8,128)(2,1)S(1)}, u32[]{:S(2)}, u32[]{:S(2)}) collective-permute-start(bf16[2,64,512]{2,1,0:T(8,128)(2,1)S(1)} %copy-done.12), channel_id=1, source_target_pairs={{4,0},{8,4},{12,8},{16,12},{20,16},{24,20},{28,24},{32,28},{36,32}... | collective-permute-start | bytes 393224 | tf_op jit(solution)/shard_map/ppermute | solution.py:61
  180.8 13.6 %collective-permute-start.27 = (bf16[2,64,512]{2,1,0:T(8,128)(2,1)S(1)}, bf16[2,64,512]{2,1,0:T(8,128)(2,1)S(1)}, u32[]{:S(2)}, u32[]{:S(2)}) collective-permute-start(bf16[2,64,512]{2,1,0:T(8,128)(2,1)S(1)} %fusion.5), channel_id=1, source_target_pairs={{192,0},{193,1},{194,2},{195,3}} | collective-permute-start | bytes 393224 | tf_op jit(solution)/shard_map/ppermute | solution.py:48
  182.1 12.3 %collective-permute-start.26 = (bf16[2,64,512]{2,1,0:T(8,128)(2,1)S(1)}, bf16[2,64,512]{2,1,0:T(8,128)(2,1)S(1)}, u32[]{:S(2)}, u32[]{:S(2)}) collective-permute-start(bf16[2,64,512]{2,1,0:T(8,128)(2,1)S(1)} %fusion.5), channel_id=1, source_target_pairs={{128,0},{129,1},{130,2},{131,3}} | collective-permute-start | bytes 393224 | tf_op jit(solution)/shard_map/ppermute | solution.py:48
  183.4 11.2 %collective-permute-start.25 = (bf16[2,64,512]{2,1,0:T(8,128)(2,1)S(1)}, bf16[2,64,512]{2,1,0:T(8,128)(2,1)S(1)}, u32[]{:S(2)}, u32[]{:S(2)}) collective-permute-start(bf16[2,64,512]{2,1,0:T(8,128)(2,1)S(1)} %fusion.5), channel_id=1, source_target_pairs={{64,0},{65,1},{66,2},{67,3}} | collective-permute-start | bytes 393224 | tf_op jit(solution)/shard_map/ppermute | solution.py:48
  (20 other events, 307.7 us)
Sparse Core Ops, SparseCore 0:
  9.8 39.3 all-gather.1
  99.2 35.4 reduce-scatter.1

commit v6 on v5

--- a/solution.py
+++ b/solution.py
@@ -20,22 +20,17 @@
     return strides
 
 
-def spread_down(value, axis):
-    count = lax.axis_size(axis)
+def spread_down(value, axis, stages):
     position = lax.axis_index(axis)
-    for stride, ways in reversed(tree_strides(count)):
-        digit = (position // stride) % ways
+    for stride, ways in stages:
         arrivals = [
-            lax.ppermute(
-                value, axis, [(i, i + turn * stride) for i in range(0, count, stride * ways)]
-            )
+            lax.ppermute(value, axis, [(i, i + turn * stride) for i in range(stride)])
             for turn in range(1, ways)
         ]
-        holds = position % (stride * ways) == 0
         fresh = arrivals[0]
         for turn in range(2, ways):
-            fresh = jnp.where(digit == turn, arrivals[turn - 1], fresh)
-        value = jnp.where(holds, value, fresh)
+            fresh = jnp.where(position // stride == turn, arrivals[turn - 1], fresh)
+        value = jnp.where(position < stride, value, fresh)
     return value
 
 
@@ -214,8 +209,10 @@
     key_value = jnp.stack([keys, values])
     low = shifted(key_value[:, -BS:], "ctx", 1)
     high = shifted(key_value[:, :BS], "ctx", -1)
-    anchor = spread_down(key_value[:, :BS], "ctx")
     arrivals = [from_behind(key_value, "ctx", offset) for offset in offsets]
+    anchor = spread_down(key_value[:, :BS], "ctx", [(1, 2), (2, 2)])
+    anchor, arrivals = lax.optimization_barrier((anchor, arrivals))
+    anchor = spread_down(anchor, "ctx", tree_strides(axis_count)[1:])
     grad_attention = lax.dot_general(
         lax.all_gather(upstream, "head", axis=1, tiled=True),
         out_weight,

time: 204 us -> 213 us (1.044); the launches traced: 203 us -> 209 us
  starting transfers between devices: 71.7 us -> 78.3 us
    ppermute x8, waiting for transfers between devices: 32.3 us -> 55.9 us  [from_behind(): return lax.ppermute(block, axis, route)]
    ppermute x9 -> x8, waiting for transfers between devices: 24.2 us -> 3.58 us  [spread_down(): lax.ppermute(value, axis, [(i, i + turn * stride) for i in range(stride)])]
    ppermute x4, waiting for transfers between devices: 4.77 us -> 0.01 us  [shifted(): return lax.ppermute(block, axis, route)]
    ppermute x9 -> x8, starting transfers between devices: 23.7 us -> 27.9 us  [spread_down(): lax.ppermute(value, axis, [(i, i + turn * stride) for i in range(stride)])]
    ppermute x8, waiting for transfers between devices: 21.9 us -> 24.3 us  [sum_up(): value = value + lax.ppermute(sent, axis, route).astype(jnp.float32)]
  transfers between devices with their start and end apart: 31 -> 30, of which waited for: 18 -> 12; matrix products, arithmetic and copies ran while one was open for 7% -> 6% of each run, Pallas kernels for 0% -> 0%
where the time goes in v6:
time: 213 us; the launch traced here: 209 us
  waiting for transfers between devices  83.8 us (39%)
  starting transfers between devices  78.3 us (37%)
  Pallas kernels  14.9 us (7%)
  between operations  14.4 us (7%)
  other arithmetic  7.49 us (4%)
  matrix products  5.38 us (3%)
  local copies, waits for them, and re-layouts  4.24 us (2%)
    ppermute x8, waiting for transfers between devices, from_behind(): return lax.ppermute(block, axis, route)  55.9 us
    ppermute x8, starting transfers between devices, from_behind(): return lax.ppermute(block, axis, route)  30.6 us
    ppermute x8, starting transfers between devices, spread_down(): lax.ppermute(value, axis, [(i, i + turn * stride) for i in range(stride)])  27.9 us
    ppermute x8, waiting for transfers between devices, sum_up(): value = value + lax.ppermute(sent, axis, route).astype(jnp.float32)  24.3 us
    pallas_call x1, Pallas kernels, attention_both_ways(): pl.pallas_call(functools.partial(attend, run_blocks, 1.0 / math.sqrt(HDIM...  14.9 us
    ppermute x8, starting transfers between devices, sum_up(): value = value + lax.ppermute(sent, axis, route).astype(jnp.float32)  10.3 us
    ppermute x4, starting transfers between devices, shifted(): return lax.ppermute(block, axis, route)  9.43 us
  transfers between devices with their start and end apart: 30, of which 12 were waited for; matrix products, arithmetic and copies ran while one was open for 6% of the time, Pallas kernels for 0%

profile of v6, /device:TPU:8, one launch (start us, length us, event | category | flops | bytes accessed | tf_op | source)
XLA Modules:
  0.0 208.6 jit_solution(17874853505049769962)
XLA Ops:
  9.0 3.4 %collective-permute-start.2 = (bf16[2,64,512]{2,1,0:T(8,128)(2,1)S(1)}, bf16[2,64,512]{2,1,0:T(8,128)(2,1)S(1)}, u32[]{:S(2)}, u32[]{:S(2)}) collective-permute-start(bf16[2,64,512]{2,1,0:T(8,128)(2,1)S(1)} %get-tuple-element.48), channel_id=1, source_target_pairs={{0,4},{1,5},{2,6},{3,7}} | collective-permute-start | bytes 393224 | tf_op jit(solution)/shard_map/ppermute | solution.py:27
  13.5 3.6 %collective-permute-start.6 = (bf16[2,256,512]{2,1,0:T(8,128)(2,1)S(1)}, bf16[2,256,512]{2,1,0:T(8,128)(2,1)S(1)}, u32[]{:S(2)}, u32[]{:S(2)}) collective-permute-start(bf16[2,256,512]{2,1,0:T(8,128)(2,1)S(1)} %pad_maximum_fusion.own_ref), channel_id=1, source_target_pairs={{160,0},{164,4},{168,8},{172,12},{176,16},{180,20},{184,24},{188,2... | collective-permute-start | bytes 1572872 | tf_op jit(solution)/shard_map/ppermute | solution.py:50
  17.1 2.3 %collective-permute-start.5 = (bf16[2,256,512]{2,1,0:T(8,128)(2,1)S(1)}, bf16[2,256,512]{2,1,0:T(8,128)(2,1)}, u32[]{:S(2)}, u32[]{:S(2)}) collective-permute-start(bf16[2,256,512]{2,1,0:T(8,128)(2,1)S(1)} %pad_maximum_fusion.own_ref), channel_id=1, source_target_pairs={{192,0},{196,4},{200,8},{204,12},{208,16},{212,20},{216,24},{220,2... | collective-permute-start | bytes 1572872 | tf_op jit(solution)/shard_map/ppermute | solution.py:50
  20.6 5.0 %collective-permute-start.7 = (bf16[2,256,512]{2,1,0:T(8,128)(2,1)S(1)}, bf16[2,256,512]{2,1,0:T(8,128)(2,1)}, u32[]{:S(2)}, u32[]{:S(2)}) collective-permute-start(bf16[2,256,512]{2,1,0:T(8,128)(2,1)S(1)} %pad_maximum_fusion.own_ref), channel_id=1, source_target_pairs={{96,0},{100,4},{104,8},{108,12},{112,16},{116,20},{120,24},{124,28... | collective-permute-start | bytes 1572872 | tf_op jit(solution)/shard_map/ppermute | solution.py:50
  25.8 4.9 %collective-permute-start.3 = (bf16[2,64,512]{2,1,0:T(8,128)(2,1)S(1)}, bf16[2,64,512]{2,1,0:T(8,128)(2,1)S(1)}, u32[]{:S(2)}, u32[]{:S(2)}) collective-permute-start(bf16[2,64,512]{2,1,0:T(8,128)(2,1)S(1)} %broadcast_select_fusion), channel_id=1, source_target_pairs={{0,8},{4,12},{1,9},{5,13},{2,10},{6,14},{3,11},{7,15}} | collective-permute-start | bytes 393224 | tf_op jit(solution)/shard_map/ppermute | solution.py:27
  30.7 2.5 %collective-permute-done.3 = bf16[2,64,512]{2,1,0:T(8,128)(2,1)S(1)} collective-permute-done((bf16[2,64,512]{2,1,0:T(8,128)(2,1)S(1)}, bf16[2,64,512]{2,1,0:T(8,128)(2,1)S(1)}, u32[]{:S(2)}, u32[]{:S(2)}) %collective-permute-start.3) | collective-permute-done | bytes 131104 | tf_op jit(solution)/shard_map/ppermute | solution.py:27
  34.5 27.2 %collective-permute-done.6.r2_ref = bf16[2,256,512]{2,1,0:T(8,128)(2,1)S(1)} collective-permute-done((bf16[2,256,512]{2,1,0:T(8,128)(2,1)S(1)}, bf16[2,256,512]{2,1,0:T(8,128)(2,1)S(1)}, u32[]{:S(2)}, u32[]{:S(2)}) %collective-permute-start.6) | collective-permute-done | bytes 524320 | tf_op jit(solution)/shard_map/ppermute | solution.py:50
  61.7 4.4 %collective-permute-start = (bf16[2,64,512]{2,1,0:T(8,128)(2,1)}, bf16[2,64,512]{2,1,0:T(8,128)(2,1)}, u32[]{:S(2)}, u32[]{:S(2)}) collective-permute-start(bf16[2,64,512]{2,1,0:T(8,128)(2,1)} %get-tuple-element.49), channel_id=1, source_target_pairs={{0,4},{4,8},{8,12},{12,16},{16,20},{20,24},{24,28},{28,32},{32,36}... | collective-permute-start | bytes 393224 | tf_op jit(solution)/shard_map/ppermute | solution.py:56
  67.4 3.9 %collective-permute-start.10 = (bf16[2,64,512]{2,1,0:T(8,128)(2,1)S(1)}, bf16[2,64,512]{2,1,0:T(8,128)(2,1)S(1)}, u32[]{:S(2)}, u32[]{:S(2)}) collective-permute-start(bf16[2,64,512]{2,1,0:T(8,128)(2,1)S(1)} %broadcast_select_fusion.1), channel_id=1, source_target_pairs={{0,16},{4,20},{8,24},{12,28},{1,17},{5,21},{9,25},{13,29},{2,18},{... | collective-permute-start | bytes 393224 | tf_op jit(solution)/shard_map/ppermute | solution.py:27
  71.3 7.7 %collective-permute-start.9 = (bf16[2,64,512]{2,1,0:T(8,128)(2,1)S(1)}, bf16[2,64,512]{2,1,0:T(8,128)(2,1)}, u32[]{:S(2)}, u32[]{:S(2)}) collective-permute-start(bf16[2,64,512]{2,1,0:T(8,128)(2,1)S(1)} %broadcast_select_fusion.1), channel_id=1, source_target_pairs={{0,32},{4,36},{8,40},{12,44},{1,33},{5,37},{9,41},{13,45},{2,34},{... | collective-permute-start | bytes 393224 | tf_op jit(solution)/shard_map/ppermute | solution.py:27
  79.0 2.8 %collective-permute-start.8 = (bf16[2,64,512]{2,1,0:T(8,128)(2,1)S(1)}, bf16[2,64,512]{2,1,0:T(8,128)(2,1)}, u32[]{:S(2)}, u32[]{:S(2)}) collective-permute-start(bf16[2,64,512]{2,1,0:T(8,128)(2,1)S(1)} %broadcast_select_fusion.1), channel_id=1, source_target_pairs={{0,48},{4,52},{8,56},{12,60},{1,49},{5,53},{9,57},{13,61},{2,50},{... | collective-permute-start | bytes 393224 | tf_op jit(solution)/shard_map/ppermute | solution.py:27
  93.5 2.7 %convolution_convert_fusion.1.g_ref = bf16[256,512]{1,0:T(8,128)(2,1)} fusion(bf16[256,2048]{1,0:T(8,128)(2,1)} %all-gather.2.cloned.1.call-done, bf16[512,2048]{1,0:T(8,128)(2,1)S(1)} %copy-done), kind=kOutput, calls=%fused_computation.1 | convolution fusion | flops 537001984 | bytes 3407872 | tf_op jit(solution)/shard_map/dot_general | solution.py:216
  96.2 14.9 %attention_both_ways.1 = (bf16[256,512]{1,0:T(8,128)(2,1)}, bf16[256,512]{1,0:T(8,128)(2,1)}, f32[2,256,512]{2,1,0:T(8,128)}, bf16[2,64,512]{2,1,0:T(8,128)(2,1)...) custom-call(s32[12]{0:T(128)} %reshape.32.picks, ...), custom_call_target="tpu_custom_call" | custom-call | flops 587202560 | bytes 8388608 | tf_op jit(solution)/shard_map/attention_both_ways/pallas_call | solution.py:161
  111.2 2.7 %convolution_convert_fusion = bf16[256,2048]{1,0:T(8,128)(2,1)} fusion(bf16[256,512]{1,0:T(8,128)(2,1)} %get-tuple-element.29, bf16[512,2048]{1,0:T(8,128)(2,1)S(1)} %copy-done), kind=kOutput, calls=%fused_computation | convolution fusion | flops 537395200 | bytes 3407872 | tf_op jit(solution)/shard_map/dot_general | solution.py:227
  115.2 3.1 %collective-permute-start.16 = (bf16[2,256,512]{2,1,0:T(8,128)(2,1)}, bf16[2,256,512]{2,1,0:T(8,128)(2,1)S(1)}, u32[]{:S(2)}, u32[]{:S(2)}) collective-permute-start(bf16[2,256,512]{2,1,0:T(8,128)(2,1)} %get-tuple-element.33), channel_id=1, source_target_pairs={{128,0},{132,4},{136,8},{140,12},{144,16},{148,20},{152,24},{156,2... | collective-permute-start | bytes 1572872 | tf_op jit(solution)/shard_map/ppermute | solution.py:50
  118.3 6.8 %collective-permute-start.17 = (bf16[2,256,512]{2,1,0:T(8,128)(2,1)}, bf16[2,256,512]{2,1,0:T(8,128)(2,1)S(1)}, u32[]{:S(2)}, u32[]{:S(2)}) collective-permute-start(bf16[2,256,512]{2,1,0:T(8,128)(2,1)} %get-tuple-element.34), channel_id=1, source_target_pairs={{64,0},{68,4},{72,8},{76,12},{80,16},{84,20},{88,24},{92,28},{96,3... | collective-permute-start | bytes 1572872 | tf_op jit(solution)/shard_map/ppermute | solution.py:50
  125.2 8.5 %collective-permute-start.18 = (bf16[2,256,512]{2,1,0:T(8,128)(2,1)}, bf16[2,256,512]{2,1,0:T(8,128)(2,1)S(1)}, u32[]{:S(2)}, u32[]{:S(2)}) collective-permute-start(bf16[2,256,512]{2,1,0:T(8,128)(2,1)} %get-tuple-element.35), channel_id=1, source_target_pairs={{96,0},{100,4},{104,8},{108,12},{112,16},{116,20},{120,24},{124,28... | collective-permute-start | bytes 1572872 | tf_op jit(solution)/shard_map/ppermute | solution.py:50
  135.0 7.1 %collective-permute-done.15 = bf16[2,64,512]{2,1,0:T(8,128)(2,1)S(1)} collective-permute-done((bf16[2,64,512]{2,1,0:T(8,128)(2,1)S(1)}, bf16[2,64,512]{2,1,0:T(8,128)(2,1)S(1)}, u32[]{:S(2)}, u32[]{:S(2)}) %collective-permute-start.15) | collective-permute-done | bytes 131104 | tf_op jit(solution)/shard_map/ppermute | solution.py:43
  142.2 7.0 %collective-permute-done.17 = bf16[2,256,512]{2,1,0:T(8,128)(2,1)S(1)} collective-permute-done((bf16[2,256,512]{2,1,0:T(8,128)(2,1)}, bf16[2,256,512]{2,1,0:T(8,128)(2,1)S(1)}, u32[]{:S(2)}, u32[]{:S(2)}) %collective-permute-start.17) | collective-permute-done | bytes 524320 | tf_op jit(solution)/shard_map/ppermute | solution.py:50
  149.2 20.4 %collective-permute-done.18 = bf16[2,256,512]{2,1,0:T(8,128)(2,1)S(1)} collective-permute-done((bf16[2,256,512]{2,1,0:T(8,128)(2,1)}, bf16[2,256,512]{2,1,0:T(8,128)(2,1)S(1)}, u32[]{:S(2)}, u32[]{:S(2)}) %collective-permute-start.18) | collective-permute-done | bytes 524320 | tf_op jit(solution)/shard_map/ppermute | solution.py:50
  173.6 2.4 %collective-permute-start.20 = (bf16[2,64,512]{2,1,0:T(8,128)(2,1)}, bf16[2,64,512]{2,1,0:T(8,128)(2,1)S(1)}, u32[]{:S(2)}, u32[]{:S(2)}) collective-permute-start(bf16[2,64,512]{2,1,0:T(8,128)(2,1)} %get-tuple-element.41), channel_id=1, source_target_pairs={{0,4},{4,8},{8,12},{12,16},{16,20},{20,24},{24,28},{28,32},{32,36}... | collective-permute-start | bytes 393224 | tf_op jit(solution)/shard_map/ppermute | solution.py:56
  186.3 2.0 convert_add_fusion
  188.4 9.0 %collective-permute-done.26 = bf16[2,64,512]{2,1,0:T(8,128)(2,1)S(1)} collective-permute-done((bf16[2,64,512]{2,1,0:T(8,128)(2,1)S(1)}, bf16[2,64,512]{2,1,0:T(8,128)(2,1)S(1)}, u32[]{:S(2)}, u32[]{:S(2)}) %collective-permute-start.26) | collective-permute-done | bytes 131104 | tf_op jit(solution)/shard_map/ppermute | solution.py:43
  197.4 3.3 %collective-permute-done.24 = bf16[2,64,512]{2,1,0:T(8,128)(2,1)S(1)} collective-permute-done((bf16[2,64,512]{2,1,0:T(8,128)(2,1)S(1)}, bf16[2,64,512]{2,1,0:T(8,128)(2,1)S(1)}, u32[]{:S(2)}, u32[]{:S(2)}) %collective-permute-start.24) | collective-permute-done | bytes 131104 | tf_op jit(solution)/shard_map/ppermute | solution.py:43
  (89 shorter events, 36.5 us)
Async XLA Ops:
  7.2 86.3 %all-gather.2.cloned.1.call-start = ((), (), s32[]{:S(2)}) async-start(), calls=%async_computation.1 | async-start | bytes 1310720 | tf_op jit(solution)/shard_map/all_gather | solution.py:217
  9.0 16.7 %collective-permute-start.2 = (bf16[2,64,512]{2,1,0:T(8,128)(2,1)S(1)}, bf16[2,64,512]{2,1,0:T(8,128)(2,1)S(1)}, u32[]{:S(2)}, u32[]{:S(2)}) collective-permute-start(bf16[2,64,512]{2,1,0:T(8,128)(2,1)S(1)} %get-tuple-element.48), channel_id=1, source_target_pairs={{0,4},{1,5},{2,6},{3,7}} | collective-permute-start | bytes 393224 | tf_op jit(solution)/shard_map/ppermute | solution.py:27
  13.5 48.2 %collective-permute-start.6 = (bf16[2,256,512]{2,1,0:T(8,128)(2,1)S(1)}, bf16[2,256,512]{2,1,0:T(8,128)(2,1)S(1)}, u32[]{:S(2)}, u32[]{:S(2)}) collective-permute-start(bf16[2,256,512]{2,1,0:T(8,128)(2,1)S(1)} %pad_maximum_fusion.own_ref), channel_id=1, source_target_pairs={{160,0},{164,4},{168,8},{172,12},{176,16},{180,20},{184,24},{188,2... | collective-permute-start | bytes 1572872 | tf_op jit(solution)/shard_map/ppermute | solution.py:50
  17.1 49.0 %collective-permute-start.5 = (bf16[2,256,512]{2,1,0:T(8,128)(2,1)S(1)}, bf16[2,256,512]{2,1,0:T(8,128)(2,1)}, u32[]{:S(2)}, u32[]{:S(2)}) collective-permute-start(bf16[2,256,512]{2,1,0:T(8,128)(2,1)S(1)} %pad_maximum_fusion.own_ref), channel_id=1, source_target_pairs={{192,0},{196,4},{200,8},{204,12},{208,16},{212,20},{216,24},{220,2... | collective-permute-start | bytes 1572872 | tf_op jit(solution)/shard_map/ppermute | solution.py:50
  19.4 46.7 %collective-permute-start.4 = (bf16[2,256,512]{2,1,0:T(8,128)(2,1)S(1)}, bf16[2,256,512]{2,1,0:T(8,128)(2,1)}, u32[]{:S(2)}, u32[]{:S(2)}) collective-permute-start(bf16[2,256,512]{2,1,0:T(8,128)(2,1)S(1)} %pad_maximum_fusion.own_ref), channel_id=1, source_target_pairs={{128,0},{132,4},{136,8},{140,12},{144,16},{148,20},{152,24},{156,2... | collective-permute-start | bytes 1572872 | tf_op jit(solution)/shard_map/ppermute | solution.py:50
  20.6 46.7 %collective-permute-start.7 = (bf16[2,256,512]{2,1,0:T(8,128)(2,1)S(1)}, bf16[2,256,512]{2,1,0:T(8,128)(2,1)}, u32[]{:S(2)}, u32[]{:S(2)}) collective-permute-start(bf16[2,256,512]{2,1,0:T(8,128)(2,1)S(1)} %pad_maximum_fusion.own_ref), channel_id=1, source_target_pairs={{96,0},{100,4},{104,8},{108,12},{112,16},{116,20},{120,24},{124,28... | collective-permute-start | bytes 1572872 | tf_op jit(solution)/shard_map/ppermute | solution.py:50
  25.7 176.1 %reduce-scatter.2.cloned.1.call-start = ((), (), s32[]{:S(2)}) async-start(), calls=%async_computation.2 | async-start | bytes 1310720 | tf_op jit(solution)/shard_map/reduce_scatter | solution.py:228
  33.2 63.0 %collective-permute-start.1 = (bf16[2,64,512]{2,1,0:T(8,128)(2,1)S(1)}, bf16[2,64,512]{2,1,0:T(8,128)(2,1)}, u32[]{:S(2)}, u32[]{:S(2)}) collective-permute-start(bf16[2,64,512]{2,1,0:T(8,128)(2,1)S(1)} %get-tuple-element.48), channel_id=1, source_target_pairs={{4,0},{8,4},{12,8},{16,12},{20,16},{24,20},{28,24},{32,28},{36,32}... | collective-permute-start | bytes 393224 | tf_op jit(solution)/shard_map/ppermute | solution.py:56
  61.7 34.5 %collective-permute-start = (bf16[2,64,512]{2,1,0:T(8,128)(2,1)}, bf16[2,64,512]{2,1,0:T(8,128)(2,1)}, u32[]{:S(2)}, u32[]{:S(2)}) collective-permute-start(bf16[2,64,512]{2,1,0:T(8,128)(2,1)} %get-tuple-element.49), channel_id=1, source_target_pairs={{0,4},{4,8},{8,12},{12,16},{16,20},{20,24},{24,28},{28,32},{32,36}... | collective-permute-start | bytes 393224 | tf_op jit(solution)/shard_map/ppermute | solution.py:56
  67.4 16.8 %collective-permute-start.10 = (bf16[2,64,512]{2,1,0:T(8,128)(2,1)S(1)}, bf16[2,64,512]{2,1,0:T(8,128)(2,1)S(1)}, u32[]{:S(2)}, u32[]{:S(2)}) collective-permute-start(bf16[2,64,512]{2,1,0:T(8,128)(2,1)S(1)} %broadcast_select_fusion.1), channel_id=1, source_target_pairs={{0,16},{4,20},{8,24},{12,28},{1,17},{5,21},{9,25},{13,29},{2,18},{... | collective-permute-start | bytes 393224 | tf_op jit(solution)/shard_map/ppermute | solution.py:27
  71.3 13.0 %collective-permute-start.9 = (bf16[2,64,512]{2,1,0:T(8,128)(2,1)S(1)}, bf16[2,64,512]{2,1,0:T(8,128)(2,1)}, u32[]{:S(2)}, u32[]{:S(2)}) collective-permute-start(bf16[2,64,512]{2,1,0:T(8,128)(2,1)S(1)} %broadcast_select_fusion.1), channel_id=1, source_target_pairs={{0,32},{4,36},{8,40},{12,44},{1,33},{5,37},{9,41},{13,45},{2,34},{... | collective-permute-start | bytes 393224 | tf_op jit(solution)/shard_map/ppermute | solution.py:27
  113.9 19.8 %collective-permute-start.14 = (bf16[2,64,512]{2,1,0:T(8,128)(2,1)S(1)}, bf16[2,64,512]{2,1,0:T(8,128)(2,1)S(1)}, u32[]{:S(2)}, u32[]{:S(2)}) collective-permute-start(bf16[2,64,512]{2,1,0:T(8,128)(2,1)S(1)} %convert_element_type.63), channel_id=1, source_target_pairs={{4,0},{12,8},{20,16},{28,24},{36,32},{44,40},{52,48},{60,56},{68,6... | collective-permute-start | bytes 393224 | tf_op jit(solution)/shard_map/ppermute | solution.py:43
  115.2 26.9 %collective-permute-start.16 = (bf16[2,256,512]{2,1,0:T(8,128)(2,1)}, bf16[2,256,512]{2,1,0:T(8,128)(2,1)S(1)}, u32[]{:S(2)}, u32[]{:S(2)}) collective-permute-start(bf16[2,256,512]{2,1,0:T(8,128)(2,1)} %get-tuple-element.33), channel_id=1, source_target_pairs={{128,0},{132,4},{136,8},{140,12},{144,16},{148,20},{152,24},{156,2... | collective-permute-start | bytes 1572872 | tf_op jit(solution)/shard_map/ppermute | solution.py:50
  118.3 30.9 %collective-permute-start.17 = (bf16[2,256,512]{2,1,0:T(8,128)(2,1)}, bf16[2,256,512]{2,1,0:T(8,128)(2,1)S(1)}, u32[]{:S(2)}, u32[]{:S(2)}) collective-permute-start(bf16[2,256,512]{2,1,0:T(8,128)(2,1)} %get-tuple-element.34), channel_id=1, source_target_pairs={{64,0},{68,4},{72,8},{76,12},{80,16},{84,20},{88,24},{92,28},{96,3... | collective-permute-start | bytes 1572872 | tf_op jit(solution)/shard_map/ppermute | solution.py:50
  125.2 44.5 %collective-permute-start.18 = (bf16[2,256,512]{2,1,0:T(8,128)(2,1)}, bf16[2,256,512]{2,1,0:T(8,128)(2,1)S(1)}, u32[]{:S(2)}, u32[]{:S(2)}) collective-permute-start(bf16[2,256,512]{2,1,0:T(8,128)(2,1)} %get-tuple-element.35), channel_id=1, source_target_pairs={{96,0},{100,4},{104,8},{108,12},{112,16},{116,20},{120,24},{124,28... | collective-permute-start | bytes 1572872 | tf_op jit(solution)/shard_map/ppermute | solution.py:50
  133.7 35.9 %collective-permute-start.19 = (bf16[2,256,512]{2,1,0:T(8,128)(2,1)}, bf16[2,256,512]{2,1,0:T(8,128)(2,1)S(1)}, u32[]{:S(2)}, u32[]{:S(2)}) collective-permute-start(bf16[2,256,512]{2,1,0:T(8,128)(2,1)} %get-tuple-element.36), channel_id=1, source_target_pairs={{160,0},{164,4},{168,8},{172,12},{176,16},{180,20},{184,24},{188,2... | collective-permute-start | bytes 1572872 | tf_op jit(solution)/shard_map/ppermute | solution.py:50
  169.7 8.7 %collective-permute-start.23 = (bf16[2,64,512]{2,1,0:T(8,128)(2,1)S(1)}, bf16[2,64,512]{2,1,0:T(8,128)(2,1)S(1)}, u32[]{:S(2)}, u32[]{:S(2)}) collective-permute-start(bf16[2,64,512]{2,1,0:T(8,128)(2,1)S(1)} %convert_element_type.72), channel_id=1, source_target_pairs={{48,0},{112,64},{176,128},{240,192},{49,1},{113,65},{177,129},{241... | collective-permute-start | bytes 393224 | tf_op jit(solution)/shard_map/ppermute | solution.py:43
  171.0 9.4 %collective-permute-start.22 = (bf16[2,64,512]{2,1,0:T(8,128)(2,1)S(1)}, bf16[2,64,512]{2,1,0:T(8,128)(2,1)S(1)}, u32[]{:S(2)}, u32[]{:S(2)}) collective-permute-start(bf16[2,64,512]{2,1,0:T(8,128)(2,1)S(1)} %convert_element_type.72), channel_id=1, source_target_pairs={{32,0},{96,64},{160,128},{224,192},{33,1},{97,65},{161,129},{225,1... | collective-permute-start | bytes 393224 | tf_op jit(solution)/shard_map/ppermute | solution.py:43
  172.3 10.0 %collective-permute-start.21 = (bf16[2,64,512]{2,1,0:T(8,128)(2,1)S(1)}, bf16[2,64,512]{2,1,0:T(8,128)(2,1)S(1)}, u32[]{:S(2)}, u32[]{:S(2)}) collective-permute-start(bf16[2,64,512]{2,1,0:T(8,128)(2,1)S(1)} %convert_element_type.72), channel_id=1, source_target_pairs={{16,0},{80,64},{144,128},{208,192},{17,1},{81,65},{145,129},{209,1... | collective-permute-start | bytes 393224 | tf_op jit(solution)/shard_map/ppermute | solution.py:43
  173.6 14.8 %collective-permute-start.20 = (bf16[2,64,512]{2,1,0:T(8,128)(2,1)}, bf16[2,64,512]{2,1,0:T(8,128)(2,1)S(1)}, u32[]{:S(2)}, u32[]{:S(2)}) collective-permute-start(bf16[2,64,512]{2,1,0:T(8,128)(2,1)} %get-tuple-element.41), channel_id=1, source_target_pairs={{0,4},{4,8},{8,12},{12,16},{16,20},{20,24},{24,28},{28,32},{32,36}... | collective-permute-start | bytes 393224 | tf_op jit(solution)/shard_map/ppermute | solution.py:56
  176.1 12.3 %collective-permute-start.27 = (bf16[2,64,512]{2,1,0:T(8,128)(2,1)S(1)}, bf16[2,64,512]{2,1,0:T(8,128)(2,1)S(1)}, u32[]{:S(2)}, u32[]{:S(2)}) collective-permute-start(bf16[2,64,512]{2,1,0:T(8,128)(2,1)S(1)} %copy-done.10), channel_id=1, source_target_pairs={{4,0},{8,4},{12,8},{16,12},{20,16},{24,20},{28,24},{32,28},{36,32}... | collective-permute-start | bytes 393224 | tf_op jit(solution)/shard_map/ppermute | solution.py:56
  182.4 15.0 %collective-permute-start.26 = (bf16[2,64,512]{2,1,0:T(8,128)(2,1)S(1)}, bf16[2,64,512]{2,1,0:T(8,128)(2,1)S(1)}, u32[]{:S(2)}, u32[]{:S(2)}) collective-permute-start(bf16[2,64,512]{2,1,0:T(8,128)(2,1)S(1)} %fusion.5), channel_id=1, source_target_pairs={{192,0},{193,1},{194,2},{195,3}} | collective-permute-start | bytes 393224 | tf_op jit(solution)/shard_map/ppermute | solution.py:43
  183.7 13.7 %collective-permute-start.25 = (bf16[2,64,512]{2,1,0:T(8,128)(2,1)S(1)}, bf16[2,64,512]{2,1,0:T(8,128)(2,1)S(1)}, u32[]{:S(2)}, u32[]{:S(2)}) collective-permute-start(bf16[2,64,512]{2,1,0:T(8,128)(2,1)S(1)} %fusion.5), channel_id=1, source_target_pairs={{128,0},{129,1},{130,2},{131,3}} | collective-permute-start | bytes 393224 | tf_op jit(solution)/shard_map/ppermute | solution.py:43
  185.0 15.7 %collective-permute-start.24 = (bf16[2,64,512]{2,1,0:T(8,128)(2,1)S(1)}, bf16[2,64,512]{2,1,0:T(8,128)(2,1)S(1)}, u32[]{:S(2)}, u32[]{:S(2)}) collective-permute-start(bf16[2,64,512]{2,1,0:T(8,128)(2,1)S(1)} %fusion.5), channel_id=1, source_target_pairs={{64,0},{65,1},{66,2},{67,3}} | collective-permute-start | bytes 393224 | tf_op jit(solution)/shard_map/ppermute | solution.py:43
  (17 other events, 379.4 us)
Sparse Core Ops, SparseCore 0:
  25.8 35.9 all-gather.1
  114.0 29.8 reduce-scatter.1
